TPU v7x, 32 devices: a whole 2x2x4 slice. The times are simulated.
32 devices in a mesh: row: 4 (over y, x), col: 8 (over z, core).
Axes of the slice: x: 2, y: 2, z: 4, core: 2. Of those that a mesh axis runs over, the one named last changes fastest.
Arguments:
- inputs: bfloat16 [4096, 2048], P('row', 'col'), may hold values from -6 to 6
- cotangent: bfloat16 [4096, 2048], P('row', 'col'), may hold values from -6 to 6
- norm_first: float32 [2048], replicated, may hold values from 0.1 to 1.9
- norm_second: float32 [2048], replicated, may hold values from 0.1 to 1.9
- query_gain: float32 [2048], replicated, may hold values from 0.1 to 1.9
- key_gain: float32 [2048], replicated, may hold values from 0.1 to 1.9
- w_query: bfloat16 [2048, 2048], P(None, 'col'), may hold values from -0.125 to 0.125
- w_key: bfloat16 [2048, 2048], P(None, 'col'), may hold values from -0.125 to 0.125
- w_value: bfloat16 [2048, 2048], P(None, 'col'), may hold values from -0.125 to 0.125
- w_out: bfloat16 [2048, 2048], P('col'), may hold values from -0.5 to 0.5
- w_router: bfloat16 [2048, 16], replicated, may hold values from -0.0625 to 0.0625
- w_gate: bfloat16 [16, 2048, 1024], P('col', None, 'row'), may hold values from -0.125 to 0.125
- w_up: bfloat16 [16, 2048, 1024], P('col', None, 'row'), may hold values from -0.125 to 0.125
- w_down: bfloat16 [16, 1024, 2048], P('col', 'row'), may hold values from -3 to 3
- adapter_a: bfloat16 [5, 8, 2048, 16], replicated, may hold values from -0.125 to 0.125
- adapter_b: bfloat16 [4, 8, 16, 2048], replicated, may hold values from -0.75 to 0.75
- adapter_router: bfloat16 [8, 16, 16], replicated, may hold values from -0.375 to 0.375
- routes: int32 [4096, 8], P('row'), may hold values from 0 to 15, all different within a row; in each aligned block of 1024 rows (0 to 1023, 1024 to 2047, ...) at most 640 rows name the same one
- prefix: int32 [4], P('row'), may hold values from 1 to 511
- adapter_index: int32 [4], P('row'), may hold values from 0 to 7
Outputs:
- layer_out: bfloat16 [4096, 2048], P('row', 'col')
- grad_inputs: float32 [4096, 2048], P('row', 'col')
- grad_a: float32 [5, 8, 2048, 16], P(None, 'row', 'col')
- grad_b: float32 [4, 8, 16, 2048], P(None, 'row', None, 'col')
- grad_router: float32 [8, 16, 16], P('row')
Inputs may be any that keep to these rules, and one draw needn't show every extreme that they name: `routes`: each token names 8 different experts; within one sequence no expert is named by more than 640 tokens, and in every draw some expert is named by exactly 640 tokens of some sequence.
All inputs are finite; a program needn't handle non-finite values.
Results may differ from a plain program's by a relative error of at most 0.023.
Values may be sent and summed in bfloat16 or wider, within the bound.
A program may use at most 256 MiB of HBM per device.

v0:
```python
import jax
import jax.numpy as jnp
from jax import lax
from jax.sharding import PartitionSpec as P

HD = 128


norm_eps = 1e-05
rope_base = 10000.0
masked_score = -1e30


def rope_tables(length, head_dim):
    half_dim = head_dim // 2
    frequency = rope_base ** (-(2.0 * jnp.arange(half_dim, dtype=jnp.float32)) / head_dim)
    angles = jnp.arange(length, dtype=jnp.float32)[:, None] * frequency[None, :]
    return (jnp.cos(angles), jnp.sin(angles))


def rotate(values, cosine_table, sine_table):
    half_dim = values.shape[-1] // 2
    first_half = values[..., :half_dim]
    second_half = values[..., half_dim:]
    return jnp.concatenate(
        [
            first_half * cosine_table - second_half * sine_table,
            second_half * cosine_table + first_half * sine_table,
        ],
        axis=-1,
    )


def unrotate(values, cosine_table, sine_table):
    half_dim = values.shape[-1] // 2
    first_half = values[..., :half_dim]
    second_half = values[..., half_dim:]
    return jnp.concatenate(
        [
            first_half * cosine_table + second_half * sine_table,
            second_half * cosine_table - first_half * sine_table,
        ],
        axis=-1,
    )


def matmul(left_side, right_side):
    return jnp.dot(left_side, right_side, preferred_element_type=jnp.float32)


def shards(
    inputs,
    cotangent,
    norm_first,
    norm_second,
    query_gain,
    key_gain,
    w_query,
    w_key,
    w_value,
    w_out,
    w_router,
    w_gate,
    w_up,
    w_down,
    adapter_a,
    adapter_b,
    adapter_router,
    routes,
    prefix,
    adapter_index,
):
    seq_len, width_part = inputs.shape
    col_count = lax.axis_size("col")
    col_index = lax.axis_index("col")
    full_width = width_part * col_count
    head_width = w_query.shape[1]
    head_count = head_width // HD
    local_experts = w_gate.shape[0]
    route_count = routes.shape[1]
    capacity = seq_len * route_count * 5 // (4 * local_experts * col_count)
    slot_count = local_experts * capacity
    feature_start = col_index * width_part
    head_start = col_index * head_width
    score_scale = HD ** (-0.5)
    f_type = jnp.float32
    b_type = jnp.bfloat16

    def columns(array, axis_num):
        return lax.dynamic_slice_in_dim(array, feature_start, width_part, axis_num)

    def head_cols(array):
        return lax.dynamic_slice_in_dim(array, head_start, head_width, 1)

    full_inputs, full_cot = (
        lax.all_gather(inputs, "col", axis=1, tiled=True),
        lax.all_gather(cotangent, "col", axis=1, tiled=True),
    )
    adapter_slot = adapter_index[0]
    chosen_a = lax.dynamic_index_in_dim(adapter_a, adapter_slot, 1, keepdims=False)
    chosen_b = lax.dynamic_index_in_dim(adapter_b, adapter_slot, 1, keepdims=False)
    chosen_router = lax.dynamic_index_in_dim(adapter_router, adapter_slot, 0, keepdims=False)
    rank_count = chosen_a.shape[2]
    input_f32 = full_inputs.astype(f_type)
    inv_first = lax.rsqrt(jnp.mean(input_f32 * input_f32, axis=1, keepdims=True) + norm_eps)
    normed = (input_f32 * inv_first * norm_first).astype(b_type)
    a_three = jnp.concatenate([chosen_a[0], chosen_a[1], chosen_a[2]], axis=1)
    middle = matmul(normed, a_three).astype(b_type)
    mid_query = middle[:, :rank_count]
    mid_key = middle[:, rank_count : 2 * rank_count]
    mid_value = middle[:, 2 * rank_count :]
    b_query = head_cols(chosen_b[0])
    b_key = head_cols(chosen_b[1])
    b_value = head_cols(chosen_b[2])
    proj_query = matmul(normed, w_query) + matmul(mid_query, b_query)
    proj_key = matmul(normed, w_key) + matmul(mid_key, b_key)
    proj_value = matmul(normed, w_value) + matmul(mid_value, b_value)
    square_sums = lax.psum(
        (jnp.sum(proj_query * proj_query, axis=1), jnp.sum(proj_key * proj_key, axis=1)), "col"
    )
    inv_query = lax.rsqrt(square_sums[0] / full_width + norm_eps)[:, None]
    inv_key = lax.rsqrt(square_sums[1] / full_width + norm_eps)[:, None]
    gain_query = lax.dynamic_slice_in_dim(query_gain, head_start, head_width, 0)
    gain_key = lax.dynamic_slice_in_dim(key_gain, head_start, head_width, 0)
    cosine_table, sine_table = rope_tables(seq_len, HD)
    cosine_table = cosine_table[:, None, :]
    sine_table = sine_table[:, None, :]
    rot_query = rotate(
        (proj_query * inv_query * gain_query).reshape(seq_len, head_count, HD),
        cosine_table,
        sine_table,
    ).astype(b_type)
    rot_key = rotate(
        (proj_key * inv_key * gain_key).reshape(seq_len, head_count, HD), cosine_table, sine_table
    ).astype(b_type)
    value_rows = proj_value.astype(b_type).reshape(seq_len, head_count, HD)
    block_rows = min(512, seq_len)
    starts = jnp.arange(seq_len // block_rows, dtype=jnp.int32) * block_rows
    key_pos = jnp.arange(seq_len, dtype=jnp.int32)
    prefix_len = prefix[0]

    def block_scores(start_row):
        block_query = lax.dynamic_slice_in_dim(rot_query, start_row, block_rows, 0)
        query_pos = start_row + jnp.arange(block_rows, dtype=jnp.int32)
        allowed = (key_pos[None, :] <= query_pos[:, None]) | (key_pos[None, :] < prefix_len)
        raw_scores = (
            jnp.einsum("qhd,khd->hqk", block_query, rot_key, preferred_element_type=f_type)
            * score_scale
        )
        return (block_query, jnp.where(allowed[None], raw_scores, masked_score))

    def attend_block(start_row):
        block_query, scores = block_scores(start_row)
        row_max = jnp.max(scores, axis=2, keepdims=True)
        exponent = jnp.exp(scores - row_max)
        row_total = jnp.sum(exponent, axis=2, keepdims=True)
        weights = (exponent / row_total).astype(b_type)
        attended_block = jnp.einsum(
            "hqk,khd->qhd", weights, value_rows, preferred_element_type=f_type
        )
        return (attended_block.astype(b_type), (row_max + jnp.log(row_total))[:, :, 0])

    attended_blocks, log_totals = lax.map(attend_block, starts)
    attended = attended_blocks.reshape(seq_len, head_width)
    a_out_rows = lax.dynamic_slice_in_dim(chosen_a[3], head_start, head_width, 0)
    out_sum, mid_out_sum = lax.psum((matmul(attended, w_out), matmul(attended, a_out_rows)), "col")
    mid_out = mid_out_sum.astype(b_type)
    hidden = input_f32 + out_sum + matmul(mid_out, chosen_b[3])
    inv_second = lax.rsqrt(jnp.mean(hidden * hidden, axis=1, keepdims=True) + norm_eps)
    normed_two = (hidden * inv_second * norm_second).astype(b_type)
    mid_router = matmul(normed_two, chosen_a[4]).astype(b_type)
    logits = matmul(normed_two, w_router) + matmul(mid_router, chosen_router)
    router_probs = jax.nn.softmax(logits, axis=1)
    expert_total = router_probs.shape[1]
    local_ids = jnp.arange(local_experts, dtype=jnp.int32)
    own_ids = col_index * local_experts + local_ids
    member = jnp.sum((routes[:, :, None] == own_ids[None, None, :]).astype(jnp.int32), axis=1)
    slot_rank = jnp.cumsum(member, axis=0) - member
    target = jnp.where(member > 0, local_ids[None, :] * capacity + slot_rank, slot_count)
    token_ids = jnp.broadcast_to(jnp.arange(seq_len, dtype=jnp.int32)[:, None], member.shape)
    slot_token = (
        jnp.zeros((slot_count,), jnp.int32)
        .at[target.reshape(-1)]
        .set(token_ids.reshape(-1), mode="drop")
    )
    slot_live = jnp.zeros((slot_count,), f_type).at[target.reshape(-1)].set(1.0, mode="drop")
    slot_local = jnp.arange(slot_count, dtype=jnp.int32) // capacity
    own_probs = lax.dynamic_slice_in_dim(router_probs, col_index * local_experts, local_experts, 1)
    slot_gate = own_probs[slot_token, slot_local] * slot_live
    buckets = jnp.where(slot_live[:, None] > 0, normed_two[slot_token], jnp.zeros((), b_type))
    full_gate, full_up, full_down = (
        lax.all_gather(w_gate, "row", axis=2, tiled=True),
        lax.all_gather(w_up, "row", axis=2, tiled=True),
        lax.all_gather(w_down, "row", axis=1, tiled=True),
    )
    rows_in = buckets.reshape(local_experts, capacity, full_width)
    gate_in = jnp.einsum("ecd,edf->ecf", rows_in, full_gate, preferred_element_type=f_type)
    up_in = jnp.einsum("ecd,edf->ecf", rows_in, full_up, preferred_element_type=f_type)
    active = (jax.nn.silu(gate_in) * up_in).astype(b_type)
    expert_out = jnp.einsum(
        "ecf,efd->ecd", active, full_down, preferred_element_type=f_type
    ).reshape(slot_count, full_width)
    dense_out = jax.ops.segment_sum(
        expert_out * slot_gate[:, None], slot_token, num_segments=seq_len
    )
    moe_part = lax.psum_scatter(
        dense_out.astype(jnp.bfloat16), "col", scatter_dimension=1, tiled=True
    ).astype(jnp.float32)
    layer_out = (columns(hidden, 1) + moe_part).astype(b_type)
    cot_rows = full_cot[slot_token].astype(f_type)
    slot_dgate = jnp.sum(cot_rows * expert_out, axis=1) * slot_live
    grad_slot_out = (slot_gate[:, None] * cot_rows).astype(b_type)
    dprob_own = jax.ops.segment_sum(
        slot_dgate, slot_token * local_experts + slot_local, num_segments=seq_len * local_experts
    ).reshape(seq_len, local_experts)
    dprob_part = lax.dynamic_update_slice_in_dim(
        jnp.zeros((seq_len, expert_total), f_type), dprob_own, col_index * local_experts, 1
    )
    sigmoid_gate = jax.nn.sigmoid(gate_in)
    grad_active = jnp.einsum(
        "ecd,efd->ecf",
        grad_slot_out.reshape(local_experts, capacity, full_width),
        full_down,
        preferred_element_type=f_type,
    )
    grad_gate_in = (
        grad_active * up_in * sigmoid_gate * (1.0 + gate_in * (1.0 - sigmoid_gate))
    ).astype(b_type)
    grad_up_in = (grad_active * gate_in * sigmoid_gate).astype(b_type)
    expert_back = (
        jnp.einsum("ecf,edf->ecd", grad_gate_in, full_gate, preferred_element_type=f_type)
        + jnp.einsum("ecf,edf->ecd", grad_up_in, full_up, preferred_element_type=f_type)
    ).reshape(slot_count, full_width)
    dense_back = jax.ops.segment_sum(expert_back, slot_token, num_segments=seq_len)
    back_sum, grad_probs = lax.psum((dense_back, dprob_part), "col")
    grad_logits = (
        router_probs * (grad_probs - jnp.sum(router_probs * grad_probs, axis=1, keepdims=True))
    ).astype(b_type)
    grad_mid_router = jnp.einsum(
        "le,re->lr", grad_logits, chosen_router, preferred_element_type=f_type
    ).astype(b_type)
    grad_normed_two = (
        back_sum
        + jnp.einsum("le,de->ld", grad_logits, w_router, preferred_element_type=f_type)
        + jnp.einsum("lr,dr->ld", grad_mid_router, chosen_a[4], preferred_element_type=f_type)
    )
    scaled_two = grad_normed_two * norm_second
    inv_cube_two = inv_second * inv_second * inv_second
    grad_hidden = (
        full_cot.astype(f_type)
        + inv_second * scaled_two
        - hidden * inv_cube_two * jnp.mean(hidden * scaled_two, axis=1, keepdims=True)
    )
    grad_attn = grad_hidden.astype(b_type)
    grad_mid_out = jnp.einsum(
        "ld,rd->lr", grad_attn, chosen_b[3], preferred_element_type=f_type
    ).astype(b_type)
    grad_attended = (
        jnp.einsum("ld,hd->lh", grad_attn, w_out, preferred_element_type=f_type)
        + jnp.einsum("lr,hr->lh", grad_mid_out, a_out_rows, preferred_element_type=f_type)
    ).astype(b_type)
    grad_b_out = jnp.einsum(
        "lr,ld->rd", mid_out, columns(grad_attn, 1), preferred_element_type=f_type
    )
    grad_a_out = jnp.einsum("lh,lr->hr", attended, grad_mid_out, preferred_element_type=f_type)
    grad_heads = grad_attended.reshape(seq_len, head_count, HD)

    def back_block(carried, packed):
        key_acc, value_acc = carried
        start_row, log_total = packed
        block_query, scores = block_scores(start_row)
        weights = jnp.exp(scores - log_total[:, :, None])
        block_grad = lax.dynamic_slice_in_dim(grad_heads, start_row, block_rows, 0)
        grad_weights = jnp.einsum(
            "qhd,khd->hqk", block_grad, value_rows, preferred_element_type=f_type
        )
        row_dot = jnp.sum(weights * grad_weights, axis=2, keepdims=True)
        grad_scores = (weights * (grad_weights - row_dot)).astype(b_type)
        query_block = (
            jnp.einsum("hqk,khd->qhd", grad_scores, rot_key, preferred_element_type=f_type)
            * score_scale
        )
        key_acc = (
            key_acc
            + jnp.einsum("hqk,qhd->khd", grad_scores, block_query, preferred_element_type=f_type)
            * score_scale
        )
        value_acc = value_acc + jnp.einsum(
            "hqk,qhd->khd", weights.astype(b_type), block_grad, preferred_element_type=f_type
        )
        return ((key_acc, value_acc), query_block)

    zero_heads = jnp.zeros((seq_len, head_count, HD), f_type)
    (grad_key_rot, grad_value_all), query_blocks = lax.scan(
        back_block, (zero_heads, zero_heads), (starts, log_totals)
    )
    grad_query_rot = query_blocks.reshape(seq_len, head_count, HD)
    scaled_query = (
        unrotate(grad_query_rot, cosine_table, sine_table).reshape(seq_len, head_width) * gain_query
    )
    scaled_key = (
        unrotate(grad_key_rot, cosine_table, sine_table).reshape(seq_len, head_width) * gain_key
    )
    norm_stats = lax.psum(
        (jnp.sum(proj_query * scaled_query, axis=1), jnp.sum(proj_key * scaled_key, axis=1)), "col"
    )
    grad_proj_query = (
        inv_query * scaled_query
        - proj_query * inv_query * inv_query * inv_query * norm_stats[0][:, None] / full_width
    ).astype(b_type)
    grad_proj_key = (
        inv_key * scaled_key
        - proj_key * inv_key * inv_key * inv_key * norm_stats[1][:, None] / full_width
    ).astype(b_type)
    grad_proj_value = grad_value_all.reshape(seq_len, head_width).astype(b_type)
    normed_part = (
        jnp.einsum("lh,dh->ld", grad_proj_query, w_query, preferred_element_type=f_type)
        + jnp.einsum("lh,dh->ld", grad_proj_key, w_key, preferred_element_type=f_type)
        + jnp.einsum("lh,dh->ld", grad_proj_value, w_value, preferred_element_type=f_type)
    )
    first_stat = jnp.sum(input_f32 * norm_first * normed_part, axis=1)
    mid_q_sum, mid_k_sum, mid_v_sum, stat_sum = (
        lax.psum(
            jnp.einsum("lh,rh->lr", grad_proj_query, b_query, preferred_element_type=f_type).astype(
                jnp.bfloat16
            ),
            "col",
        ).astype(jnp.float32),
        lax.psum(
            jnp.einsum("lh,rh->lr", grad_proj_key, b_key, preferred_element_type=f_type).astype(
                jnp.bfloat16
            ),
            "col",
        ).astype(jnp.float32),
        lax.psum(
            jnp.einsum("lh,rh->lr", grad_proj_value, b_value, preferred_element_type=f_type).astype(
                jnp.bfloat16
            ),
            "col",
        ).astype(jnp.float32),
        lax.psum(first_stat.astype(jnp.bfloat16), "col").astype(jnp.float32),
    )
    grad_middle = jnp.concatenate([mid_q_sum, mid_k_sum, mid_v_sum], axis=1).astype(b_type)
    adapter_back = jnp.einsum("lr,dr->ld", grad_middle, a_three, preferred_element_type=f_type)
    total_stat = stat_sum + jnp.sum(input_f32 * norm_first * adapter_back, axis=1)
    normed_own = lax.psum_scatter(
        normed_part.astype(jnp.bfloat16), "col", scatter_dimension=1, tiled=True
    ).astype(jnp.float32) + columns(adapter_back, 1)
    input_part = inputs.astype(f_type)
    grad_inputs = (
        columns(grad_hidden, 1)
        + inv_first * columns(norm_first, 0) * normed_own
        - input_part * inv_first * inv_first * inv_first * total_stat[:, None] / full_width
    )
    grad_a_three = jnp.einsum(
        "ld,lr->dr", columns(normed, 1), grad_middle, preferred_element_type=f_type
    )
    grad_a_router = jnp.einsum(
        "ld,lr->dr", columns(normed_two, 1), grad_mid_router, preferred_element_type=f_type
    )
    grad_a_stack = jnp.stack(
        [
            grad_a_three[:, :rank_count],
            grad_a_three[:, rank_count : 2 * rank_count],
            grad_a_three[:, 2 * rank_count :],
            grad_a_out,
            grad_a_router,
        ]
    )
    grad_b_stack = jnp.stack(
        [
            jnp.einsum("lr,lh->rh", mid_query, grad_proj_query, preferred_element_type=f_type),
            jnp.einsum("lr,lh->rh", mid_key, grad_proj_key, preferred_element_type=f_type),
            jnp.einsum("lr,lh->rh", mid_value, grad_proj_value, preferred_element_type=f_type),
            grad_b_out,
        ]
    )
    grad_router_one = jnp.einsum(
        "lr,le->re", mid_router, grad_logits, preferred_element_type=f_type
    )
    adapter_count = adapter_a.shape[1]
    pick = (jnp.arange(adapter_count, dtype=jnp.int32) == adapter_slot).astype(f_type)
    full_a = pick[None, :, None, None] * grad_a_stack[:, None]
    full_b = pick[None, :, None, None] * grad_b_stack[:, None]
    full_r = pick[:, None, None] * grad_router_one[None]
    grad_a, grad_b, grad_router = (
        lax.psum_scatter(
            full_a.astype(jnp.bfloat16), "row", scatter_dimension=1, tiled=True
        ).astype(jnp.float32),
        lax.psum_scatter(
            full_b.astype(jnp.bfloat16), "row", scatter_dimension=1, tiled=True
        ).astype(jnp.float32),
        lax.psum_scatter(
            full_r.astype(jnp.bfloat16), "row", scatter_dimension=0, tiled=True
        ).astype(jnp.float32),
    )
    return (layer_out, grad_inputs, grad_a, grad_b, grad_router)


def solution(mesh):
    placed = (
        P("row", "col"),
        P("row", "col"),
        P(),
        P(),
        P(),
        P(),
        P(None, "col"),
        P(None, "col"),
        P(None, "col"),
        P("col", None),
        P(),
        P("col", None, "row"),
        P("col", None, "row"),
        P("col", "row", None),
        P(),
        P(),
        P(),
        P("row", None),
        P("row"),
        P("row"),
    )
    return jax.shard_map(
        shards,
        mesh=mesh,
        in_specs=placed,
        out_specs=(
            P("row", "col"),
            P("row", "col"),
            P(None, "row", "col", None),
            P(None, "row", None, "col"),
            P("row", None, None),
        ),
        check_vma=False,
    )
```

profile of v0, /device:TPU:16, one launch (start us, length us, event | category | flops | bytes accessed | tf_op | source)
XLA Modules:
  0.0 1207.6 jit_solution(14886718985746648612)
XLA Ops:
  17.7 38.7 %all-gather.6.cloned.1.call-done = bf16[1024,2048]{0,1:T(8,128)(2,1)} async-done(((bf16[1024,256]{0,1:T(8,128)(2,1)}), bf16[1024,2048]{0,1:T(8,128)(2,1)}) %all-gather.6.cloned.1.call-update) | async-done | bytes 4194320 | tf_op jit(solution)/shard_map/all_gather | solution.py:96
  66.8 15.0 %all-reduce.3 = (f32[1024]{0:T(1024)S(1)}, f32[1024]{0:T(1024)S(1)}) all-reduce(f32[1024]{0:T(1024)S(1)} %get-tuple-element.416, f32[1024]{0:T(1024)S(1)} %get-tuple-element.418), channel_id=1, replica_groups=mesh['row'=4,'col'=8] {'col'}, use_global_device_ids=true, to_apply=%region_2.3 | all-reduce | flops 2048 | bytes 16384 | tf_op jit(solution)/shard_map/psum | solution.py:118
  106.0 20.4 %while.30 = (s32[]{:T(128)}, bf16[2,512,2,128]{3,2,1,0:T(2,128)(2,1)}, f32[2,2,512]{2,1,0:T(2,128)S(1)}, s32[2]{0:T(128)S(1)}, s32[]{:T(128)}, /*index=5*/bf16[1...) while((s32[]{:T(128)}, ...), condition=%wide.region_8.9_spmd.clone.clone, body=%wide.region_5.8_spmd.clone.clone.sunk | while | flops 550633984 | bytes 16816812 | solution.py:163
  136.8 8.5 scatter_custom_fusion
  160.1 13.6 %gather_fusion.2 = bf16[1280,2048]{1,0:T(8,128)(2,1)} fusion(bf16[1024,2048]{1,0:T(8,128)(2,1)} %copy.142, s32[2048]{0:T(1024)S(1)} %pad_clamp_fusion), kind=kCustom, calls=%fused_computation.2 | custom fusion | bytes 10490880 | tf_op jit(solution)/shard_map/gather | solution.py:210
  175.0 25.0 %psum.87 = bf16[1024,16]{0,1:T(8,128)(2,1)S(1)} all-reduce(f32[1024,16]{0,1:T(8,128)S(1)} %fusion.76), channel_id=1, replica_groups=mesh['row'=4,'col'=8] {'col'}, use_global_device_ids=true, to_apply=%region_10.11 | all-reduce | flops 16384 | bytes 98304 | tf_op jit(solution)/shard_map/psum | solution.py:166
  200.0 110.4 %all-reduce.12.cloned.1.call-done = f32[1024,2048]{0,1:T(8,128)} async-done(((f32[1024,2048]{0,1:T(8,128)}), f32[1024,2048]{0,1:T(8,128)}) %all-reduce.12.cloned.1.call-update) | async-done | bytes 8388624 | tf_op jit(solution)/shard_map/psum | solution.py:166
  329.3 13.6 %gather_fusion = bf16[1280,2048]{1,0:T(8,128)(2,1)} fusion(bf16[1024,2048]{1,0:T(8,128)(2,1)} %copy.139, s32[2048]{0:T(1024)S(1)} %pad_clamp_fusion), kind=kCustom, calls=%fused_computation | custom fusion | bytes 10490880 | tf_op jit(solution)/shard_map/gather | solution.py:190
  349.6 10.7 gather_fusion.1
  360.3 39.3 %all-gather.8.cloned.1.call-done = bf16[2,2048,1024]{2,1,0:T(8,128)(2,1)} async-done(((bf16[2,2048,256]{2,1,0:T(8,128)(2,1)}), bf16[2,2048,1024]{2,1,0:T(8,128)(2,1)}) %all-gather.8.cloned.1.call-update) | async-done | bytes 8388624 | tf_op jit(solution)/shard_map/all_gather | solution.py:192
  399.5 11.5 fusion.59
  411.1 77.5 %all-gather.10.cloned.1.call-done = bf16[2,2048,1024]{2,1,0:T(8,128)(2,1)} async-done(((bf16[2,2048,256]{2,1,0:T(8,128)(2,1)}), bf16[2,2048,1024]{2,1,0:T(8,128)(2,1)}) %all-gather.10.cloned.1.call-update) | async-done | bytes 8388624 | tf_op jit(solution)/shard_map/all_gather | solution.py:193
  488.6 11.6 fusion.58
  500.2 77.6 %all-gather.12.cloned.1.call-done = bf16[2,1024,2048]{2,1,0:T(8,128)(2,1)} async-done(((bf16[2,256,2048]{2,1,0:T(8,128)(2,1)}), bf16[2,1024,2048]{2,1,0:T(8,128)(2,1)}) %all-gather.12.cloned.1.call-update) | async-done | bytes 8388624 | tf_op jit(solution)/shard_map/all_gather | solution.py:194
  577.8 14.6 %fusion.46 = (f32[2,640]{1,0:T(2,128)S(1)}, f32[2,640,2048]{2,1,0:T(8,128)}) fusion(bf16[2,640,2048]{2,1,0:T(8,128)(2,1)} %bitcast.264, bf16[2,1024,2048]{2,1,0:T(8,128)(2,1)} %all-gather.12.cloned.1.call-done, f32[2,640,1024]{2,1,0:T(8,128)} %fusion.58, f32[2,640,1024]{2,1,0:T(8,128)} %fusion.59), kind=kOutput, calls=%fused_computation.70 | convolution fusion | flops 5384436736 | bytes 34608128 | tf_op jit(solution)/shard_map/ecf,efd->ecd/dot_general | solution.py:200
  592.5 11.1 fusion.55
  603.6 14.6 %fusion.65 = f32[2,640,2048]{2,1,0:T(8,128)} fusion(bf16[2,2048,1024]{2,1,0:T(8,128)(2,1)} %all-gather.8.cloned.1.call-done, f32[2,640,1024]{2,1,0:T(8,128)} %fusion.59, f32[2,640,1024]{2,1,0:T(8,128)} %fusion.55, f32[2,640,1024]{2,1,0:T(8,128)} %fusion.58), kind=kOutput, calls=%fused_computation.101 | convolution fusion | flops 5381816320 | bytes 34603008 | tf_op jit(solution)/shard_map/ecf,edf->ecd/dot_general | solution.py:231
  618.2 14.7 %convolution_add_fusion = f32[2,640,2048]{2,1,0:T(8,128)} fusion(f32[2,640,2048]{2,1,0:T(8,128)} %fusion.65, bf16[2,2048,1024]{2,1,0:T(8,128)(2,1)} %all-gather.10.cloned.1.call-done, f32[2,640,1024]{2,1,0:T(8,128)} %fusion.55, f32[2,640,1024]{2,1,0:T(8,128)} %fusion.59), kind=kOutput, calls=%fused_computation.95 | convolution fusion | flops 5379194880 | bytes 39845888 | tf_op jit(solution)/shard_map/ecf,edf->ecd/dot_general | solution.py:232
  633.0 25.0 %scatter_custom_fusion.3 = f32[1024,2048]{1,0:T(8,128)} fusion(s32[1280]{0:T(1024)S(1)} %scatter_custom_fusion, f32[1280,2048]{1,0:T(8,128)} %bitcast.277, f32[]{:T(128)} %constant.54.clone.1), kind=kCustom, calls=%fused_computation.96 | custom fusion | flops 2621440 | bytes 8389120 | tf_op jit(solution)/shard_map/scatter-add | solution.py:234
  658.0 9.3 copy.143
  667.3 9.4 scatter_custom_fusion.4
  678.1 176.9 %all-reduce.14.cloned.1.call-done = (f32[1024,2048]{0,1:T(8,128)}, f32[1024,16]{0,1:T(8,128)}) async-done(((f32[1024,2048]{0,1:T(8,128)}, f32[1024,16]{0,1:T(8,128)}), (f32[1024,2048]{0,1:T(8,128)}, f32[1024,16]{0,1:T(8,128)})) %all-reduce.14.cloned.1.call-update) | async-done | bytes 8454160 | tf_op jit(solution)/shard_map/psum | solution.py:235
  858.8 9.9 multiply_reduce_fusion.1
  882.5 40.5 %while.31 = (s32[]{:T(128)}, f32[1024,2,128]{0,2,1:T(8,128)}, f32[1024,2,128]{0,2,1:T(8,128)}, f32[2,512,2,128]{3,1,0,2:T(8,128)}, s32[2]{0:T(128)S(1)}, /*index...) while((s32[]{:T(128)}, f32[1024,2,128]{0,2,1:T(8,128)}, ...), condition=%wide.region_30.31_spmd.clone.clone, body=%wide.region_28.30_spmd.clone.clone.sunk | while | flops 1360396800 | bytes 80776040 | solution.py:294
  941.0 10.5 all-reduce.2
  961.2 57.1 %all-reduce.16.cloned.1.call-done = (bf16[1024,16]{0,1:T(8,128)(2,1)}, bf16[1024,16]{0,1:T(8,128)(2,1)}, bf16[1024,16]{0,1:T(8,128)(2,1)}) async-done(((bf16[1024,16]{0,1:T(8,128)(2,1)}, bf16[1024,16]{0,1:T(8,128)(2,1)}, bf16[1024,16]{0,1:T(8,128)(2,1)}), (bf16[1024,16]{0,1:T(8,128)(2,1)}, bf16[1024,16]{0,1:T(8,128)(2,1)}, bf16[1024,16]{0,1:T(8,128)(2,1)})) %all-reduce.16.cloned.1.call-update) | async-done | bytes 98320 | tf_op jit(solution)/shard_map/psum | solution.py:323
  1025.4 8.6 bitcast_multiply_fusion
  1033.9 24.9 %scatter_custom_fusion.2 = f32[1024,2048]{1,0:T(8,128)} fusion(s32[1280]{0:T(1024)S(1)} %scatter_custom_fusion, f32[1280,2048]{1,0:T(8,128)} %bitcast_multiply_fusion, f32[]{:T(128)} %constant.54.clone.1), kind=kCustom, calls=%fused_computation.98 | custom fusion | flops 2621440 | bytes 8389120 | tf_op jit(solution)/shard_map/scatter-add | solution.py:203
  1078.0 9.5 fusion.49
  1090.2 10.2 psum.95
  1103.5 40.5 %reduce-scatter.10.cloned.1.call-done = bf16[1024,256]{0,1:T(8,128)(2,1)} async-done(((bf16[1024,2048]{0,1:T(8,128)(2,1)}), bf16[1024,256]{0,1:T(8,128)(2,1)}) %reduce-scatter.10.cloned.1.call-update) | async-done | bytes 524304 | tf_op jit(solution)/shard_map/reduce_scatter | solution.py:206
  1146.5 48.0 %reduce-scatter.12.cloned.1.call-done = bf16[1024,256]{0,1:T(8,128)(2,1)} async-done(((bf16[1024,2048]{0,1:T(8,128)(2,1)}), bf16[1024,256]{0,1:T(8,128)(2,1)}) %reduce-scatter.12.cloned.1.call-update) | async-done | bytes 524304 | tf_op jit(solution)/shard_map/reduce_scatter | solution.py:346
  (327 shorter events, 234.8 us)
Async XLA Ops:
  7.2 58.0 %copy-start = (bf16[4,8,16,2048]{3,2,1,0:T(8,128)(2,1)S(1)}, bf16[4,8,16,2048]{3,2,1,0:T(8,128)(2,1)}, u32[]{:S(2)}) copy-start(bf16[4,8,16,2048]{3,2,1,0:T(8,128)(2,1)} %param.39) | copy-start | bytes 6291460
  7.2 52.5 %copy-start.39 = (f32[2048]{0:T(1024)S(1)}, f32[2048]{0:T(1024)}, u32[]{:S(2)}) copy-start(f32[2048]{0:T(1024)} %param.26) | copy-start | bytes 24580
  7.2 49.2 %all-gather.6.cloned.1.call-start = ((), (), s32[]{:S(2)}) async-start(), calls=%async_computation.3 | async-start | bytes 4718592 | tf_op jit(solution)/shard_map/all_gather | solution.py:96
  9.5 144.0 %all-gather.14.cloned.1.call-start = ((), (), s32[]{:S(2)}) async-start(), calls=%async_computation.9 | async-start | bytes 4718592 | tf_op jit(solution)/shard_map/all_gather | solution.py:97
  11.6 298.8 %all-reduce.12.cloned.1.call-start = ((), (), s32[]{:S(2)}) async-start(), calls=%async_computation.4 | async-start | bytes 16777216 | tf_op jit(solution)/shard_map/psum | solution.py:166
  13.1 68.8 %copy-start.49 = (f32[256]{0:T(256)}, f32[256]{0:T(256)S(1)}, u32[]{:S(2)}) copy-start(f32[256]{0:T(256)S(1)} %dynamic_slice.86) | copy-start | bytes 3076
  13.9 74.1 %copy-start.51 = (f32[256]{0:T(256)}, f32[256]{0:T(256)S(1)}, u32[]{:S(2)}) copy-start(f32[256]{0:T(256)S(1)} %dynamic_slice.89) | copy-start | bytes 3076
  17.7 46.6 %copy-start.27 = (bf16[2048,16]{0,1:T(8,128)(2,1)}, bf16[2048,16]{0,1:T(8,128)(2,1)S(1)}, u32[]{:S(2)}) copy-start(bf16[2048,16]{0,1:T(8,128)(2,1)S(1)} %get-tuple-element.392) | copy-start | bytes 196612
  17.7 46.6 %copy-start.29 = (bf16[2048,16]{0,1:T(8,128)(2,1)}, bf16[2048,16]{0,1:T(8,128)(2,1)S(1)}, u32[]{:S(2)}) copy-start(bf16[2048,16]{0,1:T(8,128)(2,1)S(1)} %get-tuple-element.393) | copy-start | bytes 196612
  17.7 46.6 %copy-start.31 = (bf16[2048,16]{0,1:T(8,128)(2,1)}, bf16[2048,16]{0,1:T(8,128)(2,1)S(1)}, u32[]{:S(2)}) copy-start(bf16[2048,16]{0,1:T(8,128)(2,1)S(1)} %get-tuple-element.394) | copy-start | bytes 196612
  65.1 34.1 %copy-start.25 = (bf16[1024,48]{0,1:T(8,128)(2,1)}, bf16[1024,48]{0,1:T(8,128)(2,1)S(1)}, u32[]{:S(2)}) copy-start(bf16[1024,48]{0,1:T(8,128)(2,1)S(1)} %convolution_convert_fusion) | copy-start | bytes 294916
  66.8 23.7 %copy-start.11 = (f32[1024,256]{0,1:T(8,128)}, f32[1024,256]{0,1:T(8,128)S(1)}, u32[]{:S(2)}) copy-start(f32[1024,256]{0,1:T(8,128)S(1)} %get-tuple-element.417) | copy-start | bytes 3145732
  132.8 266.7 %all-gather.8.cloned.1.call-start = ((), (), s32[]{:S(2)}) async-start(), calls=%async_computation.5 | async-start | bytes 10485760 | tf_op jit(solution)/shard_map/all_gather | solution.py:192
  133.4 355.2 %all-gather.10.cloned.1.call-start = ((), (), s32[]{:S(2)}) async-start(), calls=%async_computation.6 | async-start | bytes 10485760 | tf_op jit(solution)/shard_map/all_gather | solution.py:193
  134.0 443.8 %all-gather.12.cloned.1.call-start = ((), (), s32[]{:S(2)}) async-start(), calls=%async_computation.7 | async-start | bytes 10485760 | tf_op jit(solution)/shard_map/all_gather | solution.py:194
  134.6 720.4 %all-reduce.14.cloned.1.call-start = ((), (), s32[]{:S(2)}) async-start(), calls=%async_computation.12 | async-start | bytes 16908288 | tf_op jit(solution)/shard_map/psum | solution.py:235
  200.0 120.3 %copy-start.47 = (f32[2048]{0:T(1024)S(1)}, f32[2048]{0:T(1024)}, u32[]{:S(2)}) copy-start(f32[2048]{0:T(1024)} %param.27) | copy-start | bytes 24580
  329.3 17.3 %copy-start.35 = (bf16[2048,16]{0,1:T(8,128)(2,1)S(1)}, bf16[2048,16]{0,1:T(8,128)(2,1)}, u32[]{:S(2)}) copy-start(bf16[2048,16]{0,1:T(8,128)(2,1)} %param.34) | copy-start | bytes 196612
  678.0 340.3 %all-reduce.16.cloned.1.call-start = ((), (), s32[]{:S(2)}) async-start(), calls=%async_computation.13 | async-start | bytes 196608 | tf_op jit(solution)/shard_map/psum | solution.py:323
  858.8 9.9 slice-start
  858.8 11.4 slice-start.1
  929.7 9.9 copy-start.50
  932.4 19.2 %copy-start.46 = (f32[1024]{0:T(1024)S(1)}, f32[1024]{0:T(1024)}, u32[]{:S(2)}) copy-start(f32[1024]{0:T(1024)} %copy-done.45) | copy-start | bytes 12292
  934.1 19.3 %copy-start.26 = (bf16[1024,48]{0,1:T(8,128)(2,1)S(1)}, bf16[1024,48]{0,1:T(8,128)(2,1)}, u32[]{:S(2)}) copy-start(bf16[1024,48]{0,1:T(8,128)(2,1)} %copy-done.25) | copy-start | bytes 294916
  934.1 20.4 %copy-start.44 = (f32[1024]{0:T(1024)S(1)}, f32[1024]{0:T(1024)}, u32[]{:S(2)}) copy-start(f32[1024]{0:T(1024)} %copy-done.43) | copy-start | bytes 12292
  941.0 18.5 %copy-start.34 = (bf16[1024,16]{0,1:T(8,128)(2,1)S(1)}, bf16[1024,16]{0,1:T(8,128)(2,1)}, u32[]{:S(2)}) copy-start(bf16[1024,16]{0,1:T(8,128)(2,1)} %copy-done.33) | copy-start | bytes 98308
  960.4 128.5 %reduce-scatter.14.cloned.1.call-start = ((), (), s32[]{:S(2)}) async-start(), calls=%async_computation.11 | async-start | bytes 40960 | tf_op jit(solution)/shard_map/reduce_scatter | solution.py:393
  961.1 139.2 %all-reduce.18.cloned.1.call-start = ((), (), s32[]{:S(2)}) async-start(), calls=%async_computation.14 | async-start | bytes 1179648
  1025.3 118.6 %reduce-scatter.10.cloned.1.call-start = ((), (), s32[]{:S(2)}) async-start(), calls=%async_computation.8 | async-start | bytes 4718592 | tf_op jit(solution)/shard_map/reduce_scatter | solution.py:206
  1066.2 128.3 %reduce-scatter.12.cloned.1.call-start = ((), (), s32[]{:S(2)}) async-start(), calls=%async_computation.10 | async-start | bytes 4718592 | tf_op jit(solution)/shard_map/reduce_scatter | solution.py:346
  1087.5 107.0 %copy-start.20 = (bf16[1024,256]{0,1:T(8,128)(2,1)S(1)}, bf16[1024,256]{0,1:T(8,128)(2,1)}, u32[]{:S(2)}) copy-start(bf16[1024,256]{0,1:T(8,128)(2,1)} %copy.129) | copy-start | bytes 1572868
  1087.5 107.0 %copy-start.42 = (f32[1024]{0:T(1024)S(1)}, f32[1024]{0:T(1024)}, u32[]{:S(2)}) copy-start(f32[1024]{0:T(1024)} %copy-done.41) | copy-start | bytes 12292
  (43 other events, 200.3 us)
Sparse Core Ops, SparseCore 0:
  9.6 46.7 all-gather.5
  58.6 46.4 all-gather.13
  132.9 177.4 all-reduce.11
  312.1 87.4 all-gather.7
  401.2 87.3 all-gather.9
  490.3 87.4 all-gather.11
  678.1 176.7 all-reduce.13
  960.5 57.7 all-reduce.15
  1021.0 24.0 reduce-scatter.13
  1048.0 46.1 all-reduce.17
  1096.5 47.4 reduce-scatter.9
  1146.1 48.3 reduce-scatter.11
where the time goes:
time: 1220 us; the launch traced here: 1210 us
  waiting for transfers between devices  668 us (55%)
  matrix products  187 us (15%)
  other arithmetic  136 us (11%)
  local copies, waits for them, and re-layouts  130 us (11%)
  blocking collectives  60.7 us (5%)
  between operations  16.9 us (1%)
    psum x1, waiting for transfers between devices, shards(): back_sum, grad_probs = lax.psum((dense_back, dprob_part), 'col')  177 us
    psum x1, waiting for transfers between devices, shards(): lax.psum((matmul(attended, w_out), matmul(attended, a_out_rows)), 'col')  110 us
    all_gather x1, waiting for transfers between devices, shards(): lax.all_gather(w_down, 'row', axis=1, tiled=True)  77.6 us
    all_gather x1, waiting for transfers between devices, shards(): lax.all_gather(w_up, 'row', axis=2, tiled=True)  77.5 us
    psum x1, waiting for transfers between devices, shards(): lax.psum(jnp.einsum('lh,rh->lr', grad_proj_query, b_query, preferred_elem...  57.1 us
    reduce_scatter x1, waiting for transfers between devices, shards(): lax.psum_scatter(normed_part.astype(jnp.bfloat16), 'col', scatter_dimensi...  48 us
    reduce_scatter x1, waiting for transfers between devices, shards(): lax.psum_scatter(dense_out.astype(jnp.bfloat16), 'col', scatter_dimension...  40.5 us
    all_gather x1, waiting for transfers between devices, shards(): lax.all_gather(w_gate, 'row', axis=2, tiled=True)  39.3 us
  transfers between devices with their start and end apart: 12, of which 9 were waited for; matrix products, arithmetic and copies ran while one was open for 21% of the time, Pallas kernels for 0%

commit v1 on v0

v1 whole, which is shorter than its diff:
```python
import functools

import jax
import jax.numpy as jnp
from jax import lax
from jax.experimental import pallas as pl
from jax.experimental.pallas import tpu as pltpu
from jax.sharding import PartitionSpec as P

HD = 128
F32, BF16 = jnp.float32, jnp.bfloat16
MESH_ID = pl.DeviceIdType.MESH
VM = pl.BlockSpec(memory_space=pltpu.VMEM)
ANY = pl.BlockSpec(memory_space=pl.ANY)
VMEM_LIMIT = 60 * 1024 * 1024

norm_eps = 1e-05
rope_base = 10000.0
masked_score = -1e30


def nn(left, right):
    return jnp.dot(left, right, preferred_element_type=F32)


def nt(left, right):
    return lax.dot_general(left, right, (((1,), (1,)), ((), ())), preferred_element_type=F32)


def tn(left, right):
    return lax.dot_general(left, right, (((0,), (0,)), ((), ())), preferred_element_type=F32)


def remote(src, dst, send_sem, recv_sem, device):
    return pltpu.make_async_remote_copy(
        src_ref=src,
        dst_ref=dst,
        send_sem=send_sem,
        recv_sem=recv_sem,
        device_id={"col": device},
        device_id_type=MESH_ID,
    )


def line_place():
    here = lax.axis_index("col")
    core = here % 2
    return here, here // 2, core, here + 1 - 2 * core


def line_barrier(chips):
    here, chip, core, mate = line_place()
    barrier = pltpu.get_barrier_semaphore()
    has_left, has_right = chip > 0, chip < chips - 1
    pl.semaphore_signal(barrier, inc=1, device_id={"col": mate}, device_id_type=MESH_ID)

    @pl.when(has_left)
    def _():
        pl.semaphore_signal(barrier, inc=1, device_id={"col": here - 2}, device_id_type=MESH_ID)

    @pl.when(has_right)
    def _():
        pl.semaphore_signal(barrier, inc=1, device_id={"col": here + 2}, device_id_type=MESH_ID)

    inner = jnp.logical_and(has_left, has_right)

    @pl.when(inner)
    def _():
        pl.semaphore_wait(barrier, 3)

    @pl.when(jnp.logical_not(inner))
    def _():
        pl.semaphore_wait(barrier, 2)


def spot(axis, size, parts, block, part):
    rows, cols = size
    step = rows // parts
    if axis == 0:
        return (pl.ds(pl.multiple_of(block * rows + part * step, 8), step), slice(None))
    return (pl.ds(part * step, step), pl.ds(pl.multiple_of(block * cols, 128), cols))


def gather_body(chips, parts, axis, x_ref, o_ref, right_sem, left_sem, mate_sem, line_recv, mate_recv, own_sem):
    here, chip, core, mate = line_place()
    size = x_ref.shape
    step = size[0] // parts
    line_barrier(chips)

    def at(block, part):
        return o_ref.at[spot(axis, size, parts, block, part)]

    def copy(j, part, sem, recv, device, first=False, block=None):
        block = 2 * j + core if block is None else block
        src = x_ref.at[pl.ds(part * step, step)] if first else at(block, part)
        return remote(src, at(block, part), sem.at[j, part], recv.at[j, part], device)

    def forward(j, part, rightward, leftward, first):
        if rightward:

            @pl.when(chip < chips - 1)
            def _():
                copy(j, part, right_sem, line_recv, here + 2, first).start()

        if leftward:

            @pl.when(chip > 0)
            def _():
                copy(j, part, left_sem, line_recv, here - 2, first).start()

        copy(j, part, mate_sem, mate_recv, mate, first).start()

    for part in range(parts):
        forward(chip, part, True, True, True)
    own = []
    for part in range(parts):
        own.append(
            pltpu.make_async_copy(x_ref.at[pl.ds(part * step, step)], at(here, part), own_sem.at[part])
        )
        own[-1].start()
    for far in range(1, chips):
        for part in range(parts):

            @pl.when(chip - far >= 0)
            def _():
                copy(chip - far, part, right_sem, line_recv, mate).wait_recv()
                forward(chip - far, part, True, False, False)

            @pl.when(chip + far < chips)
            def _():
                copy(chip + far, part, left_sem, line_recv, mate).wait_recv()
                forward(chip + far, part, False, True, False)

    for own_copy in own:
        own_copy.wait()
    for j in range(chips):
        for part in range(parts):
            copy(j, part, mate_sem, mate_recv, mate, block=2 * j + 1 - core).wait_recv()
            copy(j, part, mate_sem, mate_recv, mate).wait_send()

            @pl.when(jnp.logical_and(j <= chip, chip < chips - 1))
            def _():
                copy(j, part, right_sem, line_recv, here + 2).wait_send()

            @pl.when(jnp.logical_and(j >= chip, chip > 0))
            def _():
                copy(j, part, left_sem, line_recv, here - 2).wait_send()


def line_gather(x, chips, axis, ident, parts=2):
    rows, cols = x.shape
    sems = pltpu.SemaphoreType.DMA((chips, parts))
    shape = (2 * chips * rows, cols) if axis == 0 else (rows, 2 * chips * cols)
    return pl.pallas_call(
        functools.partial(gather_body, chips, parts, axis),
        out_shape=jax.ShapeDtypeStruct(shape, x.dtype),
        in_specs=[VM],
        out_specs=VM,
        scratch_shapes=[sems] * 5 + [pltpu.SemaphoreType.DMA((parts,))],
        compiler_params=pltpu.CompilerParams(
            collective_id=ident, has_side_effects=True, vmem_limit_bytes=VMEM_LIMIT
        ),
        name="line_gather",
    )(x)


def reduce_body(
    chips, parts, axis, p_ref, o_ref, pair_buf, line_buf, sums, right_sem, left_sem, mate_sem, line_recv, mate_recv
):
    here, chip, core, mate = line_place()
    size = o_ref.shape
    step = size[0] // parts
    line_barrier(chips)

    def rows(part):
        return pl.ds(part * step, step)

    def at(block, part):
        return spot(axis, size, parts, block, part)

    def mate_copy(j, part):
        return remote(
            p_ref.at[at(2 * j + 1 - core, part)],
            pair_buf.at[j, rows(part)],
            mate_sem.at[j, part],
            mate_recv.at[j, part],
            mate,
        )

    def line_copy(j, slot, part, sem, device):
        return remote(
            sums.at[j, rows(part)], line_buf.at[slot, rows(part)], sem.at[j, part], line_recv.at[slot, part], device
        )

    for far in range(chips - 1, -1, -1):
        for part in range(parts):

            @pl.when(chip + far < chips)
            def _():
                mate_copy(chip + far, part).start()

            if far > 0:

                @pl.when(chip - far >= 0)
                def _():
                    mate_copy(chip - far, part).start()

    def pair_sum(j, part):
        mate_copy(j, part).wait_recv()
        return p_ref[at(2 * j + core, part)].astype(F32) + pair_buf[j, rows(part)].astype(F32)

    def pass_on(j, slot, part, more, sem, device):
        @pl.when(more)
        def _():
            line_copy(j, j, part, sem, mate).wait_recv()
            total = pair_sum(j, part) + line_buf[j, rows(part)].astype(F32)
            sums[j, rows(part)] = total.astype(BF16)

        @pl.when(jnp.logical_not(more))
        def _():
            sums[j, rows(part)] = pair_sum(j, part).astype(BF16)

        line_copy(j, slot, part, sem, device).start()

    for far in range(chips - 1, 0, -1):
        for part in range(parts):

            @pl.when(chip + far < chips)
            def _():
                pass_on(chip + far, chip + far, part, chip > 0, right_sem, here + 2)

            @pl.when(chip - far >= 0)
            def _():
                pass_on(
                    chip - far, chips if far == 1 else chip - far, part, chip < chips - 1, left_sem, here - 2
                )

    for part in range(parts):
        o_ref[rows(part)] = pair_sum(chip, part)

        @pl.when(chip > 0)
        def _():
            line_copy(chip, chip, part, right_sem, mate).wait_recv()
            o_ref[rows(part)] += line_buf[chip, rows(part)].astype(F32)

        @pl.when(chip < chips - 1)
        def _():
            line_copy(chip, chips, part, left_sem, mate).wait_recv()
            o_ref[rows(part)] += line_buf[chips, rows(part)].astype(F32)

    for j in range(chips):
        for part in range(parts):
            mate_copy(j, part).wait_send()

            @pl.when(j > chip)
            def _():
                line_copy(j, j, part, right_sem, mate).wait_send()

            @pl.when(j < chip)
            def _():
                line_copy(j, j, part, left_sem, mate).wait_send()


def line_reduce(p, chips, axis, ident, parts=2):
    rows, cols = p.shape
    if axis == 0:
        rows //= 2 * chips
    else:
        cols //= 2 * chips
    sems = pltpu.SemaphoreType.DMA((chips, parts))
    return pl.pallas_call(
        functools.partial(reduce_body, chips, parts, axis),
        out_shape=jax.ShapeDtypeStruct((rows, cols), F32),
        in_specs=[VM],
        out_specs=VM,
        scratch_shapes=[
            pltpu.VMEM((chips, rows, cols), BF16),
            pltpu.VMEM((chips + 1, rows, cols), BF16),
            pltpu.VMEM((chips, rows, cols), BF16),
            sems,
            sems,
            sems,
            pltpu.SemaphoreType.DMA((chips + 1, parts)),
            sems,
        ],
        compiler_params=pltpu.CompilerParams(
            collective_id=ident, has_side_effects=True, vmem_limit_bytes=VMEM_LIMIT
        ),
        name="line_reduce",
    )(p)


def small_body(count, x_ref, o_ref, send_sem, recv_sem):
    here = lax.axis_index("col")
    barrier = pltpu.get_barrier_semaphore()
    for hop in range(1, count):
        other = lax.rem(here + hop, count)
        pl.semaphore_signal(barrier, inc=1, device_id={"col": other}, device_id_type=MESH_ID)
    o_ref[here] = x_ref[...]
    pl.semaphore_wait(barrier, count - 1)

    def copy(hop, block):
        other = lax.rem(here + hop, count)
        return remote(x_ref, o_ref.at[block], send_sem.at[hop], recv_sem.at[hop], other)

    for hop in range(1, count):
        copy(hop, here).start()
    for hop in range(1, count):
        copy(hop, lax.rem(here + count - hop, count)).wait_recv()
    for hop in range(1, count):
        copy(hop, here).wait_send()


def small_gather(x, count, ident):
    sems = pltpu.SemaphoreType.DMA((count,))
    return pl.pallas_call(
        functools.partial(small_body, count),
        out_shape=jax.ShapeDtypeStruct((count,) + x.shape, x.dtype),
        in_specs=[VM],
        out_specs=VM,
        scratch_shapes=[sems, sems],
        compiler_params=pltpu.CompilerParams(collective_id=ident, has_side_effects=True),
        name="small_gather",
    )(x)


def moe_body(count, pieces, tile, x_ref, g_ref, gates_ref, *refs):
    weights = refs[: 3 * count]
    out_ref, dx_ref, dgate_ref, out_acc, dx_acc, wgu, wd, sems = refs[3 * count :]
    experts = weights[0].shape[0]
    hidden = wd.shape[1]
    tokens = x_ref.shape[0]
    each = experts * pieces
    steps = count * each

    def copies(a, step, slot):
        gate, up, down = weights[3 * a : 3 * a + 3]
        e, piece = step % experts, (step % each) // experts
        units = pl.ds(pl.multiple_of(piece * hidden, 128), hidden)
        return (
            pltpu.make_async_copy(gate.at[e, :, units], wgu.at[slot, :, pl.ds(0, hidden)], sems.at[slot, 0]),
            pltpu.make_async_copy(up.at[e, :, units], wgu.at[slot, :, pl.ds(hidden, hidden)], sems.at[slot, 1]),
            pltpu.make_async_copy(down.at[e, units], wd.at[slot], sems.at[slot, 2]),
        )

    def fetch(step, slot):
        for a in range(count):

            @pl.when(step // each == a)
            def _():
                for copy in copies(a, step, slot):
                    copy.start()

    fetch(0, 0)
    out_acc[...] = jnp.zeros_like(out_acc)
    dx_acc[...] = jnp.zeros_like(dx_acc)
    dgate_ref[...] = jnp.zeros_like(dgate_ref)

    def one_step(step, carry):
        slot = step % 2
        for copy in copies(0, 0, slot):
            copy.wait()

        @pl.when(step + 1 < steps)
        def _():
            fetch(step + 1, 1 - slot)

        e = step % experts

        def one_tile(t, carry):
            rows = pl.ds(pl.multiple_of(t * tile, tile), tile)
            mine = lax.broadcasted_iota(jnp.int32, (tile, experts), 1) == e
            gate = jnp.sum(jnp.where(mine, gates_ref[rows], 0.0), axis=1, keepdims=True)
            both = nn(x_ref[rows], wgu[slot])
            gate_in, up_in = both[:, :hidden], both[:, hidden:]
            sigmoid = jax.nn.sigmoid(gate_in)
            silu = gate_in * sigmoid
            active = silu * up_in
            back = nt(g_ref[rows], wd[slot])
            dgate_ref[rows] += jnp.where(mine, jnp.sum(active * back, axis=1, keepdims=True), 0.0)
            out_acc[rows] += nn((active * gate).astype(BF16), wd[slot])
            d_active = back * gate
            d_gate_in = d_active * up_in * (sigmoid + silu * (1.0 - sigmoid))
            d_up_in = d_active * silu
            d_both = jnp.concatenate([d_gate_in.astype(BF16), d_up_in.astype(BF16)], axis=1)
            dx_acc[rows] += nt(d_both, wgu[slot])
            return carry

        return lax.fori_loop(0, tokens // tile, one_tile, carry)

    lax.fori_loop(0, steps, one_step, 0)
    out_ref[...] = out_acc[...].astype(out_ref.dtype)
    dx_ref[...] = dx_acc[...].astype(dx_ref.dtype)


def moe(x, g, gates, weights, tile=512):
    tokens, width = x.shape
    experts, _, units = weights[0].shape
    hidden = min(256, units)
    count = len(weights) // 3
    return pl.pallas_call(
        functools.partial(moe_body, count, units // hidden, min(tile, tokens)),
        out_shape=(
            jax.ShapeDtypeStruct((tokens, width), BF16),
            jax.ShapeDtypeStruct((tokens, width), BF16),
            jax.ShapeDtypeStruct(gates.shape, F32),
        ),
        in_specs=[VM, VM, VM] + [ANY] * (3 * count),
        out_specs=(VM, VM, VM),
        scratch_shapes=[
            pltpu.VMEM((tokens, width), F32),
            pltpu.VMEM((tokens, width), F32),
            pltpu.VMEM((2, width, 2 * hidden), BF16),
            pltpu.VMEM((2, hidden, width), BF16),
            pltpu.SemaphoreType.DMA((2, 3)),
        ],
        compiler_params=pltpu.CompilerParams(vmem_limit_bytes=VMEM_LIMIT),
        name="moe",
    )(x, g, gates, *weights)


def rope_tables(length, head_dim):
    half_dim = head_dim // 2
    frequency = rope_base ** (-(2.0 * jnp.arange(half_dim, dtype=F32)) / head_dim)
    angles = jnp.arange(length, dtype=F32)[:, None] * frequency[None, :]
    return (jnp.cos(angles), jnp.sin(angles))


def rotate(values, cosine_table, sine_table):
    half_dim = values.shape[-1] // 2
    first_half = values[..., :half_dim]
    second_half = values[..., half_dim:]
    return jnp.concatenate(
        [
            first_half * cosine_table - second_half * sine_table,
            second_half * cosine_table + first_half * sine_table,
        ],
        axis=-1,
    )


def unrotate(values, cosine_table, sine_table):
    return rotate(values, cosine_table, -sine_table)


def shards(
    inputs,
    cotangent,
    norm_first,
    norm_second,
    query_gain,
    key_gain,
    w_query,
    w_key,
    w_value,
    w_out,
    w_router,
    w_gate,
    w_up,
    w_down,
    adapter_a,
    adapter_b,
    adapter_router,
    routes,
    prefix,
    adapter_index,
):
    seq_len, width_part = inputs.shape
    col_count = lax.axis_size("col")
    row_count = lax.axis_size("row")
    col_index = lax.axis_index("col")
    row_index = lax.axis_index("row")
    chips = col_count // 2
    full_width = width_part * col_count
    head_width = w_query.shape[1]
    head_count = head_width // HD
    local_experts = w_gate.shape[0]
    feature_start = col_index * width_part
    head_start = col_index * head_width
    own_rows = seq_len // col_count
    row_start = col_index * own_rows
    score_scale = HD ** (-0.5)

    def columns(array, axis_num):
        return lax.dynamic_slice_in_dim(array, feature_start, width_part, axis_num)

    def head_cols(array):
        return lax.dynamic_slice_in_dim(array, head_start, head_width, 1)

    def held_rows(array):
        return lax.dynamic_slice_in_dim(array, row_start, own_rows, 0)

    def col_sum(pair, ident):
        packed = jnp.stack(pair).reshape(-1, 128)
        return jnp.sum(small_gather(packed, col_count, ident), axis=0).reshape(len(pair), seq_len)

    full_gate, full_up, full_down = (
        lax.all_gather(w_gate, "row", axis=2, tiled=True),
        lax.all_gather(w_up, "row", axis=2, tiled=True),
        lax.all_gather(w_down, "row", axis=1, tiled=True),
    )
    adapter_slot = adapter_index[0]
    chosen_a = lax.dynamic_index_in_dim(adapter_a, adapter_slot, 1, keepdims=False)
    chosen_b = lax.dynamic_index_in_dim(adapter_b, adapter_slot, 1, keepdims=False)
    chosen_router = lax.dynamic_index_in_dim(adapter_router, adapter_slot, 0, keepdims=False)
    rank_count = chosen_a.shape[2]
    a_three = jnp.concatenate([chosen_a[0], chosen_a[1], chosen_a[2]], axis=1)
    b_query = head_cols(chosen_b[0])
    b_key = head_cols(chosen_b[1])
    b_value = head_cols(chosen_b[2])
    a_out_rows = lax.dynamic_slice_in_dim(chosen_a[3], head_start, head_width, 0)
    out_map = (w_out.astype(F32) + nn(a_out_rows, chosen_b[3])).astype(BF16)
    router_map = w_router.astype(F32) + nn(chosen_a[4], chosen_router)

    full_inputs = line_gather(inputs, chips, 1, 0)
    input_f32 = full_inputs.astype(F32)
    inv_first = lax.rsqrt(jnp.mean(input_f32 * input_f32, axis=1, keepdims=True) + norm_eps)
    normed = (input_f32 * inv_first * norm_first).astype(BF16)
    middle = nn(normed, a_three).astype(BF16)
    mid_query = middle[:, :rank_count]
    mid_key = middle[:, rank_count : 2 * rank_count]
    mid_value = middle[:, 2 * rank_count :]
    proj_query = nn(normed, w_query) + nn(mid_query, b_query)
    proj_key = nn(normed, w_key) + nn(mid_key, b_key)
    proj_value = nn(normed, w_value) + nn(mid_value, b_value)
    square_sums = col_sum(
        (jnp.sum(proj_query * proj_query, axis=1), jnp.sum(proj_key * proj_key, axis=1)), 1
    )
    inv_query = lax.rsqrt(square_sums[0] / full_width + norm_eps)[:, None]
    inv_key = lax.rsqrt(square_sums[1] / full_width + norm_eps)[:, None]
    gain_query = lax.dynamic_slice_in_dim(query_gain, head_start, head_width, 0)
    gain_key = lax.dynamic_slice_in_dim(key_gain, head_start, head_width, 0)
    cosine_table, sine_table = rope_tables(seq_len, HD)
    cosine_table = cosine_table[:, None, :]
    sine_table = sine_table[:, None, :]
    rot_query = rotate(
        (proj_query * inv_query * gain_query).reshape(seq_len, head_count, HD),
        cosine_table,
        sine_table,
    ).astype(BF16)
    rot_key = rotate(
        (proj_key * inv_key * gain_key).reshape(seq_len, head_count, HD), cosine_table, sine_table
    ).astype(BF16)
    value_rows = proj_value.astype(BF16).reshape(seq_len, head_count, HD)
    block_rows = min(512, seq_len)
    starts = jnp.arange(seq_len // block_rows, dtype=jnp.int32) * block_rows
    key_pos = jnp.arange(seq_len, dtype=jnp.int32)
    prefix_len = prefix[0]

    def block_scores(start_row):
        block_query = lax.dynamic_slice_in_dim(rot_query, start_row, block_rows, 0)
        query_pos = start_row + jnp.arange(block_rows, dtype=jnp.int32)
        allowed = (key_pos[None, :] <= query_pos[:, None]) | (key_pos[None, :] < prefix_len)
        raw_scores = (
            jnp.einsum("qhd,khd->hqk", block_query, rot_key, preferred_element_type=F32)
            * score_scale
        )
        return (block_query, jnp.where(allowed[None], raw_scores, masked_score))

    def attend_block(start_row):
        block_query, scores = block_scores(start_row)
        row_max = jnp.max(scores, axis=2, keepdims=True)
        exponent = jnp.exp(scores - row_max)
        row_total = jnp.sum(exponent, axis=2, keepdims=True)
        weights = (exponent / row_total).astype(BF16)
        attended_block = jnp.einsum(
            "hqk,khd->qhd", weights, value_rows, preferred_element_type=F32
        )
        return (attended_block.astype(BF16), (row_max + jnp.log(row_total))[:, :, 0])

    attended_blocks, log_totals = lax.map(attend_block, starts)
    attended = attended_blocks.reshape(seq_len, head_width)
    out_rows = line_reduce(nn(attended, out_map).astype(BF16), chips, 0, 2)
    hidden_rows = held_rows(full_inputs).astype(F32) + out_rows
    hidden = line_gather(hidden_rows.astype(BF16), chips, 0, 3)
    full_cot = line_gather(cotangent, chips, 1, 4)
    mid_out = jnp.sum(
        small_gather(nn(attended, a_out_rows).astype(BF16).reshape(-1, 128), col_count, 5).astype(F32), axis=0
    ).reshape(seq_len, rank_count).astype(BF16)

    hidden_f32 = hidden.astype(F32)
    inv_second = lax.rsqrt(jnp.mean(hidden_f32 * hidden_f32, axis=1, keepdims=True) + norm_eps)
    normed_two = (hidden_f32 * inv_second * norm_second).astype(BF16)
    mid_router = nn(normed_two, chosen_a[4]).astype(BF16)
    logits = nn(normed_two, w_router) + nn(mid_router, chosen_router)
    router_probs = jax.nn.softmax(logits, axis=1)
    expert_total = router_probs.shape[1]
    own_ids = col_index * local_experts + jnp.arange(local_experts, dtype=jnp.int32)
    member = jnp.any(routes[:, :, None] == own_ids[None, None, :], axis=1)
    own_probs = lax.dynamic_slice_in_dim(router_probs, col_index * local_experts, local_experts, 1)
    gates = jnp.where(member, own_probs, 0.0)
    moe_out, back_out, d_gate = moe(normed_two, full_cot, gates, (full_gate, full_up, full_down))
    d_gate = jnp.where(member, d_gate, 0.0)
    grad_probs = small_gather(d_gate.T.reshape(-1, 128), col_count, 6).reshape(expert_total, seq_len).T
    grad_logits = (
        router_probs * (grad_probs - jnp.sum(router_probs * grad_probs, axis=1, keepdims=True))
    ).astype(BF16)
    back_rows = line_reduce(back_out, chips, 0, 7)
    grad_normed_two = back_rows + nt(held_rows(grad_logits).astype(F32), router_map)
    hidden_held = held_rows(hidden).astype(F32)
    inv_held = held_rows(inv_second)
    scaled_two = grad_normed_two * norm_second
    grad_hidden_rows = (
        held_rows(full_cot).astype(F32)
        + inv_held * scaled_two
        - hidden_held * inv_held * inv_held * inv_held * jnp.mean(hidden_held * scaled_two, axis=1, keepdims=True)
    )
    grad_attn = line_gather(grad_hidden_rows.astype(BF16), chips, 0, 8)
    layer_out = (columns(hidden, 1).astype(F32) + line_reduce(moe_out, chips, 1, 9)).astype(BF16)

    grad_mid_router = nt(grad_logits, chosen_router).astype(BF16)
    grad_mid_out = nt(grad_attn, chosen_b[3]).astype(BF16)
    grad_attended = nt(grad_attn, out_map).astype(BF16)
    grad_b_out = tn(mid_out, columns(grad_attn, 1))
    grad_a_out = tn(attended, grad_mid_out)
    grad_heads = grad_attended.reshape(seq_len, head_count, HD)

    def back_block(carried, packed):
        key_acc, value_acc = carried
        start_row, log_total = packed
        block_query, scores = block_scores(start_row)
        weights = jnp.exp(scores - log_total[:, :, None])
        block_grad = lax.dynamic_slice_in_dim(grad_heads, start_row, block_rows, 0)
        grad_weights = jnp.einsum("qhd,khd->hqk", block_grad, value_rows, preferred_element_type=F32)
        row_dot = jnp.sum(weights * grad_weights, axis=2, keepdims=True)
        grad_scores = (weights * (grad_weights - row_dot)).astype(BF16)
        query_block = (
            jnp.einsum("hqk,khd->qhd", grad_scores, rot_key, preferred_element_type=F32)
            * score_scale
        )
        key_acc = (
            key_acc
            + jnp.einsum("hqk,qhd->khd", grad_scores, block_query, preferred_element_type=F32)
            * score_scale
        )
        value_acc = value_acc + jnp.einsum(
            "hqk,qhd->khd", weights.astype(BF16), block_grad, preferred_element_type=F32
        )
        return ((key_acc, value_acc), query_block)

    zero_heads = jnp.zeros((seq_len, head_count, HD), F32)
    (grad_key_rot, grad_value_all), query_blocks = lax.scan(
        back_block, (zero_heads, zero_heads), (starts, log_totals)
    )
    grad_query_rot = query_blocks.reshape(seq_len, head_count, HD)
    scaled_query = (
        unrotate(grad_query_rot, cosine_table, sine_table).reshape(seq_len, head_width) * gain_query
    )
    scaled_key = (
        unrotate(grad_key_rot, cosine_table, sine_table).reshape(seq_len, head_width) * gain_key
    )
    norm_stats = col_sum(
        (jnp.sum(proj_query * scaled_query, axis=1), jnp.sum(proj_key * scaled_key, axis=1)), 10
    )
    grad_proj_query = (
        inv_query * scaled_query
        - proj_query * inv_query * inv_query * inv_query * norm_stats[0][:, None] / full_width
    ).astype(BF16)
    grad_proj_key = (
        inv_key * scaled_key
        - proj_key * inv_key * inv_key * inv_key * norm_stats[1][:, None] / full_width
    ).astype(BF16)
    grad_proj_value = grad_value_all.reshape(seq_len, head_width).astype(BF16)
    part_query = nt(grad_proj_query, b_query).astype(BF16)
    part_key = nt(grad_proj_key, b_key).astype(BF16)
    part_value = nt(grad_proj_value, b_value).astype(BF16)
    part_middle = jnp.concatenate([part_query, part_key, part_value], axis=1)
    normed_part = (
        nt(grad_proj_query, w_query) + nt(grad_proj_key, w_key) + nt(grad_proj_value, w_value)
        + nt(part_middle, a_three)
    )
    first_stat = jnp.sum(input_f32 * norm_first * normed_part, axis=1)
    total_stat = col_sum((first_stat,), 11)[0]
    normed_own = line_reduce(normed_part.astype(BF16), chips, 1, 12)
    grad_inputs = (
        columns(grad_attn, 1).astype(F32)
        + inv_first * columns(norm_first, 0) * normed_own
        - inputs.astype(F32) * inv_first * inv_first * inv_first * total_stat[:, None] / full_width
    )
    grad_middle = jnp.sum(
        small_gather(part_middle.reshape(-1, 128), col_count, 13).astype(F32), axis=0
    ).reshape(seq_len, 3 * rank_count).astype(BF16)
    grad_a_three = tn(columns(normed, 1), grad_middle)
    grad_a_router = tn(columns(normed_two, 1), grad_mid_router)
    grad_a_stack = jnp.stack(
        [
            grad_a_three[:, :rank_count],
            grad_a_three[:, rank_count : 2 * rank_count],
            grad_a_three[:, 2 * rank_count :],
            grad_a_out,
            grad_a_router,
        ]
    )
    grad_b_stack = jnp.stack(
        [
            tn(mid_query, grad_proj_query),
            tn(mid_key, grad_proj_key),
            tn(mid_value, grad_proj_value),
            grad_b_out,
        ]
    )
    grad_router_one = tn(mid_router, grad_logits)
    adapter_count = adapter_a.shape[1]
    held_adapters = adapter_count // row_count
    flat = jnp.concatenate(
        [
            grad_a_stack.reshape(-1, 128),
            grad_b_stack.reshape(-1, 128),
            grad_router_one.reshape(-1, 128),
            jnp.broadcast_to(adapter_slot.astype(F32), (8, 128)),
        ]
    ).astype(BF16)
    every = lax.all_gather(flat, "row", axis=0).astype(F32)
    owners = every[:, -1, 0]
    held_ids = (row_index * held_adapters + jnp.arange(held_adapters)).astype(F32)
    pick = (owners[None, :] == held_ids[:, None]).astype(F32)
    summed = jnp.sum(pick[:, :, None, None] * every[None], axis=1)
    a_lines = grad_a_stack.size // 128
    b_lines = grad_b_stack.size // 128
    r_lines = grad_router_one.size // 128
    grad_a = summed[:, :a_lines].reshape((held_adapters,) + grad_a_stack.shape).transpose(1, 0, 2, 3)
    grad_b = summed[:, a_lines : a_lines + b_lines].reshape((held_adapters,) + grad_b_stack.shape)
    grad_b = grad_b.transpose(1, 0, 2, 3)
    grad_router = summed[:, a_lines + b_lines : a_lines + b_lines + r_lines].reshape(
        (held_adapters,) + grad_router_one.shape
    )
    return (layer_out, grad_inputs, grad_a, grad_b, grad_router)


def solution(mesh):
    placed = (
        P("row", "col"),
        P("row", "col"),
        P(),
        P(),
        P(),
        P(),
        P(None, "col"),
        P(None, "col"),
        P(None, "col"),
        P("col", None),
        P(),
        P("col", None, "row"),
        P("col", None, "row"),
        P("col", "row", None),
        P(),
        P(),
        P(),
        P("row", None),
        P("row"),
        P("row"),
    )
    return jax.shard_map(
        shards,
        mesh=mesh,
        in_specs=placed,
        out_specs=(
            P("row", "col"),
            P("row", "col"),
            P(None, "row", "col", None),
            P(None, "row", None, "col"),
            P("row", None, None),
        ),
        check_vma=False,
    )
```

time: 1220 us -> 721 us (0.59)
  waiting for transfers between devices: 668 us -> 2.06 us
  Pallas kernels: 0 us -> 456 us
  local copies, waits for them, and re-layouts: 130 us -> 38.7 us
  matrix products: 187 us -> 113 us
  other arithmetic: 136 us -> 67.9 us
  blocking collectives: 60.7 us -> 9.42 us
    pallas_call x0 -> x15, Pallas kernels: none -> 456 us  [the longest x4 167 us: line_reduce(): pl.pallas_call(functools.partial(reduce_body, chips, parts, axis), out_sh...]
    psum x3 -> x0, waiting for transfers between devices: 344 us -> none  [the longest x1 177 us: shards(): back_sum, grad_probs = lax.psum((dense_back, dprob_part), 'col')]
    reduce_scatter x3 -> x0, waiting for transfers between devices: 88.5 us -> none  [the longest x1 48 us: shards(): lax.psum_scatter(normed_part.astype(jnp.bfloat16), 'col', scatter_dimensi...]
    all_gather x1, waiting for transfers between devices: 77.6 us -> 0.01 us  [shards(): lax.all_gather(w_down, 'row', axis=1, tiled=True)]
    all_gather x1, waiting for transfers between devices: 77.5 us -> 0.01 us  [shards(): lax.all_gather(w_up, 'row', axis=2, tiled=True)]
    dot_general x50 -> x40, matrix products: 177 us -> 99.5 us  [the longest x9 35.2 us: nt(): lax.dot_general(left, right, (((1,), (1,)), ((), ())), preferred_element_...]
    psum x4 -> x0, blocking collectives: 60.7 us -> none  [the longest x1 25 us: shards(): lax.psum((matmul(attended, w_out), matmul(attended, a_out_rows)), 'col')]
    scatter-add x3 -> x0, other arithmetic: 59.2 us -> none  [the longest x1 25 us: shards(): jax.ops.segment_sum(expert_back, slot_token, num_segments=seq_len)]
  transfers between devices with their start and end apart: 12 -> 3, of which waited for: 9 -> 0; matrix products, arithmetic and copies ran while one was open for 21% -> 13% of each run, Pallas kernels for 0% -> 26%
where the time goes in v1:
time: 721 us; the launch traced here: 711 us
  Pallas kernels  456 us (63%)
  matrix products  113 us (16%)
  other arithmetic  67.9 us (9%)
  local copies, waits for them, and re-layouts  38.7 us (5%)
  between operations  15.6 us (2%)
  blocking collectives  9.42 us (1%)
  loops' own time  8.48 us (1%)
    pallas_call x4, Pallas kernels, line_reduce(): pl.pallas_call(functools.partial(reduce_body, chips, parts, axis), out_sh...  167 us
    pallas_call x4, Pallas kernels, line_gather(): pl.pallas_call(functools.partial(gather_body, chips, parts, axis), out_sh...  156 us
    pallas_call x1, Pallas kernels, moe(): pl.pallas_call(functools.partial(moe_body, count, units // hidden, min(ti...  66.3 us
    pallas_call x6, Pallas kernels, small_gather(): pl.pallas_call(functools.partial(small_body, count), out_shape=jax.ShapeD...  66 us
    dot_general x9, matrix products, nt(): lax.dot_general(left, right, (((1,), (1,)), ((), ())), preferred_element_...  35.2 us
    dot_general x13, matrix products, nn(): return jnp.dot(left, right, preferred_element_type=F32)  28.5 us
  transfers between devices with their start and end apart: 3, of which 0 were waited for; matrix products, arithmetic and copies ran while one was open for 13% of the time, Pallas kernels for 26%

profile of v1, /device:TPU:16, one launch (start us, length us, event | category | flops | bytes accessed | tf_op | source)
XLA Modules:
  0.0 710.5 jit_solution(1562747747168145097)
XLA Ops:
  10.1 38.7 %line_gather.4 = bf16[1024,2048]{1,0:T(8,128)(2,1)} custom-call(bf16[1024,256]{1,0:T(8,128)(2,1)} %x_ref.2), custom_call_target="tpu_custom_call" | custom-call | tf_op jit(solution)/shard_map/line_gather/pallas_call | solution.py:154
  51.9 3.5 fusion.50
  61.1 3.7 convolution_convert_fusion.2
  68.5 9.3 %small_gather.6 = f32[8,16,128]{2,1,0:T(8,128)} custom-call(f32[16,128]{1,0:T(8,128)} %reshape.454.x_ref), custom_call_target="tpu_custom_call" | custom-call | tf_op jit(solution)/shard_map/small_gather/pallas_call | solution.py:316
  90.0 3.8 fusion.137
  106.6 21.2 %while.30 = (s32[]{:T(128)}, bf16[2,512,2,128]{3,2,1,0:T(2,128)(2,1)S(1)}, f32[2,2,512]{2,1,0:T(2,128)S(1)}, s32[2]{0:T(128)S(1)}, s32[]{:T(128)}, /*index=5*/bf...) while((s32[]{:T(128)}, ...), condition=%wide.region_7.8_spmd.clone.clone, body=%wide.region_4.7_spmd.clone.clone.sunk | while | flops 550633984 | bytes 16816304 | solution.py:571
  127.8 4.7 convolution_convert_fusion.p_ref
  132.6 41.8 %line_reduce.4 = f32[128,2048]{1,0:T(8,128)} custom-call(bf16[1024,2048]{1,0:T(8,128)(2,1)} %convolution_convert_fusion.p_ref), custom_call_target="tpu_custom_call" | custom-call | tf_op jit(solution)/shard_map/line_reduce/pallas_call | solution.py:271
  176.7 38.1 %line_gather.5 = bf16[1024,2048]{1,0:T(8,128)(2,1)} custom-call(bf16[128,2048]{1,0:T(8,128)(2,1)} %add_convert_fusion.1.x_ref), custom_call_target="tpu_custom_call" | custom-call | tf_op jit(solution)/shard_map/line_gather/pallas_call | solution.py:154
  215.2 41.2 %line_gather.6.g_ref = bf16[1024,2048]{1,0:T(8,128)(2,1)} custom-call(bf16[1024,256]{1,0:T(8,128)(2,1)} %x_ref.3), custom_call_target="tpu_custom_call" | custom-call | tf_op jit(solution)/shard_map/line_gather/pallas_call | solution.py:154
  261.6 12.1 %small_gather.11 = bf16[8,128,128]{2,1,0:T(8,128)(2,1)} custom-call(bf16[128,128]{1,0:T(8,128)(2,1)} %reshape.467.x_ref), custom_call_target="tpu_custom_call" | custom-call | tf_op jit(solution)/shard_map/small_gather/pallas_call | solution.py:316
  286.3 66.3 %moe.1 = (bf16[1024,2048]{1,0:T(8,128)(2,1)}, bf16[1024,2048]{1,0:T(8,128)(2,1)}, f32[1024,2]{1,0:T(8,128)}) custom-call(bf16[1024,2048]{1,0:T(8,128)(2,1)} %copy-done.3, bf16[1024,2048]{1,0:T(8,128)(2,1)} %line_gather.6.g_ref, f32[1024,2]{1,0:T(8,128)} %dynamic-slice_select_fusion.gates_ref, bf16[2,2048,1024]{2,1,0:T(8,128)(2,1)} %all-gather.4.cloned.1.call-done.refs_0_, ...), custom_call_target="tpu_custom_call" | custom-call | tf_op jit(solution)/shard_map/moe/pallas_call | solution.py:401
  356.3 8.0 %small_gather.7 = f32[8,16,128]{2,1,0:T(8,128)} custom-call(f32[16,128]{1,0:T(8,128)} %reshape.459.x_ref), custom_call_target="tpu_custom_call" | custom-call | tf_op jit(solution)/shard_map/small_gather/pallas_call | solution.py:316
  369.2 41.8 %line_reduce.6 = f32[128,2048]{1,0:T(8,128)} custom-call(bf16[1024,2048]{1,0:T(8,128)(2,1)} %get-tuple-element.128.p_ref), custom_call_target="tpu_custom_call" | custom-call | tf_op jit(solution)/shard_map/line_reduce/pallas_call | solution.py:271
  416.6 38.0 %line_gather.7 = bf16[1024,2048]{1,0:T(8,128)(2,1)} custom-call(bf16[128,2048]{1,0:T(8,128)(2,1)} %fusion.72.x_ref), custom_call_target="tpu_custom_call" | custom-call | tf_op jit(solution)/shard_map/line_gather/pallas_call | solution.py:154
  454.7 4.6 convolution_convert_fusion.1
  459.2 42.8 %while.31 = (s32[]{:T(128)}, f32[1024,2,128]{0,2,1:T(8,128)}, f32[1024,2,128]{0,2,1:T(8,128)}, f32[2,512,2,128]{3,1,0,2:T(8,128)}, s32[2]{0:T(128)S(1)}, /*index...) while((s32[]{:T(128)}, f32[1024,2,128]{0,2,1:T(8,128)}, ...), condition=%wide.region_16.17_spmd.clone.clone, body=%wide.region_14.16_spmd.clone.clone.sunk | while | flops 1360396800 | bytes 78678856 | solution.py:642
  470.7 3.4 fusion.217
  491.2 3.6 fusion.217
  497.9 3.7 fusion.218
  504.6 3.4 multiply_subtract_fusion.2
  510.6 9.3 %small_gather.8 = f32[8,16,128]{2,1,0:T(8,128)} custom-call(f32[16,128]{1,0:T(8,128)} %reshape.465.x_ref), custom_call_target="tpu_custom_call" | custom-call | tf_op jit(solution)/shard_map/small_gather/pallas_call | solution.py:316
  532.4 21.1 %small_gather.10 = bf16[8,384,128]{2,1,0:T(8,128)(2,1)} custom-call(bf16[384,128]{1,0:T(8,128)(2,1)} %reshape.466.x_ref), custom_call_target="tpu_custom_call" | custom-call | tf_op jit(solution)/shard_map/small_gather/pallas_call | solution.py:316
  557.1 3.6 fusion.62
  566.3 9.4 %all_gather.16 = bf16[4,298,128]{2,1,0:T(8,128)(2,1)S(1)} all-gather(bf16[1,298,128]{2,1,0:T(8,128)(2,1)S(1)} %maximum_maximum_fusion), channel_id=1, replica_groups=mesh['row'=4,'col'=8] {'row'}, dimensions={0}, use_global_device_ids=true | all-gather | bytes 381440 | tf_op jit(solution)/shard_map/all_gather | solution.py:713
  577.6 4.5 fusion.92
  582.2 4.5 fusion.139
  586.7 4.6 fusion.140
  596.5 13.4 %fusion.52 = (f32[1024]{0:T(1024)}, bf16[1024,2048]{1,0:T(8,128)(2,1)}) fusion(bf16[1024,2048]{1,0:T(8,128)(2,1)} %line_gather.4, f32[2048]{0:T(1024)S(1)} %copy-done.51, f32[1024,2048]{1,0:T(8,128)} %fusion.92, bf16[1024,256]{0,1:T(8,128)(2,1)S(1)} %bitcast.240, bf16[2048,256]{1,0:T(8,128)(2,1)} %param.32, f32[1024,2048]{1,0:T(8,128)} %fusion.139, ...), kind=kOutput, calls=%fused_computation.67 | convolution fusion | flops 1090518016 | bytes 35139584 | tf_op jit(solution)/shard_map/dot_general | solution.py:27
  609.9 41.9 %line_reduce.7 = f32[1024,256]{1,0:T(8,128)} custom-call(bf16[1024,2048]{1,0:T(8,128)(2,1)} %get-tuple-element.398.p_ref), custom_call_target="tpu_custom_call" | custom-call | tf_op jit(solution)/shard_map/line_reduce/pallas_call | solution.py:271
  651.8 6.2 small_gather.9
  658.8 41.9 %line_reduce.5 = f32[1024,256]{1,0:T(8,128)} custom-call(bf16[1024,2048]{1,0:T(8,128)(2,1)} %get-tuple-element.127.p_ref), custom_call_target="tpu_custom_call" | custom-call | tf_op jit(solution)/shard_map/line_reduce/pallas_call | solution.py:271
  (303 shorter events, 156.4 us)
Async XLA Ops:
  7.2 57.6 %copy-start = (bf16[4,8,16,2048]{3,2,1,0:T(8,128)(2,1)S(1)}, bf16[4,8,16,2048]{3,2,1,0:T(8,128)(2,1)}, u32[]{:S(2)}) copy-start(bf16[4,8,16,2048]{3,2,1,0:T(8,128)(2,1)} %param.39) | copy-start | bytes 6291460
  7.2 279.1 %all-gather.4.cloned.1.call-start = ((), (), s32[]{:S(2)}) async-start(), calls=%async_computation | async-start | bytes 10485760 | tf_op jit(solution)/shard_map/all_gather | solution.py:498
  7.9 278.4 %all-gather.6.cloned.1.call-start = ((), (), s32[]{:S(2)}) async-start(), calls=%async_computation.1 | async-start | bytes 10485760 | tf_op jit(solution)/shard_map/all_gather | solution.py:499
  8.7 277.6 %all-gather.8.cloned.1.call-start = ((), (), s32[]{:S(2)}) async-start(), calls=%async_computation.2 | async-start | bytes 10485760 | tf_op jit(solution)/shard_map/all_gather | solution.py:500
  10.1 41.8 %copy-start.50 = (f32[2048]{0:T(1024)S(1)}, f32[2048]{0:T(1024)}, u32[]{:S(2)}) copy-start(f32[2048]{0:T(1024)} %param.26) | copy-start | bytes 24580
  61.0 6.8 copy-start.37
  61.0 6.8 copy-start.39
  61.0 6.8 copy-start.41
  64.8 29.0 %copy-start.35 = (bf16[1024,48]{0,1:T(8,128)(2,1)}, bf16[1024,48]{0,1:T(8,128)(2,1)S(1)}, u32[]{:S(2)}) copy-start(bf16[1024,48]{0,1:T(8,128)(2,1)S(1)} %convolution_convert_fusion.2) | copy-start | bytes 294916
  66.5 20.7 %copy-start.5 = (f32[1024,256]{1,0:T(8,128)}, f32[1024,256]{1,0:T(8,128)S(1)}, u32[]{:S(2)}) copy-start(f32[1024,256]{1,0:T(8,128)S(1)} %get-tuple-element.426) | copy-start | bytes 3145732
  78.7 11.3 %copy-start.54 = (f32[1024]{0:T(1024)}, f32[1024]{0:T(1024)S(1)}, u32[]{:S(2)}) copy-start(f32[1024]{0:T(1024)S(1)} %get-tuple-element.420) | copy-start | bytes 12292
  78.7 11.3 %copy-start.56 = (f32[1024]{0:T(1024)}, f32[1024]{0:T(1024)S(1)}, u32[]{:S(2)}) copy-start(f32[1024]{0:T(1024)S(1)} %get-tuple-element.421) | copy-start | bytes 12292
  86.1 7.7 %copy-start.60 = (f32[256]{0:T(256)}, f32[256]{0:T(256)S(1)}, u32[]{:S(2)}) copy-start(f32[256]{0:T(256)S(1)} %dynamic_slice.98) | copy-start | bytes 3076
  127.8 131.8 %copy-start.25 = (bf16[2,512,2,128]{3,2,1,0:T(2,128)(2,1)}, bf16[2,512,2,128]{3,2,1,0:T(2,128)(2,1)S(1)}, u32[]{:S(2)}) copy-start(bf16[2,512,2,128]{3,2,1,0:T(2,128)(2,1)S(1)} %get-tuple-element.126) | copy-start | bytes 1572868
  174.4 40.4 %copy-start.59 = (s32[1024,8]{0,1:T(8,128)S(1)}, s32[1024,8]{0,1:T(8,128)}, u32[]{:S(2)}) copy-start(s32[1024,8]{0,1:T(8,128)} %param.41) | copy-start | bytes 98308
  256.5 20.3 %copy-start.58 = (f32[2048]{0:T(1024)S(1)}, f32[2048]{0:T(1024)}, u32[]{:S(2)}) copy-start(f32[2048]{0:T(1024)} %param.27) | copy-start | bytes 24580
  508.0 12.8 %copy-start.57 = (f32[1024]{0:T(1024)S(1)}, f32[1024]{0:T(1024)}, u32[]{:S(2)}) copy-start(f32[1024]{0:T(1024)} %copy-done.56) | copy-start | bytes 12292
  508.6 15.1 %copy-start.36 = (bf16[1024,48]{0,1:T(8,128)(2,1)S(1)}, bf16[1024,48]{0,1:T(8,128)(2,1)}, u32[]{:S(2)}) copy-start(bf16[1024,48]{0,1:T(8,128)(2,1)} %copy-done.35) | copy-start | bytes 294916
  508.6 15.7 %copy-start.55 = (f32[1024]{0:T(1024)S(1)}, f32[1024]{0:T(1024)}, u32[]{:S(2)}) copy-start(f32[1024]{0:T(1024)} %copy-done.54) | copy-start | bytes 12292
  525.0 32.1 %copy-start.26 = (bf16[2,512,2,128]{3,2,1,0:T(2,128)(2,1)S(1)}, bf16[2,512,2,128]{3,2,1,0:T(2,128)(2,1)}, u32[]{:S(2)}) copy-start(bf16[2,512,2,128]{3,2,1,0:T(2,128)(2,1)} %copy-done.25) | copy-start | bytes 1572868
  560.6 16.9 %copy-start.38 = (bf16[2048,16]{0,1:T(8,128)(2,1)S(1)}, bf16[2048,16]{0,1:T(8,128)(2,1)}, u32[]{:S(2)}) copy-start(bf16[2048,16]{0,1:T(8,128)(2,1)} %copy-done.37) | copy-start | bytes 196612
  560.6 16.9 %copy-start.40 = (bf16[2048,16]{0,1:T(8,128)(2,1)S(1)}, bf16[2048,16]{0,1:T(8,128)(2,1)}, u32[]{:S(2)}) copy-start(bf16[2048,16]{0,1:T(8,128)(2,1)} %copy-done.39) | copy-start | bytes 196612
  560.7 16.9 %copy-start.42 = (bf16[2048,16]{0,1:T(8,128)(2,1)S(1)}, bf16[2048,16]{0,1:T(8,128)(2,1)}, u32[]{:S(2)}) copy-start(bf16[2048,16]{0,1:T(8,128)(2,1)} %copy-done.41) | copy-start | bytes 196612
  560.7 16.9 %copy-start.44 = (bf16[1024,16]{0,1:T(8,128)(2,1)S(1)}, bf16[1024,16]{0,1:T(8,128)(2,1)}, u32[]{:S(2)}) copy-start(bf16[1024,16]{0,1:T(8,128)(2,1)} %copy-done.43) | copy-start | bytes 98308
  560.7 16.9 %copy-start.46 = (bf16[1024,16]{0,1:T(8,128)(2,1)S(1)}, bf16[1024,16]{0,1:T(8,128)(2,1)}, u32[]{:S(2)}) copy-start(bf16[1024,16]{0,1:T(8,128)(2,1)} %copy-done.45) | copy-start | bytes 98308
  560.7 16.9 %copy-start.48 = (bf16[1024,16]{0,1:T(8,128)(2,1)S(1)}, bf16[1024,16]{0,1:T(8,128)(2,1)}, u32[]{:S(2)}) copy-start(bf16[1024,16]{0,1:T(8,128)(2,1)} %copy-done.47) | copy-start | bytes 98308
  586.7 8.4 %slice-start.1 = ((f32[2,298,128]{2,1,0:T(8,128)}), f32[2,128,128]{2,1,0:T(8,128)S(1)}, s32[]{:S(2)}) async-start(f32[2,298,128]{2,1,0:T(8,128)} %copy-done.28), calls=%async_computation.4 | async-start | bytes 262144 | tf_op jit(solution)/shard_map/slice | solution.py:722
  586.7 9.8 %copy-start.51 = (f32[2048]{0:T(1024)S(1)}, f32[2048]{0:T(1024)}, u32[]{:S(2)}) copy-start(f32[2048]{0:T(1024)} %param.26) | copy-start | bytes 24580
  609.9 90.8 %copy-start.53 = (f32[1024]{0:T(1024)S(1)}, f32[1024]{0:T(1024)}, u32[]{:S(2)}) copy-start(f32[1024]{0:T(1024)} %copy-done.52) | copy-start | bytes 12292
  609.9 90.8 %copy-start.65 = (f32[256]{0:T(256)S(1)}, f32[256]{0:T(256)}, u32[]{:S(2)}) copy-start(f32[256]{0:T(256)} %dynamic_slice.110) | copy-start | bytes 3076
  651.8 48.8 %copy-start.21 = (f32[1024,256]{1,0:T(8,128)S(1)}, f32[1024,256]{1,0:T(8,128)}, u32[]{:S(2)}) copy-start(f32[1024,256]{1,0:T(8,128)} %line_reduce.7) | copy-start | bytes 3145732
  658.8 41.9 %copy-start.27 = (bf16[1024,256]{1,0:T(8,128)(2,1)S(1)}, bf16[1024,256]{1,0:T(8,128)(2,1)}, u32[]{:S(2)}) copy-start(bf16[1024,256]{1,0:T(8,128)(2,1)} %x_ref.2) | copy-start | bytes 1572868
  (43 other events, 163.1 us)
Sparse Core Ops, SparseCore 0:
  9.8 88.4 all-gather.3
  100.1 87.3 all-gather.5
  189.3 87.4 all-gather.7

commit v2 on v1

v2 whole, which is shorter than its diff:
```python
import functools

import jax
import jax.numpy as jnp
from jax import lax
from jax.experimental import pallas as pl
from jax.experimental.pallas import tpu as pltpu
from jax.sharding import PartitionSpec as P

HD = 128
F32, BF16 = jnp.float32, jnp.bfloat16
MESH_ID = pl.DeviceIdType.MESH
VM = pl.BlockSpec(memory_space=pltpu.VMEM)
ANY = pl.BlockSpec(memory_space=pl.ANY)
VMEM_LIMIT = 60 * 1024 * 1024

norm_eps = 1e-05
rope_base = 10000.0
masked_score = -1e30


def nn(left, right):
    return jnp.dot(left, right, preferred_element_type=F32)


def nt(left, right):
    return lax.dot_general(left, right, (((1,), (1,)), ((), ())), preferred_element_type=F32)


def tn(left, right):
    return lax.dot_general(left, right, (((0,), (0,)), ((), ())), preferred_element_type=F32)


def remote(src, dst, send_sem, recv_sem, device):
    return pltpu.make_async_remote_copy(
        src_ref=src,
        dst_ref=dst,
        send_sem=send_sem,
        recv_sem=recv_sem,
        device_id={"col": device},
        device_id_type=MESH_ID,
    )


def line_place():
    here = lax.axis_index("col")
    core = here % 2
    return here, here // 2, core, here + 1 - 2 * core


def line_barrier(chips):
    here, chip, core, mate = line_place()
    barrier = pltpu.get_barrier_semaphore()
    has_left, has_right = chip > 0, chip < chips - 1
    pl.semaphore_signal(barrier, inc=1, device_id={"col": mate}, device_id_type=MESH_ID)

    @pl.when(has_left)
    def _():
        pl.semaphore_signal(barrier, inc=1, device_id={"col": here - 2}, device_id_type=MESH_ID)

    @pl.when(has_right)
    def _():
        pl.semaphore_signal(barrier, inc=1, device_id={"col": here + 2}, device_id_type=MESH_ID)

    inner = jnp.logical_and(has_left, has_right)

    @pl.when(inner)
    def _():
        pl.semaphore_wait(barrier, 3)

    @pl.when(jnp.logical_not(inner))
    def _():
        pl.semaphore_wait(barrier, 2)


def spot(axis, size, parts, block, part):
    rows, cols = size
    step = rows // parts
    if axis == 0:
        return (pl.ds(pl.multiple_of(block * rows + part * step, 8), step), slice(None))
    return (pl.ds(part * step, step), pl.ds(pl.multiple_of(block * cols, 128), cols))


def gather_body(chips, parts, axis, x_ref, o_ref, right_sem, left_sem, mate_sem, line_recv, mate_recv, own_sem):
    here, chip, core, mate = line_place()
    size = x_ref.shape
    step = size[0] // parts
    line_barrier(chips)

    def at(block, part):
        return o_ref.at[spot(axis, size, parts, block, part)]

    def copy(j, part, sem, recv, device, first=False, block=None):
        block = 2 * j + core if block is None else block
        src = x_ref.at[pl.ds(part * step, step)] if first else at(block, part)
        return remote(src, at(block, part), sem.at[j, part], recv.at[j, part], device)

    def forward(j, part, rightward, leftward, first):
        if rightward:

            @pl.when(chip < chips - 1)
            def _():
                copy(j, part, right_sem, line_recv, here + 2, first).start()

        if leftward:

            @pl.when(chip > 0)
            def _():
                copy(j, part, left_sem, line_recv, here - 2, first).start()

        copy(j, part, mate_sem, mate_recv, mate, first).start()

    for part in range(parts):
        forward(chip, part, True, True, True)
    own = []
    for part in range(parts):
        own.append(
            pltpu.make_async_copy(x_ref.at[pl.ds(part * step, step)], at(here, part), own_sem.at[part])
        )
        own[-1].start()
    for far in range(1, chips):
        for part in range(parts):

            @pl.when(chip - far >= 0)
            def _():
                copy(chip - far, part, right_sem, line_recv, mate).wait_recv()
                forward(chip - far, part, True, False, False)

            @pl.when(chip + far < chips)
            def _():
                copy(chip + far, part, left_sem, line_recv, mate).wait_recv()
                forward(chip + far, part, False, True, False)

    for own_copy in own:
        own_copy.wait()
    for j in range(chips):
        for part in range(parts):
            copy(j, part, mate_sem, mate_recv, mate, block=2 * j + 1 - core).wait_recv()
            copy(j, part, mate_sem, mate_recv, mate).wait_send()

            @pl.when(jnp.logical_and(j <= chip, chip < chips - 1))
            def _():
                copy(j, part, right_sem, line_recv, here + 2).wait_send()

            @pl.when(jnp.logical_and(j >= chip, chip > 0))
            def _():
                copy(j, part, left_sem, line_recv, here - 2).wait_send()


def line_gather(x, chips, axis, ident, parts=2):
    rows, cols = x.shape
    sems = pltpu.SemaphoreType.DMA((chips, parts))
    shape = (2 * chips * rows, cols) if axis == 0 else (rows, 2 * chips * cols)
    return pl.pallas_call(
        functools.partial(gather_body, chips, parts, axis),
        out_shape=jax.ShapeDtypeStruct(shape, x.dtype),
        in_specs=[VM],
        out_specs=VM,
        scratch_shapes=[sems] * 5 + [pltpu.SemaphoreType.DMA((parts,))],
        compiler_params=pltpu.CompilerParams(
            collective_id=ident, has_side_effects=True, vmem_limit_bytes=VMEM_LIMIT
        ),
        name="line_gather",
    )(x)


def reduce_body(
    chips, parts, axis, p_ref, o_ref, pair_buf, line_buf, sums, right_sem, left_sem, mate_sem, line_recv, mate_recv
):
    here, chip, core, mate = line_place()
    size = o_ref.shape
    step = size[0] // parts
    line_barrier(chips)

    def rows(part):
        return pl.ds(part * step, step)

    def at(block, part):
        return spot(axis, size, parts, block, part)

    def mate_copy(j, part):
        return remote(
            p_ref.at[at(2 * j + 1 - core, part)],
            pair_buf.at[j, rows(part)],
            mate_sem.at[j, part],
            mate_recv.at[j, part],
            mate,
        )

    def line_copy(j, slot, part, sem, device):
        return remote(
            sums.at[j, rows(part)], line_buf.at[slot, rows(part)], sem.at[j, part], line_recv.at[slot, part], device
        )

    for far in range(chips - 1, -1, -1):
        for part in range(parts):

            @pl.when(chip + far < chips)
            def _():
                mate_copy(chip + far, part).start()

            if far > 0:

                @pl.when(chip - far >= 0)
                def _():
                    mate_copy(chip - far, part).start()

    def pair_sum(j, part):
        mate_copy(j, part).wait_recv()
        return p_ref[at(2 * j + core, part)].astype(F32) + pair_buf[j, rows(part)].astype(F32)

    def pass_on(j, slot, part, more, sem, device):
        @pl.when(more)
        def _():
            line_copy(j, j, part, sem, mate).wait_recv()
            total = pair_sum(j, part) + line_buf[j, rows(part)].astype(F32)
            sums[j, rows(part)] = total.astype(BF16)

        @pl.when(jnp.logical_not(more))
        def _():
            sums[j, rows(part)] = pair_sum(j, part).astype(BF16)

        line_copy(j, slot, part, sem, device).start()

    for far in range(chips - 1, 0, -1):
        for part in range(parts):

            @pl.when(chip + far < chips)
            def _():
                pass_on(chip + far, chip + far, part, chip > 0, right_sem, here + 2)

            @pl.when(chip - far >= 0)
            def _():
                pass_on(
                    chip - far, chips if far == 1 else chip - far, part, chip < chips - 1, left_sem, here - 2
                )

    for part in range(parts):
        o_ref[rows(part)] = pair_sum(chip, part)

        @pl.when(chip > 0)
        def _():
            line_copy(chip, chip, part, right_sem, mate).wait_recv()
            o_ref[rows(part)] += line_buf[chip, rows(part)].astype(F32)

        @pl.when(chip < chips - 1)
        def _():
            line_copy(chip, chips, part, left_sem, mate).wait_recv()
            o_ref[rows(part)] += line_buf[chips, rows(part)].astype(F32)

    for j in range(chips):
        for part in range(parts):
            mate_copy(j, part).wait_send()

            @pl.when(j > chip)
            def _():
                line_copy(j, j, part, right_sem, mate).wait_send()

            @pl.when(j < chip)
            def _():
                line_copy(j, j, part, left_sem, mate).wait_send()


def line_reduce(p, chips, axis, ident, parts=2):
    rows, cols = p.shape
    if axis == 0:
        rows //= 2 * chips
    else:
        cols //= 2 * chips
    sems = pltpu.SemaphoreType.DMA((chips, parts))
    return pl.pallas_call(
        functools.partial(reduce_body, chips, parts, axis),
        out_shape=jax.ShapeDtypeStruct((rows, cols), F32),
        in_specs=[VM],
        out_specs=VM,
        scratch_shapes=[
            pltpu.VMEM((chips, rows, cols), BF16),
            pltpu.VMEM((chips + 1, rows, cols), BF16),
            pltpu.VMEM((chips, rows, cols), BF16),
            sems,
            sems,
            sems,
            pltpu.SemaphoreType.DMA((chips + 1, parts)),
            sems,
        ],
        compiler_params=pltpu.CompilerParams(
            collective_id=ident, has_side_effects=True, vmem_limit_bytes=VMEM_LIMIT
        ),
        name="line_reduce",
    )(p)


def small_body(count, x_ref, o_ref, send_sem, recv_sem):
    here = lax.axis_index("col")
    barrier = pltpu.get_barrier_semaphore()
    for hop in range(1, count):
        other = lax.rem(here + hop, count)
        pl.semaphore_signal(barrier, inc=1, device_id={"col": other}, device_id_type=MESH_ID)
    o_ref[here] = x_ref[...]
    pl.semaphore_wait(barrier, count - 1)

    def copy(hop, block):
        other = lax.rem(here + hop, count)
        return remote(x_ref, o_ref.at[block], send_sem.at[hop], recv_sem.at[hop], other)

    for hop in range(1, count):
        copy(hop, here).start()
    for hop in range(1, count):
        copy(hop, lax.rem(here + count - hop, count)).wait_recv()
    for hop in range(1, count):
        copy(hop, here).wait_send()


def small_gather(x, count, ident):
    sems = pltpu.SemaphoreType.DMA((count,))
    return pl.pallas_call(
        functools.partial(small_body, count),
        out_shape=jax.ShapeDtypeStruct((count,) + x.shape, x.dtype),
        in_specs=[VM],
        out_specs=VM,
        scratch_shapes=[sems, sems],
        compiler_params=pltpu.CompilerParams(collective_id=ident, has_side_effects=True),
        name="small_gather",
    )(x)


def turn_body(chips, parts, first, last, held, late_count, *refs):
    p_ref = refs[0]
    operands = refs[1 : 1 + held]
    o_ref = refs[1 + held]
    results = refs[2 + held : 2 + held + late_count]
    sums_in, pair_buf, line_buf, sums = refs[2 + held + late_count : 6 + held + late_count]
    reduce_sems = refs[6 + held + late_count : 11 + held + late_count]
    gather_sems = refs[11 + held + late_count : 16 + held + late_count]
    reduce_body(chips, parts, 0, p_ref, sums_in, pair_buf, line_buf, sums, *reduce_sems)
    here = lax.axis_index("col")
    own = o_ref.shape[0] // (2 * chips)
    kept = first(sums_in, operands, results, o_ref, pl.ds(pl.multiple_of(here * own, 8), own))
    gather_rows(chips, parts, o_ref, *gather_sems, lambda: last(kept, operands, results))


def gather_rows(chips, parts, o_ref, right_sem, left_sem, mate_sem, line_recv, mate_recv, beside):
    here, chip, core, mate = line_place()
    size = (o_ref.shape[0] // (2 * chips), o_ref.shape[1])

    def copy(j, part, sem, recv, device, block=None):
        block = 2 * j + core if block is None else block
        ref = o_ref.at[spot(0, size, parts, block, part)]
        return remote(ref, ref, sem.at[j, part], recv.at[j, part], device)

    def forward(j, part, rightward, leftward):
        if rightward:

            @pl.when(chip < chips - 1)
            def _():
                copy(j, part, right_sem, line_recv, here + 2).start()

        if leftward:

            @pl.when(chip > 0)
            def _():
                copy(j, part, left_sem, line_recv, here - 2).start()

        copy(j, part, mate_sem, mate_recv, mate).start()

    for part in range(parts):
        forward(chip, part, True, True)
    beside()
    for far in range(1, chips):
        for part in range(parts):

            @pl.when(chip - far >= 0)
            def _():
                copy(chip - far, part, right_sem, line_recv, mate).wait_recv()
                forward(chip - far, part, True, False)

            @pl.when(chip + far < chips)
            def _():
                copy(chip + far, part, left_sem, line_recv, mate).wait_recv()
                forward(chip + far, part, False, True)

    for j in range(chips):
        for part in range(parts):
            copy(j, part, mate_sem, mate_recv, mate, block=2 * j + 1 - core).wait_recv()
            copy(j, part, mate_sem, mate_recv, mate).wait_send()

            @pl.when(jnp.logical_and(j <= chip, chip < chips - 1))
            def _():
                copy(j, part, right_sem, line_recv, here + 2).wait_send()

            @pl.when(jnp.logical_and(j >= chip, chip > 0))
            def _():
                copy(j, part, left_sem, line_recv, here - 2).wait_send()


def line_turn(p, operands, width, results, first, last, chips, ident, parts=2):
    rows, cols = p.shape
    own = rows // (2 * chips)
    sems = pltpu.SemaphoreType.DMA((chips, parts))
    longer = pltpu.SemaphoreType.DMA((chips + 1, parts))
    return pl.pallas_call(
        functools.partial(turn_body, chips, parts, first, last, len(operands), len(results)),
        out_shape=(jax.ShapeDtypeStruct((rows, width), BF16),) + tuple(results),
        in_specs=[VM] * (1 + len(operands)),
        out_specs=(VM,) * (1 + len(results)),
        scratch_shapes=[
            pltpu.VMEM((own, cols), F32),
            pltpu.VMEM((chips, own, cols), BF16),
            pltpu.VMEM((chips + 1, own, cols), BF16),
            pltpu.VMEM((chips, own, cols), BF16),
            sems,
            sems,
            sems,
            longer,
            sems,
        ]
        + [sems] * 5,
        compiler_params=pltpu.CompilerParams(
            collective_id=ident, has_side_effects=True, vmem_limit_bytes=VMEM_LIMIT
        ),
        name="line_turn",
    )(p, *operands)


def inverse_rms(values):
    return lax.rsqrt(jnp.mean(values * values, axis=1, keepdims=True) + norm_eps)


def turn_forward(width, experts, sums, operands, results, o_ref, own):
    x_ref, gain_ref, a_ref, router_ref, up_ref = operands
    hidden_ref, mid_ref, mid_router_ref, probs_ref = results
    hidden = x_ref[...].astype(F32) + sums[:, :width]
    mid_ref[...] = sums[:, width:].astype(BF16)
    hidden_ref[...] = hidden
    normed = (hidden * inverse_rms(hidden) * gain_ref[...]).astype(BF16)
    o_ref[own, :width] = normed
    mid_router = nt(normed, a_ref[...]).astype(BF16)
    mid_router_ref[...] = mid_router
    logits = nt(normed, router_ref[...]) + nn(mid_router, up_ref[...])
    lane = lax.broadcasted_iota(jnp.int32, logits.shape, 1)
    logits = jnp.where(lane < experts, logits, masked_score)
    exponent = jnp.exp(logits - jnp.max(logits, axis=1, keepdims=True))
    probs = exponent / jnp.sum(exponent, axis=1, keepdims=True)
    probs_ref[...] = probs
    high = probs.astype(BF16)
    rest = probs - high.astype(F32)
    o_ref[own, width:] = (high.astype(F32) + pltpu.roll(rest, experts, 1)).astype(BF16)
    return None


def turn_backward(width, experts, sums, operands, results, o_ref, own):
    g_ref, hidden_ref, gain_ref, a_ref, router_ref, up_ref, probs_ref, mid_router_ref, mid_ref = operands
    pair = sums[:, width:]
    lanes = pair.shape[1]
    grad_probs = pair + pltpu.roll(pair, lanes - experts, 1)
    probs = probs_ref[...]
    grad_logits = (probs * (grad_probs - jnp.sum(probs * grad_probs, axis=1, keepdims=True))).astype(BF16)
    grad_mid = nt(grad_logits, up_ref[...]).astype(BF16)
    grad_normed = sums[:, :width] + nn(grad_logits, router_ref[...]) + nn(grad_mid, a_ref[...])
    hidden = hidden_ref[...]
    inv = inverse_rms(hidden)
    scaled = grad_normed * gain_ref[...]
    grad_hidden = (
        g_ref[...].astype(F32)
        + inv * scaled
        - hidden * (inv * inv * inv * jnp.mean(hidden * scaled, axis=1, keepdims=True))
    )
    grad_hidden = grad_hidden.astype(BF16)
    o_ref[own, :] = grad_hidden
    return grad_logits, grad_mid, grad_hidden


def turn_late(kept, operands, results):
    _, hidden_ref, gain_ref, _, _, _, _, mid_router_ref, mid_ref = operands
    grad_logits, grad_mid, grad_hidden = kept
    hidden = hidden_ref[...]
    normed = (hidden * inverse_rms(hidden) * gain_ref[...]).astype(BF16)
    rank = grad_mid.shape[1]
    late_ref, router_ref = results
    late_ref[pl.ds(0, rank)] = tn(grad_mid, normed)
    late_ref[pl.ds(rank, rank)] = tn(mid_ref[:, :rank], grad_hidden)
    router_ref[...] = tn(mid_router_ref[...], grad_logits)


def row_sums(values):
    high = values.astype(BF16)
    rest = (values - high.astype(F32)).astype(BF16)
    ones = jnp.ones((8, values.shape[1]), BF16)
    return nt(ones, high) + nt(ones, rest)


def project_body(tile, x_ref, gain_ref, wq, wk, wv, a_ref, b_ref, proj_ref, mid_ref, inv_ref, sq_ref):
    part = wq.shape[1]
    for t in range(x_ref.shape[0] // tile):
        rows = pl.ds(t * tile, tile)
        x = x_ref[rows].astype(F32)
        inv = inverse_rms(x)
        inv_ref[rows] = inv
        normed = (x * inv * gain_ref[...]).astype(BF16)
        mid = nt(normed, a_ref[...]).astype(BF16)
        mid_ref[rows] = mid
        for m, w in enumerate((wq, wk, wv)):
            cols = pl.ds(m * part, part)
            proj = nn(normed, w[...]) + nn(mid, b_ref[:, cols])
            proj_ref[rows, cols] = proj
            if m < 2:
                sq_ref[pl.ds(m, 1), rows] = row_sums(proj * proj)[0:1]


def project(x, gain, weights, a_rows, b_cols):
    seq_len, width = x.shape
    part = weights[0].shape[1]
    rank = a_rows.shape[0]
    return pl.pallas_call(
        functools.partial(project_body, min(256, seq_len)),
        out_shape=(
            jax.ShapeDtypeStruct((seq_len, 3 * part), F32),
            jax.ShapeDtypeStruct((seq_len, rank), BF16),
            jax.ShapeDtypeStruct((seq_len, 1), F32),
            jax.ShapeDtypeStruct((2, seq_len), F32),
        ),
        in_specs=[VM] * 7,
        out_specs=(VM,) * 4,
        compiler_params=pltpu.CompilerParams(vmem_limit_bytes=VMEM_LIMIT),
        name="project",
    )(x, gain, *weights, a_rows, b_cols)


def key_limit(start, tile, seq_len, reach):
    return min(seq_len, max(start + tile, reach))


def allowed_keys(start, tile, limit, prefix_len):
    query = start + lax.broadcasted_iota(jnp.int32, (tile, limit), 0)
    key = lax.broadcasted_iota(jnp.int32, (tile, limit), 1)
    return jnp.logical_or(key <= query, key < prefix_len)


def attend_body(
    tile, reach, scale, prefix_ref, proj_ref, inv_ref, gains_ref, cos_ref, sin_ref, map_ref,
    p_ref, att_ref, q_ref, k_ref, v_ref, log_ref,
):
    seq_len, part = att_ref.shape
    prefix_len = prefix_ref[0]
    for h in range(part // HD):
        cols = pl.ds(h * HD, HD)
        for m, ref in ((0, q_ref), (1, k_ref)):
            plain = proj_ref[:, pl.ds(m * part + h * HD, HD)] * inv_ref[:, m : m + 1] * gains_ref[m : m + 1, cols]
            ref[:, cols] = (plain * cos_ref[...] + pltpu.roll(plain, HD // 2, 1) * sin_ref[...]).astype(BF16)
        v_ref[:, cols] = proj_ref[:, pl.ds(2 * part + h * HD, HD)].astype(BF16)
    for start in range(0, seq_len, tile):
        rows = pl.ds(start, tile)
        limit = key_limit(start, tile, seq_len, reach)
        allowed = allowed_keys(start, tile, limit, prefix_len)
        for h in range(part // HD):
            cols = pl.ds(h * HD, HD)
            scores = nt(q_ref[rows, cols], k_ref[pl.ds(0, limit), cols]) * scale
            scores = jnp.where(allowed, scores, masked_score)
            top = jnp.max(scores, axis=1, keepdims=True)
            exponent = jnp.exp(scores - top)
            total = jnp.sum(exponent, axis=1, keepdims=True)
            weights = (exponent / total).astype(BF16)
            att_ref[rows, cols] = nn(weights, v_ref[pl.ds(0, limit), cols]).astype(BF16)
            log_ref[rows, h : h + 1] = top + jnp.log(total)
        p_ref[rows] = nn(att_ref[rows], map_ref[...]).astype(BF16)


def attend(prefix, proj, inv, gains, tables, out_map, reach, scale):
    seq_len = proj.shape[0]
    part = proj.shape[1] // 3
    heads = jax.ShapeDtypeStruct((seq_len, part), BF16)
    return pl.pallas_call(
        functools.partial(attend_body, min(256, seq_len), reach, scale),
        out_shape=(
            jax.ShapeDtypeStruct((seq_len, out_map.shape[1]), BF16),
            heads,
            heads,
            heads,
            heads,
            jax.ShapeDtypeStruct((seq_len, part // HD), F32),
        ),
        in_specs=[pl.BlockSpec(memory_space=pltpu.SMEM)] + [VM] * 6,
        out_specs=(VM,) * 6,
        compiler_params=pltpu.CompilerParams(vmem_limit_bytes=VMEM_LIMIT),
        name="attend",
    )(prefix, proj, inv, gains, *tables, out_map)


def attend_back_body(
    tile, reach, scale, prefix_ref, g_ref, map_ref, b_ref, att_ref, q_ref, k_ref, v_ref, log_ref, proj_ref,
    gains_ref, cos_ref, sin_ref, scaled_ref, dv_ref, stat_ref, ga_ref, da_ref, dq_acc, dk_acc, dv_acc,
):
    seq_len, part = att_ref.shape
    prefix_len = prefix_ref[0]
    grad_a = jnp.zeros(ga_ref.shape, F32)
    for start in range(0, seq_len, tile):
        rows = pl.ds(start, tile)
        grads = g_ref[rows]
        da_ref[rows] = nt(grads, map_ref[...]).astype(BF16)
        grad_mid = nt(grads, b_ref[...]).astype(BF16)
        grad_a += tn(grad_mid, att_ref[rows])
    ga_ref[...] = grad_a
    dk_acc[...] = jnp.zeros_like(dk_acc)
    dv_acc[...] = jnp.zeros_like(dv_acc)
    for start in range(0, seq_len, tile):
        rows = pl.ds(start, tile)
        limit = key_limit(start, tile, seq_len, reach)
        keys = pl.ds(0, limit)
        allowed = allowed_keys(start, tile, limit, prefix_len)
        for h in range(part // HD):
            cols = pl.ds(h * HD, HD)
            query, key = q_ref[rows, cols], k_ref[keys, cols]
            grads = da_ref[rows, cols]
            scores = jnp.where(allowed, nt(query, key) * scale, masked_score)
            weights = jnp.exp(scores - log_ref[rows, h : h + 1])
            grad_weights = nt(grads, v_ref[keys, cols])
            dot = jnp.sum(weights * grad_weights, axis=1, keepdims=True)
            grad_scores = (weights * (grad_weights - dot)).astype(BF16)
            dq_acc[rows, cols] = nn(grad_scores, key) * scale
            dk_acc[keys, cols] += tn(grad_scores, query) * scale
            dv_acc[keys, cols] += tn(weights.astype(BF16), grads)
    dv_ref[...] = dv_acc[...].astype(BF16)
    for m, acc in ((0, dq_acc), (1, dk_acc)):
        for start in range(0, seq_len, tile):
            rows = pl.ds(start, tile)
            total = jnp.zeros((8, tile), F32)
            for h in range(part // HD):
                cols = pl.ds(h * HD, HD)
                here = pl.ds(m * part + h * HD, HD)
                plain = acc[rows, cols]
                turned = plain * cos_ref[rows] - pltpu.roll(plain, HD // 2, 1) * sin_ref[rows]
                scaled = turned * gains_ref[m : m + 1, cols]
                scaled_ref[rows, here] = scaled
                total += row_sums(proj_ref[rows, here] * scaled)
            stat_ref[pl.ds(m, 1), rows] = total[0:1]


def attend_back(prefix, grads, out_map, b_out, saved, proj, gains, tables, reach, scale):
    seq_len = proj.shape[0]
    part = proj.shape[1] // 3
    return pl.pallas_call(
        functools.partial(attend_back_body, min(256, seq_len), reach, scale),
        out_shape=(
            jax.ShapeDtypeStruct((seq_len, 2 * part), F32),
            jax.ShapeDtypeStruct((seq_len, part), BF16),
            jax.ShapeDtypeStruct((2, seq_len), F32),
            jax.ShapeDtypeStruct((b_out.shape[0], part), F32),
        ),
        in_specs=[pl.BlockSpec(memory_space=pltpu.SMEM)] + [VM] * 12,
        out_specs=(VM,) * 4,
        scratch_shapes=[pltpu.VMEM((seq_len, part), BF16)] + [pltpu.VMEM((seq_len, part), F32)] * 3,
        compiler_params=pltpu.CompilerParams(vmem_limit_bytes=VMEM_LIMIT),
        name="attend_back",
    )(prefix, grads, out_map, b_out, *saved, proj, gains, *tables)


def inputs_back_body(
    tile, extra, scaled_ref, dv_ref, proj_ref, inv_ref, stat_ref, wq, wk, wv, b_ref, a_ref, x_ref, inv1_ref,
    gain_ref, mid_ref, late_ref, router_ref, p_ref, gb_ref,
):
    seq_len, width = x_ref.shape
    part = dv_ref.shape[1]
    ranks = a_ref.shape[0]
    rank = ranks // 3
    grad_b = [jnp.zeros((rank, part), F32) for _ in range(3)]
    grad_a = jnp.zeros((ranks, width), F32)
    stats = jnp.zeros((8, width), F32)
    line = lax.broadcasted_iota(jnp.int32, (8, width), 0)
    for t in range(seq_len // tile):
        rows = pl.ds(t * tile, tile)
        normed_part = jnp.zeros((tile, width), F32)
        middles = []
        for m, w in enumerate((wq, wk, wv)):
            if m < 2:
                cols = pl.ds(m * part, part)
                inv = inv_ref[rows, m : m + 1]
                shift = inv * inv * inv * stat_ref[rows, m : m + 1]
                grad = (inv * scaled_ref[rows, cols] - proj_ref[rows, cols] * shift).astype(BF16)
            else:
                grad = dv_ref[rows]
            middles.append(nt(grad, b_ref[pl.ds(m * rank, rank)]).astype(BF16))
            normed_part += nt(grad, w[...]) + nn(middles[m], a_ref[pl.ds(m * rank, rank)])
            grad_b[m] += tn(mid_ref[rows, m * rank : (m + 1) * rank], grad)
        p_ref[rows] = normed_part.astype(BF16)
        scaled_x = x_ref[rows].astype(F32) * gain_ref[...]
        normed = (scaled_x * inv1_ref[rows]).astype(BF16)
        grad_a += jnp.concatenate([tn(middle, normed) for middle in middles], axis=0)
        first = row_sums(scaled_x * normed_part)
        for j in range(tile // part):
            wide = jnp.concatenate([first[:, j * part : (j + 1) * part]] * (width // part), axis=1)
            stats = jnp.where(line == (t * tile) // part + j, wide, stats)
    for m in range(3):
        gb_ref[pl.ds(m * rank, rank)] = grad_b[m]
    high = stats.astype(BF16).astype(F32)
    router = router_ref[...]
    if part > router.shape[1]:
        router = jnp.concatenate([router, jnp.zeros((rank, part - router.shape[1]), F32)], axis=1)
    pieces = [
        grad_a,
        late_ref[...],
        jnp.concatenate([router] * (width // part), axis=1),
        high,
        stats - high,
    ]
    used = sum(piece.shape[0] for piece in pieces)
    pieces.append(jnp.zeros((extra - used, width), F32))
    start = seq_len
    p_ref[pl.ds(start, extra)] = jnp.concatenate(pieces, axis=0).astype(BF16)


def inputs_back(extra, *operands):
    x = operands[10]
    seq_len, width = x.shape
    part = operands[1].shape[1]
    ranks = operands[9].shape[0]
    return pl.pallas_call(
        functools.partial(inputs_back_body, min(256, seq_len), extra),
        out_shape=(
            jax.ShapeDtypeStruct((seq_len + extra, width), BF16),
            jax.ShapeDtypeStruct((ranks, part), F32),
        ),
        in_specs=[VM] * len(operands),
        out_specs=(VM,) * 2,
        compiler_params=pltpu.CompilerParams(vmem_limit_bytes=VMEM_LIMIT),
        name="inputs_back",
    )(*operands)


def moe_body(experts, chosen, tile, done, x_ref, g_ref, routes_ref, *refs):
    count = len(chosen)
    weights = refs[: 3 * count]
    refs = refs[3 * count :]
    if done:
        earlier, hidden_ref, refs = refs[:3], refs[3], refs[4:]
    out_ref, dx_ref = refs[:2]
    gate_ref = None if done else refs[2]
    out_acc, dx_acc, gate_acc, wgu, wd, sems = refs[2 if done else 3 :]
    hidden = wd.shape[1]
    tokens, width = g_ref.shape
    lanes = gate_acc.shape[1]
    pieces = weights[0].shape[2] // hidden
    here = lax.axis_index("col")
    local = experts // lax.axis_size("col")

    def copies(a, piece, slot):
        gate, up, down = weights[3 * a : 3 * a + 3]
        which, at_gate, at_down = chosen[a]
        units = pl.ds(pl.multiple_of(piece * hidden, 128), hidden)
        return (
            pltpu.make_async_copy(gate.at[at_gate, :, units], wgu.at[slot, :, pl.ds(0, hidden)], sems.at[slot, 0]),
            pltpu.make_async_copy(up.at[at_gate, :, units], wgu.at[slot, :, pl.ds(hidden, hidden)], sems.at[slot, 1]),
            pltpu.make_async_copy(down.at[at_down, units], wd.at[slot], sems.at[slot, 2]),
        )

    for copy in copies(0, 0, 0):
        copy.start()
    if done:
        out_acc[...] = earlier[0][...].astype(F32)
        dx_acc[...] = earlier[1][...].astype(F32)
        gate_acc[...] = earlier[2][...]
        own = hidden_ref.shape[0]
        out_acc[pl.ds(pl.multiple_of(here * own, 8), own)] += hidden_ref[...]
    else:
        out_acc[...] = jnp.zeros_like(out_acc)
        dx_acc[...] = jnp.zeros_like(dx_acc)
        gate_acc[...] = jnp.zeros_like(gate_acc)

    for a in range(count):
        e = here * local + chosen[a][0]

        def one_step(piece, carry):
            slot = piece % 2
            for copy in copies(a, 0, slot):
                copy.wait()

            @pl.when(piece + 1 < pieces)
            def _():
                for copy in copies(a, piece + 1, 1 - slot):
                    copy.start()

            if a + 1 < count:

                @pl.when(piece + 1 == pieces)
                def _():
                    for copy in copies(a + 1, 0, 1 - slot):
                        copy.start()

            def one_tile(t, carry):
                rows = pl.ds(pl.multiple_of(t * tile, tile), tile)
                lane = lax.broadcasted_iota(jnp.int32, (tile, lanes), 1)
                mine = lane == e
                halves = jnp.logical_or(mine, lane == e + experts)
                named = jnp.sum(jnp.where(routes_ref[rows] == e, 1.0, 0.0), axis=1, keepdims=True)
                gate = jnp.sum(jnp.where(halves, x_ref[rows, width:].astype(F32), 0.0), axis=1, keepdims=True)
                gate = gate * named
                both = nn(x_ref[rows, :width], wgu[slot])
                gate_in, up_in = both[:, :hidden], both[:, hidden:]
                sigmoid = jax.nn.sigmoid(gate_in)
                silu = gate_in * sigmoid
                active = silu * up_in
                back = nt(g_ref[rows], wd[slot])
                d_gate = jnp.sum(active * back, axis=1, keepdims=True) * named
                gate_acc[rows] += jnp.where(mine, d_gate, 0.0)
                out_acc[rows] += nn((active * gate).astype(BF16), wd[slot])
                d_active = back * gate
                d_gate_in = d_active * up_in * (sigmoid + silu * (1.0 - sigmoid))
                d_up_in = d_active * silu
                d_both = jnp.concatenate([d_gate_in.astype(BF16), d_up_in.astype(BF16)], axis=1)
                dx_acc[rows] += nt(d_both, wgu[slot])
                return carry

            return lax.fori_loop(0, tokens // tile, one_tile, carry)

        lax.fori_loop(0, pieces, one_step, 0)
    out_ref[...] = out_acc[...].astype(BF16)
    if done:
        dx_ref[:, :width] = dx_acc[...].astype(BF16)
        high = gate_acc[...].astype(BF16).astype(F32)
        rest = gate_acc[...] - high
        dx_ref[:, width:] = (high + pltpu.roll(rest, experts, 1)).astype(BF16)
    else:
        dx_ref[...] = dx_acc[...].astype(BF16)
        gate_ref[...] = gate_acc[...]


def moe(x, g, routes, experts, chosen, weights, earlier=None, hidden_rows=None, tile=512):
    tokens, width = g.shape
    units = weights[0].shape[2]
    hidden = min(256, units)
    lanes = x.shape[1] - width
    done = earlier is not None
    outs = [jax.ShapeDtypeStruct((tokens, width), BF16)]
    outs.append(jax.ShapeDtypeStruct((tokens, width + (lanes if done else 0)), BF16))
    if not done:
        outs.append(jax.ShapeDtypeStruct((tokens, lanes), F32))
    more = (tuple(earlier) + (hidden_rows,)) if done else ()
    return pl.pallas_call(
        functools.partial(moe_body, experts, chosen, min(tile, tokens), done),
        out_shape=tuple(outs),
        in_specs=[VM] * 3 + [ANY] * len(weights) + [VM] * len(more),
        out_specs=(VM,) * len(outs),
        scratch_shapes=[
            pltpu.VMEM((tokens, width), F32),
            pltpu.VMEM((tokens, width), F32),
            pltpu.VMEM((tokens, lanes), F32),
            pltpu.VMEM((2, width, 2 * hidden), BF16),
            pltpu.VMEM((2, hidden, width), BF16),
            pltpu.SemaphoreType.DMA((2, 3)),
        ],
        compiler_params=pltpu.CompilerParams(vmem_limit_bytes=VMEM_LIMIT),
        name="moe",
    )(x, g, routes, *weights, *more)


def rope_tables(length, head_dim):
    half_dim = head_dim // 2
    frequency = rope_base ** (-(2.0 * jnp.arange(half_dim, dtype=F32)) / head_dim)
    angles = jnp.arange(length, dtype=F32)[:, None] * frequency[None, :]
    cosine, sine = jnp.cos(angles), jnp.sin(angles)
    return jnp.concatenate([cosine, cosine], axis=1), jnp.concatenate([-sine, sine], axis=1)


def shards(
    inputs,
    cotangent,
    norm_first,
    norm_second,
    query_gain,
    key_gain,
    w_query,
    w_key,
    w_value,
    w_out,
    w_router,
    w_gate,
    w_up,
    w_down,
    adapter_a,
    adapter_b,
    adapter_router,
    routes,
    prefix,
    adapter_index,
):
    seq_len, width_part = inputs.shape
    col_count = lax.axis_size("col")
    row_count = lax.axis_size("row")
    col_index = lax.axis_index("col")
    row_index = lax.axis_index("row")
    chips = col_count // 2
    full_width = width_part * col_count
    head_width = w_query.shape[1]
    local_experts = w_gate.shape[0]
    expert_total = w_router.shape[1]
    feature_start = col_index * width_part
    head_start = col_index * head_width
    own_rows = seq_len // col_count
    row_start = col_index * own_rows
    score_scale = HD ** (-0.5)
    reach = seq_len // 2
    lanes = 128

    def columns(array, axis_num):
        return lax.dynamic_slice_in_dim(array, feature_start, width_part, axis_num)

    def head_cols(array, axis_num=1):
        return lax.dynamic_slice_in_dim(array, head_start, head_width, axis_num)

    def held_rows(array):
        return lax.dynamic_slice_in_dim(array, row_start, own_rows, 0)

    def col_sum(pair, ident):
        return jnp.sum(small_gather(pair, col_count, ident), axis=0)

    full_gate = lax.all_gather(w_gate, "row", axis=2, tiled=True)
    full_up = lax.all_gather(w_up, "row", axis=2, tiled=True)
    full_down = [
        lax.all_gather(w_down[e : e + 1], "row", axis=1, tiled=True) for e in range(local_experts)
    ]
    adapter_slot = adapter_index[0]
    chosen_a = lax.dynamic_index_in_dim(adapter_a, adapter_slot, 1, keepdims=False).swapaxes(1, 2)
    chosen_b = lax.dynamic_index_in_dim(adapter_b, adapter_slot, 1, keepdims=False)
    chosen_router = lax.dynamic_index_in_dim(adapter_router, adapter_slot, 0, keepdims=False)
    rank = chosen_a.shape[1]
    a_three = chosen_a[:3].reshape(3 * rank, full_width)
    b_three = head_cols(chosen_b[:3].reshape(3 * rank, full_width))
    blank = jnp.zeros((rank, head_width), BF16)
    b_cols = jnp.concatenate(
        [
            jnp.concatenate([b_three[m * rank : (m + 1) * rank] if n == m else blank for n in range(3)], axis=0)
            for m in range(3)
        ],
        axis=1,
    )
    a_out = head_cols(chosen_a[3])
    out_map = (w_out.astype(F32) + tn(a_out, chosen_b[3])).astype(BF16)
    out_wide = jnp.concatenate([out_map, a_out.T, jnp.zeros((head_width, lanes - rank), BF16)], axis=1)
    router_rows = jnp.pad(w_router.T, ((0, lanes - expert_total), (0, 0)))
    router_up = jnp.pad(chosen_router, ((0, 0), (0, lanes - expert_total)))
    gains = jnp.stack([head_cols(query_gain, 0), head_cols(key_gain, 0)])
    tables = rope_tables(seq_len, HD)
    gain_first, gain_second = norm_first[None], norm_second[None]

    full_inputs = line_gather(inputs, chips, 1, 0)
    proj, mid, inv_first, squares = project(
        full_inputs, gain_first, (w_query, w_key, w_value), a_three, b_cols
    )
    inv = lax.rsqrt(col_sum(squares, 1) / full_width + norm_eps).T
    part_out, attended, rot_query, rot_key, value_rows, log_totals = attend(
        prefix, proj, inv, gains, tables, out_wide, reach, score_scale
    )
    wide = full_width + lanes
    row_shape = jax.ShapeDtypeStruct
    normed_two, hidden_rows, mid_out, mid_router, probs = line_turn(
        part_out,
        (held_rows(full_inputs), gain_second, chosen_a[4], router_rows, router_up),
        wide,
        (
            row_shape((own_rows, full_width), F32),
            row_shape((own_rows, lanes), BF16),
            row_shape((own_rows, rank), BF16),
            row_shape((own_rows, lanes), F32),
        ),
        functools.partial(turn_forward, full_width, expert_total),
        lambda kept, operands, results: None,
        chips,
        2,
    )
    full_cot = line_gather(cotangent, chips, 1, 4)

    early = tuple((e, e, 0) for e in range(local_experts - 1)) if local_experts > 1 else ()
    final = ((local_experts - 1, local_experts - 1, 0),)
    first = moe(
        normed_two,
        full_cot,
        routes,
        expert_total,
        early,
        sum([(full_gate, full_up, full_down[e]) for e, _, _ in early], ()),
    )
    moe_out, back_out = moe(
        normed_two,
        full_cot,
        routes,
        expert_total,
        final,
        (full_gate, full_up, full_down[-1]),
        first,
        hidden_rows,
    )
    grad_attn, late, router_late = line_turn(
        back_out,
        (
            held_rows(full_cot),
            hidden_rows,
            gain_second,
            chosen_a[4],
            router_rows,
            router_up,
            probs,
            mid_router,
            mid_out,
        ),
        full_width,
        (row_shape((2 * rank, full_width), F32), row_shape((rank, lanes), F32)),
        functools.partial(turn_backward, full_width, expert_total),
        turn_late,
        chips,
        7,
    )
    moe_out, grad_attn = lax.optimization_barrier((moe_out, grad_attn))
    layer_out = lax.psum_scatter(moe_out, "col", scatter_dimension=1, tiled=True)

    scaled, grad_value, norm_stats, grad_a_out = attend_back(
        prefix,
        grad_attn,
        out_map,
        chosen_b[3],
        (attended, rot_query, rot_key, value_rows, log_totals),
        proj,
        gains,
        tables,
        reach,
        score_scale,
    )
    stats = (col_sum(norm_stats, 10) / full_width).T
    extra = 128
    normed_part, grad_b_three = inputs_back(
        extra,
        scaled,
        grad_value,
        proj,
        inv,
        stats,
        w_query,
        w_key,
        w_value,
        b_three,
        a_three,
        full_inputs,
        inv_first,
        gain_first,
        mid,
        late,
        router_late,
    )
    summed_part = line_reduce(normed_part, chips, 1, 12)
    stat_rows = seq_len // width_part
    tail = summed_part[seq_len:]
    stat_start = 6 * rank
    first_stat = (
        tail[stat_start : stat_start + stat_rows] + tail[stat_start + 8 : stat_start + 8 + stat_rows]
    ).reshape(seq_len, 1)
    grad_inputs = (
        columns(grad_attn, 1).astype(F32)
        + inv_first * columns(norm_first, 0) * summed_part[:seq_len]
        - inputs.astype(F32) * (inv_first * inv_first * inv_first * first_stat / full_width)
    )

    held_adapters = adapter_a.shape[1] // row_count
    flat = jnp.concatenate(
        [
            tail[: 6 * rank],
            grad_a_out,
            grad_b_three,
            jnp.broadcast_to(adapter_slot.astype(F32), (8, width_part)),
        ]
    ).astype(BF16)
    every = lax.all_gather(flat, "row", axis=0).astype(F32)
    owners = every[:, -1, 0]
    held_ids = (row_index * held_adapters + jnp.arange(held_adapters)).astype(F32)
    pick = (owners[None, :] == held_ids[:, None])[:, :, None, None]
    summed = jnp.sum(jnp.where(pick, every[None], 0.0), axis=1)
    pieces = [summed[:, n * rank : (n + 1) * rank] for n in range(10)]
    query_a, key_a, value_a, router_a, out_b, router_up_grad, out_a, query_b, key_b, value_b = pieces
    grad_a = jnp.stack([query_a, key_a, value_a, out_a, router_a]).swapaxes(2, 3)
    grad_b = jnp.stack([query_b, key_b, value_b, out_b])
    grad_router = router_up_grad[:, :, :expert_total]
    return (layer_out, grad_inputs, grad_a, grad_b, grad_router)


def solution(mesh):
    placed = (
        P("row", "col"),
        P("row", "col"),
        P(),
        P(),
        P(),
        P(),
        P(None, "col"),
        P(None, "col"),
        P(None, "col"),
        P("col", None),
        P(),
        P("col", None, "row"),
        P("col", None, "row"),
        P("col", "row", None),
        P(),
        P(),
        P(),
        P("row", None),
        P("row"),
        P("row"),
    )
    return jax.shard_map(
        shards,
        mesh=mesh,
        in_specs=placed,
        out_specs=(
            P("row", "col"),
            P("row", "col"),
            P(None, "row", "col", None),
            P(None, "row", None, "col"),
            P("row", None, None),
        ),
        check_vma=False,
    )
```

time: 721 us -> 549 us (0.76)
  matrix products: 113 us -> 0.45 us
  other arithmetic: 67.9 us -> 12.6 us
  waiting for transfers between devices: 2.06 us -> 26.9 us
  local copies, waits for them, and re-layouts: 38.7 us -> 23.3 us
  loops' own time: 8.48 us -> 0 us
    pallas_call x1 -> x8, Pallas kernels: 66.3 us -> 309 us  [the longest x2 166 us: line_turn(): pl.pallas_call(functools.partial(turn_body, chips, parts, first, last, le...]
    pallas_call x4 -> x1, Pallas kernels: 167 us -> 46.5 us  [line_reduce(): pl.pallas_call(functools.partial(reduce_body, chips, parts, axis), out_sh...]
    dot_general x36 -> x0, matrix products: 102 us -> none  [the longest x9 35.2 us: nt(): lax.dot_general(left, right, (((1,), (1,)), ((), ())), preferred_element_...]
    pallas_call x4 -> x2, Pallas kernels: 156 us -> 77.9 us  [line_gather(): pl.pallas_call(functools.partial(gather_body, chips, parts, axis), out_sh...]
    pallas_call x6 -> x2, Pallas kernels: 66 us -> 19.3 us  [small_gather(): pl.pallas_call(functools.partial(small_body, count), out_shape=jax.ShapeD...]
    all_gather x3 -> x4, waiting for transfers between devices: 0.01 us -> 25 us  [the longest x2 16.3 us: shards(): lax.all_gather(w_down[e:e + 1], 'row', axis=1, tiled=True)]
    convert_element_type x11 -> x0, other arithmetic: 23.1 us -> none  [the longest x2 4.71 us: back_block(): grad_scores = (weights * (grad_weights - row_dot)).astype(BF16)]
    reduce_sum x14 -> x3, other arithmetic: 17.1 us -> 1.91 us  [the longest x2 1.75 us: col_sum(): return jnp.sum(small_gather(pair, col_count, ident), axis=0)]
  transfers between devices with their start and end apart: 3 -> 5, of which waited for: 0 -> 2; matrix products, arithmetic and copies ran while one was open for 13% -> 6% of each run, Pallas kernels for 26% -> 61%
where the time goes in v2:
time: 549 us; the launch traced here: 542 us
  Pallas kernels  453 us (83%)
  waiting for transfers between devices  26.9 us (5%)
  local copies, waits for them, and re-layouts  23.3 us (4%)
  between operations  15.8 us (3%)
  other arithmetic  12.6 us (2%)
  blocking collectives  9.53 us (2%)
    pallas_call x2, Pallas kernels, line_turn(): pl.pallas_call(functools.partial(turn_body, chips, parts, first, last, le...  166 us
    pallas_call x2, Pallas kernels, moe(): pl.pallas_call(functools.partial(moe_body, experts, chosen, min(tile, tok...  78.9 us
    pallas_call x2, Pallas kernels, line_gather(): pl.pallas_call(functools.partial(gather_body, chips, parts, axis), out_sh...  77.9 us
    pallas_call x1, Pallas kernels, line_reduce(): pl.pallas_call(functools.partial(reduce_body, chips, parts, axis), out_sh...  46.5 us
    pallas_call x1, Pallas kernels, inputs_back(): pl.pallas_call(functools.partial(inputs_back_body, min(256, seq_len), ext...  22 us
    pallas_call x2, Pallas kernels, small_gather(): pl.pallas_call(functools.partial(small_body, count), out_shape=jax.ShapeD...  19.3 us
    all_gather x2, waiting for transfers between devices, shards(): lax.all_gather(w_down[e:e + 1], 'row', axis=1, tiled=True)  16.3 us
    pallas_call x1, Pallas kernels, attend_back(): pl.pallas_call(functools.partial(attend_back_body, min(256, seq_len), rea...  15.3 us
  transfers between devices with their start and end apart: 5, of which 2 were waited for; matrix products, arithmetic and copies ran while one was open for 6% of the time, Pallas kernels for 61%

profile of v2, /device:TPU:16, one launch (start us, length us, event | category | flops | bytes accessed | tf_op | source)
XLA Modules:
  0.0 541.5 jit_solution(14029170039392607116)
XLA Ops:
  7.2 3.2 fusion.17
  14.0 38.8 %line_gather.2.x_ref = bf16[1024,2048]{1,0:T(8,128)(2,1)} custom-call(bf16[1024,256]{1,0:T(8,128)(2,1)} %x_ref.2), custom_call_target="tpu_custom_call" | custom-call | tf_op jit(solution)/shard_map/line_gather/pallas_call | solution.py:154
  52.8 1.0 constant_dynamic-slice_fusion
  55.0 14.6 %project.1 = (f32[1024,768]{1,0:T(8,128)}, bf16[1024,48]{1,0:T(8,128)(2,1)}, f32[1024,1]{1,0:T(8,128)}, f32[2,1024]{1,0:T(2,128)}) custom-call(bf16[1024,2048]{1,0:T(8,128)(2,1)} %line_gather.2.x_ref, f32[1,2048]{1,0:T(1,128)} %bitcast.81, bf16[2048,256]{1,0:T(8,128)(2,1)} %wq.3, bf16[2048,256]{1,0:T(8,128)(2,1)} %wk.3, bf16[2048,256]{1,0:T(8,128)(2,1)} %wv.3, ...), custom_call_target="tpu_custom_call" | custom-call | tf_op jit(solution)/shard_map/project/pallas_call | solution.py:514
  69.7 9.3 %small_gather.2 = f32[8,2,1024]{2,1,0:T(2,128)} custom-call(f32[2,1024]{1,0:T(2,128)} %get-tuple-element.37.x_ref), custom_call_target="tpu_custom_call" | custom-call | tf_op jit(solution)/shard_map/small_gather/pallas_call | solution.py:316
  78.9 0.9 reduce_sum.27
  79.8 1.0 copy.51
  86.0 39.1 %line_gather.3.g_ref = bf16[1024,2048]{1,0:T(8,128)(2,1)} custom-call(bf16[1024,256]{1,0:T(8,128)(2,1)} %x_ref.3), custom_call_target="tpu_custom_call" | custom-call | tf_op jit(solution)/shard_map/line_gather/pallas_call | solution.py:154
  125.1 1.0 copy.54.routes_ref
  127.4 1.9 concatenate.44.map_ref
  130.0 2.0 fusion.6
  131.9 1.3 pad_maximum_fusion
  133.3 11.7 %attend.1 = (bf16[1024,2176]{1,0:T(8,128)(2,1)}, bf16[1024,256]{1,0:T(8,128)(2,1)}, bf16[1024,256]{1,0:T(8,128)(2,1)}, bf16[1024,256]{1,0:T(8,128)(2,1)}, bf16[1024,256]{1,0:T(8,128)(2,1)}, /*index=5*/f32[1024,2]{1,0:T(8,128)}) custom-call(s32[1]{0:T(128)S(6)} %copy.63.prefix_ref, f32[1024,768]{1,0:T(8,128)} %get-tuple-element.36.proj_ref, ...), custom_call_target="tpu_custom_call" | custom-call | tf_op jit(solution)/shard_map/attend/pallas_call | solution.py:572
  145.0 1.9 constant_dynamic-slice_fusion.2.refs_1_
  146.8 85.4 %line_turn.2 = (bf16[1024,2176]{1,0:T(8,128)(2,1)}, f32[128,2048]{1,0:T(8,128)}, bf16[128,128]{1,0:T(8,128)(2,1)}, bf16[128,16]{1,0:T(8,128)(2,1)}, f32[128,128]{1,0:T(8,128)}) custom-call(bf16[1024,2176]{1,0:T(8,128)(2,1)} %get-tuple-element.38.refs_0_, bf16[128,2048]{1,0:T(8,128)(2,1)} %constant_dynamic-slice_fusion.2.refs_1_, f32[1,2048]{1,0:T(1,128)} %bitcast.83, ...), custom_call_target="tpu_custom_call" | custom-call | tf_op jit(solution)/shard_map/line_turn/pallas_call | solution.py:401
  232.2 1.9 constant_dynamic-slice_fusion.1.refs_1_
  234.1 8.6 %all-gather.7.cloned.1.call-done.refs_1_ = bf16[2,2048,1024]{2,1,0:T(8,128)(2,1)} async-done(((bf16[2,2048,256]{2,1,0:T(8,128)(2,1)}), bf16[2,2048,1024]{2,1,0:T(8,128)(2,1)}) %all-gather.7.cloned.1.call-update) | async-done | bytes 8388624 | tf_op jit(solution)/shard_map/all_gather | solution.py:916
  242.8 38.0 %moe.2 = (bf16[1024,2048]{1,0:T(8,128)(2,1)}, bf16[1024,2048]{1,0:T(8,128)(2,1)}, f32[1024,128]{1,0:T(8,128)}) custom-call(bf16[1024,2176]{1,0:T(8,128)(2,1)} %get-tuple-element.39.x_ref, bf16[1024,2048]{1,0:T(8,128)(2,1)} %line_gather.3.g_ref, s32[1024,8]{1,0:T(8,128)} %copy.54.routes_ref, bf16[2,2048,1024]{2,1,0:T(8,128)(2,1)} %all-gather.5.cloned.1.call-done.refs_0_, ...), custom_call_target="tpu_custom_call" | custom-call | tf_op jit(solution)/shard_map/moe/pallas_call | solution.py:837
  280.7 16.3 %all-gather.9.cloned.1.call-done.refs_2_ = bf16[1,1024,2048]{2,1,0:T(8,128)(2,1)} async-done(((bf16[1,256,2048]{2,1,0:T(8,128)(2,1)}), bf16[1,1024,2048]{2,1,0:T(8,128)(2,1)}) %all-gather.9.cloned.1.call-update) | async-done | bytes 4194320 | tf_op jit(solution)/shard_map/all_gather | solution.py:918
  297.1 40.9 %moe.3 = (bf16[1024,2048]{1,0:T(8,128)(2,1)}, bf16[1024,2176]{1,0:T(8,128)(2,1)}) custom-call(bf16[1024,2176]{1,0:T(8,128)(2,1)} %get-tuple-element.39.x_ref, bf16[1024,2048]{1,0:T(8,128)(2,1)} %line_gather.3.g_ref, s32[1024,8]{1,0:T(8,128)} %copy.54.routes_ref, bf16[2,2048,1024]{2,1,0:T(8,128)(2,1)} %all-gather.5.cloned.1.call-done.refs_0_, ...), custom_call_target="tpu_custom_call" | custom-call | tf_op jit(solution)/shard_map/moe/pallas_call | solution.py:837
  338.0 81.1 %line_turn.3 = (bf16[1024,2048]{1,0:T(8,128)(2,1)}, f32[32,2048]{1,0:T(8,128)}, f32[16,128]{1,0:T(8,128)}) custom-call(bf16[1024,2176]{1,0:T(8,128)(2,1)} %get-tuple-element.45.refs_0_, bf16[128,2048]{1,0:T(8,128)(2,1)} %constant_dynamic-slice_fusion.1.refs_1_, f32[128,2048]{1,0:T(8,128)} %get-tuple-element.43.refs_6_.refs_2_, f32[1,2048]{1,0:T(1,128)} %bitcast.84, ...), custom_call_target="tpu_custom_call" | custom-call | tf_op jit(solution)/shard_map/line_turn/pallas_call | solution.py:401
  420.0 15.3 %attend_back.1 = (f32[1024,512]{1,0:T(8,128)}, bf16[1024,256]{1,0:T(8,128)(2,1)}, f32[2,1024]{1,0:T(2,128)}, f32[16,256]{1,0:T(8,128)}) custom-call(s32[1]{0:T(128)S(6)} %copy.63.prefix_ref, bf16[1024,2048]{1,0:T(8,128)(2,1)} %get-tuple-element.51.g_ref, bf16[256,2048]{1,0:T(8,128)(2,1)} %copy-done.2, bf16[16,2048]{1,0:T(8,128)(2,1)} %copy-done.6, ...), custom_call_target="tpu_custom_call" | custom-call | tf_op jit(solution)/shard_map/attend_back/pallas_call | solution.py:641
  435.3 10.0 %small_gather.3 = f32[8,2,1024]{2,1,0:T(2,128)} custom-call(f32[2,1024]{1,0:T(2,128)} %get-tuple-element.60.x_ref), custom_call_target="tpu_custom_call" | custom-call | tf_op jit(solution)/shard_map/small_gather/pallas_call | solution.py:316
  445.4 0.9 reduce_sum.28
  446.3 1.1 copy.55
  447.3 22.0 %inputs_back.1 = (bf16[1152,2048]{1,0:T(8,128)(2,1)}, f32[48,256]{1,0:T(8,128)}) custom-call(f32[1024,512]{1,0:T(8,128)} %get-tuple-element.58.scaled_ref, bf16[1024,256]{1,0:T(8,128)(2,1)} %get-tuple-element.59.dv_ref, f32[1024,768]{1,0:T(8,128)} %get-tuple-element.36.proj_ref, f32[1024,2]{1,0:T(8,128)} %bitcast.73, f32[1024,2]{1,0:T(8,128)} %bitcast.74, ...), custom_call_target="tpu_custom_call" | custom-call | tf_op jit(solution)/shard_map/inputs_back/pallas_call | solution.py:716
  469.3 46.5 %line_reduce.1 = f32[1152,256]{1,0:T(8,128)} custom-call(bf16[1152,2048]{1,0:T(8,128)(2,1)} %get-tuple-element.64.p_ref), custom_call_target="tpu_custom_call" | custom-call | tf_op jit(solution)/shard_map/line_reduce/pallas_call | solution.py:271
  515.9 1.0 fusion.9
  517.0 9.5 %all_gather.20 = bf16[4,168,256]{2,1,0:T(8,128)(2,1)S(1)} all-gather(bf16[1,168,256]{2,1,0:T(8,128)(2,1)S(1)} %maximum_maximum_fusion), channel_id=1, replica_groups=mesh['row'=4,'col'=8] {'row'}, dimensions={0}, use_global_device_ids=true | all-gather | bytes 430080 | tf_op jit(solution)/shard_map/all_gather | solution.py:1069
  528.2 1.0 copy.58
  529.9 1.5 fusion.16
  532.2 2.4 multiply_subtract_fusion
  (81 shorter events, 14.6 us)
Async XLA Ops:
  7.2 6.1 %copy-start = (bf16[5,8,2048,16]{2,3,1,0:T(8,128)(2,1)S(1)}, bf16[5,8,2048,16]{2,3,1,0:T(8,128)(2,1)}, u32[]{:S(2)}) copy-start(bf16[5,8,2048,16]{2,3,1,0:T(8,128)(2,1)} %param.34) | copy-start | bytes 7864324
  7.2 226.9 %all-gather.11.cloned.1.call-start = ((), (), s32[]{:S(2)}) async-start(), calls=%async_computation.4 | async-start | bytes 5242880 | tf_op jit(solution)/shard_map/all_gather | solution.py:918
  10.5 223.6 %all-gather.5.cloned.1.call-start = ((), (), s32[]{:S(2)}) async-start(), calls=%async_computation.1 | async-start | bytes 10485760 | tf_op jit(solution)/shard_map/all_gather | solution.py:915
  11.2 231.5 %all-gather.7.cloned.1.call-start = ((), (), s32[]{:S(2)}) async-start(), calls=%async_computation.2 | async-start | bytes 10485760 | tf_op jit(solution)/shard_map/all_gather | solution.py:916
  12.0 285.1 %all-gather.9.cloned.1.call-start = ((), (), s32[]{:S(2)}) async-start(), calls=%async_computation.3 | async-start | bytes 5242880 | tf_op jit(solution)/shard_map/all_gather | solution.py:918
  12.6 522.0 %reduce-scatter.2.cloned.1.call-start = ((), (), s32[]{:S(2)}) async-start(), calls=%async_computation.5 | async-start | bytes 4718592 | tf_op jit(solution)/shard_map/reduce_scatter | solution.py:1012
  14.0 39.8 %copy-start.12 = (pred[48]{0:T(512)(128)(4,1)S(1)}, pred[48]{0:T(512)(128)(4,1)}, u32[]{:S(2)}) copy-start(pred[48]{0:T(512)(128)(4,1)} %constant.19.clone.1) | copy-start | bytes 148
  55.0 30.1 %copy-start.7 = (bf16[2048,16]{0,1:T(8,128)(2,1)S(1)}, bf16[2048,16]{0,1:T(8,128)(2,1)}, u32[]{:S(2)}) copy-start(bf16[2048,16]{0,1:T(8,128)(2,1)} %param.30) | copy-start | bytes 196612
  85.1 40.0 %copy-start.9 = (s32[1024,8]{0,1:T(8,128)S(1)}, s32[1024,8]{0,1:T(8,128)}, u32[]{:S(2)}) copy-start(s32[1024,8]{0,1:T(8,128)} %param.37) | copy-start | bytes 98308
  86.0 41.0 %copy-start.5 = (bf16[256,2048]{1,0:T(8,128)(2,1)S(1)}, bf16[256,2048]{1,0:T(8,128)(2,1)}, u32[]{:S(2)}) copy-start(bf16[256,2048]{1,0:T(8,128)(2,1)} %param.29) | copy-start | bytes 3145732
  127.0 5.0 copy-start.6
  127.4 5.9 %copy-start.2 = (bf16[256,2048]{1,0:T(8,128)(2,1)}, bf16[256,2048]{1,0:T(8,128)(2,1)S(1)}, u32[]{:S(2)}) copy-start(bf16[256,2048]{1,0:T(8,128)(2,1)S(1)} %fusion.map_ref) | copy-start | bytes 3145732
  469.3 46.5 %copy-start.10 = (f32[16,256]{1,0:T(8,128)S(1)}, f32[16,256]{1,0:T(8,128)}, u32[]{:S(2)}) copy-start(f32[16,256]{1,0:T(8,128)} %get-tuple-element.65) | copy-start | bytes 49156
  469.3 46.5 %copy-start.8 = (f32[48,256]{1,0:T(8,128)S(1)}, f32[48,256]{1,0:T(8,128)}, u32[]{:S(2)}) copy-start(f32[48,256]{1,0:T(8,128)} %get-tuple-element.66) | copy-start | bytes 147460
  515.9 16.3 %copy-start.4 = (bf16[1024,256]{1,0:T(8,128)(2,1)S(1)}, bf16[1024,256]{1,0:T(8,128)(2,1)}, u32[]{:S(2)}) copy-start(bf16[1024,256]{1,0:T(8,128)(2,1)} %x_ref.2) | copy-start | bytes 1572868
  528.2 6.4 %copy-start.1 = (bf16[5,8,2048,16]{2,3,1,0:T(8,128)(2,1)S(1)}, bf16[5,8,2048,16]{2,3,1,0:T(8,128)(2,1)}, u32[]{:S(2)}) copy-start(bf16[5,8,2048,16]{2,3,1,0:T(8,128)(2,1)} %param.34) | copy-start | bytes 7864324
  529.3 3.0 copy-start.3
  531.6 0.7 copy-start.11
Sparse Core Ops, SparseCore 0:
  10.6 53.6 all-gather.10
  66.1 87.3 all-gather.4
  155.3 87.3 all-gather.6
  244.5 52.5 all-gather.8
  419.3 51.0 reduce-scatter.1

commit v3 on v2

--- a/solution.py
+++ b/solution.py
@@ -48,10 +48,12 @@
     return here, here // 2, core, here + 1 - 2 * core
 
 
-def line_barrier(chips):
+def line_barrier(chips, across=()):
     here, chip, core, mate = line_place()
     barrier = pltpu.get_barrier_semaphore()
     has_left, has_right = chip > 0, chip < chips - 1
+    for other in across:
+        pl.semaphore_signal(barrier, inc=1, device_id={"row": other}, device_id_type=MESH_ID)
     pl.semaphore_signal(barrier, inc=1, device_id={"col": mate}, device_id_type=MESH_ID)
 
     @pl.when(has_left)
@@ -66,11 +68,11 @@
 
     @pl.when(inner)
     def _():
-        pl.semaphore_wait(barrier, 3)
+        pl.semaphore_wait(barrier, 3 + len(across))
 
     @pl.when(jnp.logical_not(inner))
     def _():
-        pl.semaphore_wait(barrier, 2)
+        pl.semaphore_wait(barrier, 2 + len(across))
 
 
 def spot(axis, size, parts, block, part):
@@ -81,11 +83,23 @@
     return (pl.ds(part * step, step), pl.ds(pl.multiple_of(block * cols, 128), cols))
 
 
-def gather_body(chips, parts, axis, x_ref, o_ref, right_sem, left_sem, mate_sem, line_recv, mate_recv, own_sem):
+def run(*steps):
+    steps = list(steps)
+    while steps:
+        for one in list(steps):
+            if next(one, steps) is steps:
+                steps.remove(one)
+
+
+def gather_body(chips, parts, axis, x_ref, o_ref, *sems):
+    line_barrier(chips)
+    run(gather_steps(chips, parts, axis, x_ref, o_ref, *sems))
+
+
+def gather_steps(chips, parts, axis, x_ref, o_ref, right_sem, left_sem, mate_sem, line_recv, mate_recv, own_sem):
     here, chip, core, mate = line_place()
     size = x_ref.shape
     step = size[0] // parts
-    line_barrier(chips)
 
     def at(block, part):
         return o_ref.at[spot(axis, size, parts, block, part)]
@@ -118,6 +132,7 @@
             pltpu.make_async_copy(x_ref.at[pl.ds(part * step, step)], at(here, part), own_sem.at[part])
         )
         own[-1].start()
+    yield
     for far in range(1, chips):
         for part in range(parts):
 
@@ -130,6 +145,8 @@
             def _():
                 copy(chip + far, part, left_sem, line_recv, mate).wait_recv()
                 forward(chip + far, part, False, True, False)
+
+        yield
 
     for own_copy in own:
         own_copy.wait()
@@ -164,13 +181,17 @@
     )(x)
 
 
-def reduce_body(
+def reduce_body(chips, parts, axis, *refs):
+    line_barrier(chips)
+    run(reduce_steps(chips, parts, axis, *refs))
+
+
+def reduce_steps(
     chips, parts, axis, p_ref, o_ref, pair_buf, line_buf, sums, right_sem, left_sem, mate_sem, line_recv, mate_recv
 ):
     here, chip, core, mate = line_place()
     size = o_ref.shape
     step = size[0] // parts
-    line_barrier(chips)
 
     def rows(part):
         return pl.ds(part * step, step)
@@ -205,6 +226,8 @@
                 def _():
                     mate_copy(chip - far, part).start()
 
+    yield
+
     def pair_sum(j, part):
         mate_copy(j, part).wait_recv()
         return p_ref[at(2 * j + core, part)].astype(F32) + pair_buf[j, rows(part)].astype(F32)
@@ -234,6 +257,8 @@
                 pass_on(
                     chip - far, chips if far == 1 else chip - far, part, chip < chips - 1, left_sem, here - 2
                 )
+
+        yield
 
     for part in range(parts):
         o_ref[rows(part)] = pair_sum(chip, part)
@@ -324,19 +349,96 @@
     )(x)
 
 
-def turn_body(chips, parts, first, last, held, late_count, *refs):
-    p_ref = refs[0]
-    operands = refs[1 : 1 + held]
-    o_ref = refs[1 + held]
-    results = refs[2 + held : 2 + held + late_count]
-    sums_in, pair_buf, line_buf, sums = refs[2 + held + late_count : 6 + held + late_count]
-    reduce_sems = refs[6 + held + late_count : 11 + held + late_count]
-    gather_sems = refs[11 + held + late_count : 16 + held + late_count]
-    reduce_body(chips, parts, 0, p_ref, sums_in, pair_buf, line_buf, sums, *reduce_sems)
+def row_copy(src, dst, sems, which, device):
+    return pltpu.make_async_remote_copy(
+        src_ref=src,
+        dst_ref=dst,
+        send_sem=sems[0].at[which],
+        recv_sem=sems[1].at[which],
+        device_id={"row": device},
+        device_id_type=MESH_ID,
+    )
+
+
+def row_partners():
+    here = lax.axis_index("row")
+    major, minor = here // 2, here % 2
+    return 2 * major + 1 - minor, 2 * (1 - major) + minor
+
+
+def row_gather_steps(x_ref, o_ref, *sems):
+    near, next_one = row_partners()
+    half = x_ref.shape[0] // 2
+
+    def side(neighbour, first):
+        slot, device = (0, near) if neighbour == 0 else (1, next_one)
+        rows = pl.ds(first * half, half)
+        return row_copy(x_ref.at[rows], o_ref.at[slot, rows], sems, 2 * slot + first, device)
+
+    def onward(neighbour):
+        slot, device = (0, next_one) if neighbour == 0 else (1, near)
+        rows = pl.ds(slot * half, half)
+        return row_copy(o_ref.at[slot, rows], o_ref.at[2, rows], sems, 4 + slot, device)
+
+    side(0, 0).start()
+    side(1, 1).start()
+    side(0, 1).start()
+    side(1, 0).start()
+    yield
+    yield
+    yield
+    yield
+    side(0, 0).wait_recv()
+    onward(0).start()
+    side(1, 1).wait_recv()
+    onward(1).start()
+    yield
+    for neighbour in range(2):
+        side(neighbour, 1 - neighbour).wait_recv()
+        onward(neighbour).wait_recv()
+        onward(neighbour).wait_send()
+        side(neighbour, 0).wait_send()
+        side(neighbour, 1).wait_send()
+
+
+def turn_body(chips, parts, first, last, held, late_count, riders, *refs):
+    refs = list(refs)
+
+    def take(count):
+        taken = refs[:count]
+        del refs[:count]
+        return taken
+
+    (p_ref,) = take(1)
+    operands = take(held)
+    rider_in = take(riders)
+    (o_ref,) = take(1)
+    results = take(late_count)
+    rider_out = take(riders)
+    sums_in, pair_buf, line_buf, sums = take(4)
+    reduce_sems = take(5)
+    gather_sems = take(5)
+    line_barrier(chips, row_partners() if riders > 1 else ())
+    steps = [reduce_steps(chips, parts, 0, p_ref, sums_in, pair_buf, line_buf, sums, *reduce_sems)]
+    if riders > 0:
+        steps.append(gather_steps(chips, 2, 1, rider_in[0], rider_out[0], *take(6)))
+    if riders > 1:
+        across = row_gather_steps(rider_in[1], rider_out[1], *take(2))
+        next(across)
+    run(*steps)
     here = lax.axis_index("col")
     own = o_ref.shape[0] // (2 * chips)
     kept = first(sums_in, operands, results, o_ref, pl.ds(pl.multiple_of(here * own, 8), own))
-    gather_rows(chips, parts, o_ref, *gather_sems, lambda: last(kept, operands, results))
+
+    def beside():
+        if riders > 1:
+            for _ in range(4):
+                next(across)
+        last(kept, operands, results)
+
+    gather_rows(chips, parts, o_ref, *gather_sems, beside)
+    if riders > 1:
+        run(across)
 
 
 def gather_rows(chips, parts, o_ref, right_sem, left_sem, mate_sem, line_recv, mate_recv, beside):
@@ -393,16 +495,25 @@
                 copy(j, part, left_sem, line_recv, here - 2).wait_send()
 
 
-def line_turn(p, operands, width, results, first, last, chips, ident, parts=2):
+def line_turn(p, operands, width, results, first, last, chips, ident, riders=(), parts=2):
     rows, cols = p.shape
     own = rows // (2 * chips)
     sems = pltpu.SemaphoreType.DMA((chips, parts))
     longer = pltpu.SemaphoreType.DMA((chips + 1, parts))
+    more = []
+    ridden = []
+    if len(riders) > 0:
+        height, part = riders[0].shape
+        ridden.append(jax.ShapeDtypeStruct((height, 2 * chips * part), BF16))
+        more += [pltpu.SemaphoreType.DMA((chips, 2))] * 5 + [pltpu.SemaphoreType.DMA((2,))]
+    if len(riders) > 1:
+        ridden.append(jax.ShapeDtypeStruct((3,) + riders[1].shape, BF16))
+        more += [pltpu.SemaphoreType.DMA((6,))] * 2
     return pl.pallas_call(
-        functools.partial(turn_body, chips, parts, first, last, len(operands), len(results)),
-        out_shape=(jax.ShapeDtypeStruct((rows, width), BF16),) + tuple(results),
-        in_specs=[VM] * (1 + len(operands)),
-        out_specs=(VM,) * (1 + len(results)),
+        functools.partial(turn_body, chips, parts, first, last, len(operands), len(results), len(riders)),
+        out_shape=(jax.ShapeDtypeStruct((rows, width), BF16),) + tuple(results) + tuple(ridden),
+        in_specs=[VM] * (1 + len(operands)) + [VM, ANY][: len(riders)],
+        out_specs=(VM,) * (1 + len(results)) + (VM, ANY)[: len(riders)],
         scratch_shapes=[
             pltpu.VMEM((own, cols), F32),
             pltpu.VMEM((chips, own, cols), BF16),
@@ -414,12 +525,13 @@
             longer,
             sems,
         ]
-        + [sems] * 5,
+        + [sems] * 5
+        + more,
         compiler_params=pltpu.CompilerParams(
             collective_id=ident, has_side_effects=True, vmem_limit_bytes=VMEM_LIMIT
         ),
         name="line_turn",
-    )(p, *operands)
+    )(p, *operands, *riders)
 
 
 def inverse_rms(values):
@@ -483,6 +595,8 @@
 
 
 def row_sums(values):
+    lanes = 128
+    values = sum(values[:, n : n + lanes] for n in range(0, values.shape[1], lanes))
     high = values.astype(BF16)
     rest = (values - high.astype(F32)).astype(BF16)
     ones = jnp.ones((8, values.shape[1]), BF16)
@@ -656,41 +770,46 @@
 
 def inputs_back_body(
     tile, extra, scaled_ref, dv_ref, proj_ref, inv_ref, stat_ref, wq, wk, wv, b_ref, a_ref, x_ref, inv1_ref,
-    gain_ref, mid_ref, late_ref, router_ref, p_ref, gb_ref,
+    gain_ref, mid_ref, late_ref, router_ref, p_ref, gb_ref, w_ref, w_sems,
 ):
     seq_len, width = x_ref.shape
     part = dv_ref.shape[1]
     ranks = a_ref.shape[0]
     rank = ranks // 3
-    grad_b = [jnp.zeros((rank, part), F32) for _ in range(3)]
+    fetches = [
+        pltpu.make_async_copy(w, w_ref.at[:, pl.ds(m * part, part)], w_sems.at[m]) for m, w in enumerate((wq, wk, wv))
+    ]
+    for fetch in fetches:
+        fetch.start()
+    grad_b = jnp.zeros((ranks, 3 * part), F32)
     grad_a = jnp.zeros((ranks, width), F32)
     stats = jnp.zeros((8, width), F32)
     line = lax.broadcasted_iota(jnp.int32, (8, width), 0)
     for t in range(seq_len // tile):
         rows = pl.ds(t * tile, tile)
-        normed_part = jnp.zeros((tile, width), F32)
-        middles = []
-        for m, w in enumerate((wq, wk, wv)):
-            if m < 2:
-                cols = pl.ds(m * part, part)
-                inv = inv_ref[rows, m : m + 1]
-                shift = inv * inv * inv * stat_ref[rows, m : m + 1]
-                grad = (inv * scaled_ref[rows, cols] - proj_ref[rows, cols] * shift).astype(BF16)
-            else:
-                grad = dv_ref[rows]
-            middles.append(nt(grad, b_ref[pl.ds(m * rank, rank)]).astype(BF16))
-            normed_part += nt(grad, w[...]) + nn(middles[m], a_ref[pl.ds(m * rank, rank)])
-            grad_b[m] += tn(mid_ref[rows, m * rank : (m + 1) * rank], grad)
+        grads = []
+        for m in range(2):
+            cols = pl.ds(m * part, part)
+            inv = inv_ref[rows, m : m + 1]
+            shift = inv * inv * inv * stat_ref[rows, m : m + 1]
+            grads.append((inv * scaled_ref[rows, cols] - proj_ref[rows, cols] * shift).astype(BF16))
+        grads = jnp.concatenate(grads + [dv_ref[rows]], axis=1)
+        middle = nt(grads, b_ref[...]).astype(BF16)
+        if t == 0:
+            for fetch in fetches:
+                fetch.wait()
+        normed_part = nt(grads, w_ref[...]) + nn(middle, a_ref[...])
+        grad_b += tn(mid_ref[rows], grads)
         p_ref[rows] = normed_part.astype(BF16)
         scaled_x = x_ref[rows].astype(F32) * gain_ref[...]
         normed = (scaled_x * inv1_ref[rows]).astype(BF16)
-        grad_a += jnp.concatenate([tn(middle, normed) for middle in middles], axis=0)
+        grad_a += tn(middle, normed)
         first = row_sums(scaled_x * normed_part)
         for j in range(tile // part):
             wide = jnp.concatenate([first[:, j * part : (j + 1) * part]] * (width // part), axis=1)
             stats = jnp.where(line == (t * tile) // part + j, wide, stats)
     for m in range(3):
-        gb_ref[pl.ds(m * rank, rank)] = grad_b[m]
+        gb_ref[pl.ds(m * rank, rank)] = grad_b[m * rank : (m + 1) * rank, m * part : (m + 1) * part]
     high = stats.astype(BF16).astype(F32)
     router = router_ref[...]
     if part > router.shape[1]:
@@ -704,8 +823,7 @@
     ]
     used = sum(piece.shape[0] for piece in pieces)
     pieces.append(jnp.zeros((extra - used, width), F32))
-    start = seq_len
-    p_ref[pl.ds(start, extra)] = jnp.concatenate(pieces, axis=0).astype(BF16)
+    p_ref[pl.ds(seq_len, extra)] = jnp.concatenate(pieces, axis=0).astype(BF16)
 
 
 def inputs_back(extra, *operands):
@@ -719,126 +837,117 @@
             jax.ShapeDtypeStruct((seq_len + extra, width), BF16),
             jax.ShapeDtypeStruct((ranks, part), F32),
         ),
-        in_specs=[VM] * len(operands),
+        in_specs=[ANY if 5 <= n < 8 else VM for n in range(len(operands))],
         out_specs=(VM,) * 2,
+        scratch_shapes=[pltpu.VMEM((width, 3 * part), BF16), pltpu.SemaphoreType.DMA((3,))],
         compiler_params=pltpu.CompilerParams(vmem_limit_bytes=VMEM_LIMIT),
         name="inputs_back",
     )(*operands)
 
 
-def moe_body(experts, chosen, tile, done, x_ref, g_ref, routes_ref, *refs):
-    count = len(chosen)
-    weights = refs[: 3 * count]
-    refs = refs[3 * count :]
-    if done:
-        earlier, hidden_ref, refs = refs[:3], refs[3], refs[4:]
-    out_ref, dx_ref = refs[:2]
-    gate_ref = None if done else refs[2]
-    out_acc, dx_acc, gate_acc, wgu, wd, sems = refs[2 if done else 3 :]
+def moe_body(experts, tile, count, x_ref, g_ref, routes_ref, hidden_ref, gate_w, up_w, *refs):
+    downs = refs[:count]
+    out_ref, dx_ref, out_acc, dx_acc, gate_acc, wgu, wd, sems = refs[count:]
     hidden = wd.shape[1]
     tokens, width = g_ref.shape
     lanes = gate_acc.shape[1]
-    pieces = weights[0].shape[2] // hidden
+    local = gate_w.shape[0]
+    pieces = gate_w.shape[2] // hidden
+    steps = local * pieces
     here = lax.axis_index("col")
-    local = experts // lax.axis_size("col")
-
-    def copies(a, piece, slot):
-        gate, up, down = weights[3 * a : 3 * a + 3]
-        which, at_gate, at_down = chosen[a]
-        units = pl.ds(pl.multiple_of(piece * hidden, 128), hidden)
-        return (
-            pltpu.make_async_copy(gate.at[at_gate, :, units], wgu.at[slot, :, pl.ds(0, hidden)], sems.at[slot, 0]),
-            pltpu.make_async_copy(up.at[at_gate, :, units], wgu.at[slot, :, pl.ds(hidden, hidden)], sems.at[slot, 1]),
-            pltpu.make_async_copy(down.at[at_down, units], wd.at[slot], sems.at[slot, 2]),
-        )
-
-    for copy in copies(0, 0, 0):
-        copy.start()
-    if done:
-        out_acc[...] = earlier[0][...].astype(F32)
-        dx_acc[...] = earlier[1][...].astype(F32)
-        gate_acc[...] = earlier[2][...]
-        own = hidden_ref.shape[0]
-        out_acc[pl.ds(pl.multiple_of(here * own, 8), own)] += hidden_ref[...]
-    else:
-        out_acc[...] = jnp.zeros_like(out_acc)
-        dx_acc[...] = jnp.zeros_like(dx_acc)
-        gate_acc[...] = jnp.zeros_like(gate_acc)
-
-    for a in range(count):
-        e = here * local + chosen[a][0]
-
-        def one_step(piece, carry):
-            slot = piece % 2
-            for copy in copies(a, 0, slot):
-                copy.wait()
-
-            @pl.when(piece + 1 < pieces)
-            def _():
-                for copy in copies(a, piece + 1, 1 - slot):
-                    copy.start()
-
-            if a + 1 < count:
-
-                @pl.when(piece + 1 == pieces)
-                def _():
-                    for copy in copies(a + 1, 0, 1 - slot):
-                        copy.start()
-
-            def one_tile(t, carry):
-                rows = pl.ds(pl.multiple_of(t * tile, tile), tile)
-                lane = lax.broadcasted_iota(jnp.int32, (tile, lanes), 1)
-                mine = lane == e
-                halves = jnp.logical_or(mine, lane == e + experts)
-                named = jnp.sum(jnp.where(routes_ref[rows] == e, 1.0, 0.0), axis=1, keepdims=True)
-                gate = jnp.sum(jnp.where(halves, x_ref[rows, width:].astype(F32), 0.0), axis=1, keepdims=True)
-                gate = gate * named
-                both = nn(x_ref[rows, :width], wgu[slot])
-                gate_in, up_in = both[:, :hidden], both[:, hidden:]
-                sigmoid = jax.nn.sigmoid(gate_in)
-                silu = gate_in * sigmoid
-                active = silu * up_in
-                back = nt(g_ref[rows], wd[slot])
-                d_gate = jnp.sum(active * back, axis=1, keepdims=True) * named
-                gate_acc[rows] += jnp.where(mine, d_gate, 0.0)
-                out_acc[rows] += nn((active * gate).astype(BF16), wd[slot])
-                d_active = back * gate
-                d_gate_in = d_active * up_in * (sigmoid + silu * (1.0 - sigmoid))
-                d_up_in = d_active * silu
-                d_both = jnp.concatenate([d_gate_in.astype(BF16), d_up_in.astype(BF16)], axis=1)
-                dx_acc[rows] += nt(d_both, wgu[slot])
-                return carry
-
-            return lax.fori_loop(0, tokens // tile, one_tile, carry)
-
-        lax.fori_loop(0, pieces, one_step, 0)
+    row = lax.axis_index("row")
+
+    def start(step, slot):
+        e, piece = step // pieces, step % pieces
+        if count == 1:
+            place = piece
+        else:
+            place = 2 * ((row // 2 + piece // 2) % 2) + (row + piece) % 2
+        units = pl.ds(pl.multiple_of(place * hidden, 128), hidden)
+        pltpu.make_async_copy(gate_w.at[e, :, units], wgu.at[slot, :, pl.ds(0, hidden)], sems.at[slot, 0]).start()
+        pltpu.make_async_copy(up_w.at[e, :, units], wgu.at[slot, :, pl.ds(hidden, hidden)], sems.at[slot, 1]).start()
+        if count == 1:
+            pltpu.make_async_copy(downs[0].at[e, units], wd.at[slot], sems.at[slot, 2]).start()
+        else:
+
+            @pl.when(piece == 0)
+            def _():
+                pltpu.make_async_copy(downs[0].at[e], wd.at[slot], sems.at[slot, 2]).start()
+
+            @pl.when(piece > 0)
+            def _():
+                other = lax.max(piece - 1, 0)
+                pltpu.make_async_copy(downs[1].at[other, e], wd.at[slot], sems.at[slot, 2]).start()
+
+    def finish(slot):
+        units = pl.ds(0, hidden)
+        pltpu.make_async_copy(gate_w.at[0, :, units], wgu.at[slot, :, units], sems.at[slot, 0]).wait()
+        pltpu.make_async_copy(up_w.at[0, :, units], wgu.at[slot, :, units], sems.at[slot, 1]).wait()
+        pltpu.make_async_copy(downs[0].at[0, units], wd.at[slot], sems.at[slot, 2]).wait()
+
+    start(0, 0)
+    out_acc[...] = jnp.zeros_like(out_acc)
+    dx_acc[...] = jnp.zeros_like(dx_acc)
+    gate_acc[...] = jnp.zeros_like(gate_acc)
+    own = hidden_ref.shape[0]
+    out_acc[pl.ds(pl.multiple_of(here * own, 8), own)] = hidden_ref[...]
+
+    def one_step(step, carry):
+        slot = step % 2
+        finish(slot)
+
+        @pl.when(step + 1 < steps)
+        def _():
+            start(step + 1, 1 - slot)
+
+        e = here * local + step // pieces
+
+        def one_tile(t, carry):
+            rows = pl.ds(pl.multiple_of(t * tile, tile), tile)
+            lane = lax.broadcasted_iota(jnp.int32, (tile, lanes), 1)
+            mine = lane == e
+            halves = jnp.logical_or(mine, lane == e + experts)
+            named = jnp.sum(jnp.where(routes_ref[rows] == e, 1.0, 0.0), axis=1, keepdims=True)
+            gate = jnp.sum(jnp.where(halves, x_ref[rows, width:].astype(F32), 0.0), axis=1, keepdims=True)
+            gate = gate * named
+            both = nn(x_ref[rows, :width], wgu[slot])
+            gate_in, up_in = both[:, :hidden], both[:, hidden:]
+            sigmoid = jax.nn.sigmoid(gate_in)
+            silu = gate_in * sigmoid
+            active = silu * up_in
+            back = nt(g_ref[rows], wd[slot])
+            d_gate = jnp.sum(active * back, axis=1, keepdims=True) * named
+            gate_acc[rows] += jnp.where(mine, d_gate, 0.0)
+            out_acc[rows] += nn((active * gate).astype(BF16), wd[slot])
+            d_active = back * gate
+            d_gate_in = d_active * up_in * (sigmoid + silu * (1.0 - sigmoid))
+            d_up_in = d_active * silu
+            d_both = jnp.concatenate([d_gate_in.astype(BF16), d_up_in.astype(BF16)], axis=1)
+            dx_acc[rows] += nt(d_both, wgu[slot])
+            return carry
+
+        return lax.fori_loop(0, tokens // tile, one_tile, carry)
+
+    lax.fori_loop(0, steps, one_step, 0)
     out_ref[...] = out_acc[...].astype(BF16)
-    if done:
-        dx_ref[:, :width] = dx_acc[...].astype(BF16)
-        high = gate_acc[...].astype(BF16).astype(F32)
-        rest = gate_acc[...] - high
-        dx_ref[:, width:] = (high + pltpu.roll(rest, experts, 1)).astype(BF16)
-    else:
-        dx_ref[...] = dx_acc[...].astype(BF16)
-        gate_ref[...] = gate_acc[...]
-
-
-def moe(x, g, routes, experts, chosen, weights, earlier=None, hidden_rows=None, tile=512):
+    dx_ref[:, :width] = dx_acc[...].astype(BF16)
+    high = gate_acc[...].astype(BF16).astype(F32)
+    rest = gate_acc[...] - high
+    dx_ref[:, width:] = (high + pltpu.roll(rest, experts, 1)).astype(BF16)
+
+
+def moe(x, g, routes, hidden_rows, experts, gate_w, up_w, downs, tile=512):
     tokens, width = g.shape
-    units = weights[0].shape[2]
-    hidden = min(256, units)
     lanes = x.shape[1] - width
-    done = earlier is not None
-    outs = [jax.ShapeDtypeStruct((tokens, width), BF16)]
-    outs.append(jax.ShapeDtypeStruct((tokens, width + (lanes if done else 0)), BF16))
-    if not done:
-        outs.append(jax.ShapeDtypeStruct((tokens, lanes), F32))
-    more = (tuple(earlier) + (hidden_rows,)) if done else ()
+    hidden = downs[0].shape[1] if len(downs) > 1 else min(256, gate_w.shape[2])
     return pl.pallas_call(
-        functools.partial(moe_body, experts, chosen, min(tile, tokens), done),
-        out_shape=tuple(outs),
-        in_specs=[VM] * 3 + [ANY] * len(weights) + [VM] * len(more),
-        out_specs=(VM,) * len(outs),
+        functools.partial(moe_body, experts, min(tile, tokens), len(downs)),
+        out_shape=(
+            jax.ShapeDtypeStruct((tokens, width), BF16),
+            jax.ShapeDtypeStruct((tokens, width + lanes), BF16),
+        ),
+        in_specs=[VM] * 4 + [ANY] * (2 + len(downs)),
+        out_specs=(VM, VM),
         scratch_shapes=[
             pltpu.VMEM((tokens, width), F32),
             pltpu.VMEM((tokens, width), F32),
@@ -849,7 +958,7 @@
         ],
         compiler_params=pltpu.CompilerParams(vmem_limit_bytes=VMEM_LIMIT),
         name="moe",
-    )(x, g, routes, *weights, *more)
+    )(x, g, routes, hidden_rows, gate_w, up_w, *downs)
 
 
 def rope_tables(length, head_dim):
@@ -914,9 +1023,8 @@
 
     full_gate = lax.all_gather(w_gate, "row", axis=2, tiled=True)
     full_up = lax.all_gather(w_up, "row", axis=2, tiled=True)
-    full_down = [
-        lax.all_gather(w_down[e : e + 1], "row", axis=1, tiled=True) for e in range(local_experts)
-    ]
+    across = row_count == 4
+    riders = (cotangent, w_down) if across else (cotangent,)
     adapter_slot = adapter_index[0]
     chosen_a = lax.dynamic_index_in_dim(adapter_a, adapter_slot, 1, keepdims=False).swapaxes(1, 2)
     chosen_b = lax.dynamic_index_in_dim(adapter_b, adapter_slot, 1, keepdims=False)
@@ -951,7 +1059,7 @@
     )
     wide = full_width + lanes
     row_shape = jax.ShapeDtypeStruct
-    normed_two, hidden_rows, mid_out, mid_router, probs = line_turn(
+    normed_two, hidden_rows, mid_out, mid_router, probs, full_cot, *down_others = line_turn(
         part_out,
         (held_rows(full_inputs), gain_second, chosen_a[4], router_rows, router_up),
         wide,
@@ -965,29 +1073,14 @@
         lambda kept, operands, results: None,
         chips,
         2,
+        riders,
     )
-    full_cot = line_gather(cotangent, chips, 1, 4)
-
-    early = tuple((e, e, 0) for e in range(local_experts - 1)) if local_experts > 1 else ()
-    final = ((local_experts - 1, local_experts - 1, 0),)
-    first = moe(
-        normed_two,
-        full_cot,
-        routes,
-        expert_total,
-        early,
-        sum([(full_gate, full_up, full_down[e]) for e, _, _ in early], ()),
-    )
-    moe_out, back_out = moe(
-        normed_two,
-        full_cot,
-        routes,
-        expert_total,
-        final,
-        (full_gate, full_up, full_down[-1]),
-        first,
-        hidden_rows,
-    )
+    if across:
+        downs = (w_down,) + tuple(down_others)
+    else:
+        downs = (lax.all_gather(w_down, "row", axis=1, tiled=True),)
+
+    moe_out, back_out = moe(normed_two, full_cot, routes, hidden_rows, expert_total, full_gate, full_up, downs)
     grad_attn, late, router_late = line_turn(
         back_out,
         (
@@ -1035,7 +1128,7 @@
         w_query,
         w_key,
         w_value,
-        b_three,
+        b_cols,
         a_three,
         full_inputs,
         inv_first,

time: 549 us -> 521 us (0.949)
  waiting for transfers between devices: 26.9 us -> 2.9 us
    pallas_call x2, Pallas kernels: 166 us -> 220 us  [line_turn(): pl.pallas_call(functools.partial(turn_body, chips, parts, first, last, le...]
    pallas_call x2 -> x1, Pallas kernels: 77.9 us -> 38.7 us  [line_gather(): pl.pallas_call(functools.partial(gather_body, chips, parts, axis), out_sh...]
    all_gather x2 -> x0, waiting for transfers between devices: 16.3 us -> none  [shards(): lax.all_gather(w_down[e:e + 1], 'row', axis=1, tiled=True)]
    pallas_call x2 -> x1, Pallas kernels: 78.9 us -> 67.4 us  [moe(): pl.pallas_call(functools.partial(moe_body, experts, min(tile, tokens), le...]
    all_gather x1, waiting for transfers between devices: 8.65 us -> 1.5 us  [shards(): full_up = lax.all_gather(w_up, 'row', axis=2, tiled=True)]
  transfers between devices with their start and end apart: 5 -> 3, of which waited for: 2 -> 1; matrix products, arithmetic and copies ran while one was open for 6% -> 6% of each run, Pallas kernels for 61% -> 59%
where the time goes in v3:
time: 521 us; the launch traced here: 514 us
  Pallas kernels  453 us (87%)
  local copies, waits for them, and re-layouts  20.5 us (4%)
  between operations  15.8 us (3%)
  other arithmetic  12.5 us (2%)
  blocking collectives  9.22 us (2%)
    pallas_call x2, Pallas kernels, line_turn(): pl.pallas_call(functools.partial(turn_body, chips, parts, first, last, le...  220 us
    pallas_call x1, Pallas kernels, moe(): pl.pallas_call(functools.partial(moe_body, experts, min(tile, tokens), le...  67.4 us
    pallas_call x1, Pallas kernels, line_reduce(): pl.pallas_call(functools.partial(reduce_body, chips, parts, axis), out_sh...  46.5 us
    pallas_call x1, Pallas kernels, line_gather(): pl.pallas_call(functools.partial(gather_body, chips, parts, axis), out_sh...  38.7 us
    pallas_call x2, Pallas kernels, small_gather(): pl.pallas_call(functools.partial(small_body, count), out_shape=jax.ShapeD...  19.4 us
    pallas_call x1, Pallas kernels, inputs_back(): pl.pallas_call(functools.partial(inputs_back_body, min(256, seq_len), ext...  18.8 us
    pallas_call x1, Pallas kernels, attend_back(): pl.pallas_call(functools.partial(attend_back_body, min(256, seq_len), rea...  15.4 us
    pallas_call x1, Pallas kernels, project(): pl.pallas_call(functools.partial(project_body, min(256, seq_len)), out_sh...  14.8 us
  transfers between devices with their start and end apart: 3, of which 1 were waited for; matrix products, arithmetic and copies ran while one was open for 6% of the time, Pallas kernels for 59%

profile of v3, /device:TPU:16, one launch (start us, length us, event | category | flops | bytes accessed | tf_op | source)
XLA Modules:
  0.0 514.2 jit_solution(5835927721318725031)
XLA Ops:
  10.1 38.7 %line_gather.1.x_ref = bf16[1024,2048]{1,0:T(8,128)(2,1)} custom-call(bf16[1024,256]{1,0:T(8,128)(2,1)} %x_ref.1), custom_call_target="tpu_custom_call" | custom-call | tf_op jit(solution)/shard_map/line_gather/pallas_call | solution.py:171
  48.8 1.0 constant_dynamic-slice_fusion
  50.5 14.8 %project.1 = (f32[1024,768]{1,0:T(8,128)}, bf16[1024,48]{1,0:T(8,128)(2,1)}, f32[1024,1]{1,0:T(8,128)}, f32[2,1024]{1,0:T(2,128)}) custom-call(bf16[1024,2048]{1,0:T(8,128)(2,1)} %line_gather.1.x_ref, f32[1,2048]{1,0:T(1,128)} %bitcast.81, bf16[2048,256]{1,0:T(8,128)(2,1)} %wq.3, bf16[2048,256]{1,0:T(8,128)(2,1)} %wk.3, bf16[2048,256]{1,0:T(8,128)(2,1)} %wv.3, ...), custom_call_target="tpu_custom_call" | custom-call | tf_op jit(solution)/shard_map/project/pallas_call | solution.py:628
  65.3 9.4 %small_gather.2 = f32[8,2,1024]{2,1,0:T(2,128)} custom-call(f32[2,1024]{1,0:T(2,128)} %get-tuple-element.36.x_ref), custom_call_target="tpu_custom_call" | custom-call | tf_op jit(solution)/shard_map/small_gather/pallas_call | solution.py:341
  74.7 0.9 reduce_sum.27
  75.6 1.1 copy.47
  77.4 0.8 dynamic_slice.41
  80.9 0.9 pad.10.refs_4_.refs_5_
  81.8 1.0 copy.49.routes_ref
  82.8 0.8 dynamic-slice_bitcast_fusion.1.b_ref
  84.1 2.3 concatenate.44.map_ref
  87.1 2.0 fusion.6
  89.0 1.3 pad_maximum_fusion
  90.3 11.8 %attend.1 = (bf16[1024,2176]{1,0:T(8,128)(2,1)}, bf16[1024,256]{1,0:T(8,128)(2,1)}, bf16[1024,256]{1,0:T(8,128)(2,1)}, bf16[1024,256]{1,0:T(8,128)(2,1)}, bf16[1024,256]{1,0:T(8,128)(2,1)}, /*index=5*/f32[1024,2]{1,0:T(8,128)}) custom-call(s32[1]{0:T(128)S(6)} %copy.58.prefix_ref, f32[1024,768]{1,0:T(8,128)} %get-tuple-element.35.proj_ref, ...), custom_call_target="tpu_custom_call" | custom-call | tf_op jit(solution)/shard_map/attend/pallas_call | solution.py:686
  102.1 1.9 constant_dynamic-slice_fusion.2.refs_1_
  104.0 138.5 %line_turn.2 = (bf16[1024,2176]{1,0:T(8,128)(2,1)}, f32[128,2048]{1,0:T(8,128)}, bf16[128,128]{1,0:T(8,128)(2,1)}, bf16[128,16]{1,0:T(8,128)(2,1)}, f32[128,128]...) custom-call(bf16[1024,2176]{1,0:T(8,128)(2,1)} %get-tuple-element.37.refs_0_, ...), custom_call_target="tpu_custom_call" | custom-call | tf_op jit(solution)/shard_map/line_turn/pallas_call | solution.py:512
  242.5 1.9 constant_dynamic-slice_fusion.1.refs_1_
  244.4 1.5 all-gather.5.cloned.1.call-done.up_w
  245.9 67.4 %moe.1 = (bf16[1024,2048]{1,0:T(8,128)(2,1)}, bf16[1024,2176]{1,0:T(8,128)(2,1)}) custom-call(bf16[1024,2176]{1,0:T(8,128)(2,1)} %get-tuple-element.38.x_ref, bf16[1024,2048]{1,0:T(8,128)(2,1)} %get-tuple-element.39.g_ref, s32[1024,8]{1,0:T(8,128)} %copy.49.routes_ref, f32[128,2048]{1,0:T(8,128)} %get-tuple-element.40.hidden_ref.refs_2_, ...), custom_call_target="tpu_custom_call" | custom-call | tf_op jit(solution)/shard_map/moe/pallas_call | solution.py:943
  313.3 81.5 %line_turn.3 = (bf16[1024,2048]{1,0:T(8,128)(2,1)}, f32[32,2048]{1,0:T(8,128)}, f32[16,128]{1,0:T(8,128)}) custom-call(bf16[1024,2176]{1,0:T(8,128)(2,1)} %get-tuple-element.43.refs_0_, bf16[128,2048]{1,0:T(8,128)(2,1)} %constant_dynamic-slice_fusion.1.refs_1_, f32[128,2048]{1,0:T(8,128)} %get-tuple-element.40.hidden_ref.refs_2_, f32[1,2048]{1,0:T(1,128)} %bitcast.84, ...), custom_call_target="tpu_custom_call" | custom-call | tf_op jit(solution)/shard_map/line_turn/pallas_call | solution.py:512
  394.8 0.8 dynamic_slice.49
  395.6 15.4 %attend_back.1 = (f32[1024,512]{1,0:T(8,128)}, bf16[1024,256]{1,0:T(8,128)(2,1)}, f32[2,1024]{1,0:T(2,128)}, f32[16,256]{1,0:T(8,128)}) custom-call(s32[1]{0:T(128)S(6)} %copy.58.prefix_ref, bf16[1024,2048]{1,0:T(8,128)(2,1)} %get-tuple-element.49.g_ref, bf16[256,2048]{1,0:T(8,128)(2,1)} %copy-done.2, bf16[16,2048]{1,0:T(8,128)(2,1)} %copy-done.5, ...), custom_call_target="tpu_custom_call" | custom-call | tf_op jit(solution)/shard_map/attend_back/pallas_call | solution.py:755
  411.1 10.1 %small_gather.3 = f32[8,2,1024]{2,1,0:T(2,128)} custom-call(f32[2,1024]{1,0:T(2,128)} %get-tuple-element.58.x_ref), custom_call_target="tpu_custom_call" | custom-call | tf_op jit(solution)/shard_map/small_gather/pallas_call | solution.py:341
  421.1 0.9 reduce_sum.28
  422.0 1.0 copy.50
  423.1 18.8 %inputs_back.1 = (bf16[1152,2048]{1,0:T(8,128)(2,1)}, f32[48,256]{1,0:T(8,128)}) custom-call(f32[1024,512]{1,0:T(8,128)} %get-tuple-element.56.scaled_ref, bf16[1024,256]{1,0:T(8,128)(2,1)} %get-tuple-element.57.dv_ref, f32[1024,768]{1,0:T(8,128)} %get-tuple-element.35.proj_ref, f32[1024,2]{1,0:T(8,128)} %bitcast.73, f32[1024,2]{1,0:T(8,128)} %bitcast.74, ...), custom_call_target="tpu_custom_call" | custom-call | tf_op jit(solution)/shard_map/inputs_back/pallas_call | solution.py:834
  441.9 46.5 %line_reduce.1 = f32[1152,256]{1,0:T(8,128)} custom-call(bf16[1152,2048]{1,0:T(8,128)(2,1)} %get-tuple-element.62.refs_0_), custom_call_target="tpu_custom_call" | custom-call | tf_op jit(solution)/shard_map/line_reduce/pallas_call | solution.py:296
  488.5 0.9 fusion.9
  489.5 9.2 %all_gather.12 = bf16[4,168,256]{2,1,0:T(8,128)(2,1)S(1)} all-gather(bf16[1,168,256]{2,1,0:T(8,128)(2,1)S(1)} %maximum_maximum_fusion), channel_id=1, replica_groups=mesh['row'=4,'col'=8] {'row'}, dimensions={0}, use_global_device_ids=true | all-gather | bytes 430080 | tf_op jit(solution)/shard_map/all_gather | solution.py:1162
  500.4 1.0 copy.53
  502.2 1.7 fusion.16
  504.6 2.7 multiply_subtract_fusion
  (70 shorter events, 10.2 us)
Async XLA Ops:
  7.2 2.2 copy-start
  7.2 237.2 %all-gather.3.cloned.1.call-start = ((), (), s32[]{:S(2)}) async-start(), calls=%async_computation.1 | async-start | bytes 10485760 | tf_op jit(solution)/shard_map/all_gather | solution.py:1024
  7.9 238.0 %all-gather.5.cloned.1.call-start = ((), (), s32[]{:S(2)}) async-start(), calls=%async_computation.2 | async-start | bytes 10485760 | tf_op jit(solution)/shard_map/all_gather | solution.py:1025
  8.7 498.6 %reduce-scatter.2.cloned.1.call-start = ((), (), s32[]{:S(2)}) async-start(), calls=%async_computation.3 | async-start | bytes 4718592 | tf_op jit(solution)/shard_map/reduce_scatter | solution.py:1105
  10.1 39.7 %copy-start.11 = (pred[48]{0:T(512)(128)(4,1)S(1)}, pred[48]{0:T(512)(128)(4,1)}, u32[]{:S(2)}) copy-start(pred[48]{0:T(512)(128)(4,1)} %constant.19.clone.1) | copy-start | bytes 148
  50.5 30.4 %copy-start.6 = (bf16[2048,16]{0,1:T(8,128)(2,1)S(1)}, bf16[2048,16]{0,1:T(8,128)(2,1)}, u32[]{:S(2)}) copy-start(bf16[2048,16]{0,1:T(8,128)(2,1)} %param.30) | copy-start | bytes 196612
  50.5 31.2 %copy-start.8 = (s32[1024,8]{0,1:T(8,128)S(1)}, s32[1024,8]{0,1:T(8,128)}, u32[]{:S(2)}) copy-start(s32[1024,8]{0,1:T(8,128)} %param.37) | copy-start | bytes 98308
  65.3 18.3 %copy-start.4 = (bf16[256,2048]{1,0:T(8,128)(2,1)S(1)}, bf16[256,2048]{1,0:T(8,128)(2,1)}, u32[]{:S(2)}) copy-start(bf16[256,2048]{1,0:T(8,128)(2,1)} %param.29) | copy-start | bytes 3145732
  83.6 2.8 copy-start.5
  84.1 6.3 %copy-start.2 = (bf16[256,2048]{1,0:T(8,128)(2,1)}, bf16[256,2048]{1,0:T(8,128)(2,1)S(1)}, u32[]{:S(2)}) copy-start(bf16[256,2048]{1,0:T(8,128)(2,1)S(1)} %fusion.map_ref) | copy-start | bytes 3145732
  441.8 46.6 %copy-start.9 = (f32[16,256]{1,0:T(8,128)S(1)}, f32[16,256]{1,0:T(8,128)}, u32[]{:S(2)}) copy-start(f32[16,256]{1,0:T(8,128)} %get-tuple-element.63) | copy-start | bytes 49156
  441.9 46.6 %copy-start.7 = (f32[48,256]{1,0:T(8,128)S(1)}, f32[48,256]{1,0:T(8,128)}, u32[]{:S(2)}) copy-start(f32[48,256]{1,0:T(8,128)} %get-tuple-element.64) | copy-start | bytes 147460
  498.7 5.9 %copy-start.3 = (bf16[1024,256]{1,0:T(8,128)(2,1)S(1)}, bf16[1024,256]{1,0:T(8,128)(2,1)}, u32[]{:S(2)}) copy-start(bf16[1024,256]{1,0:T(8,128)(2,1)} %x_ref.1) | copy-start | bytes 1572868
  501.5 5.8 %copy-start.1 = (bf16[5,8,2048,16]{2,3,1,0:T(8,128)(2,1)S(1)}, bf16[5,8,2048,16]{2,3,1,0:T(8,128)(2,1)}, u32[]{:S(2)}) copy-start(bf16[5,8,2048,16]{2,3,1,0:T(8,128)(2,1)} %param.34) | copy-start | bytes 7864324
  503.9 0.7 copy-start.10
Sparse Core Ops, SparseCore 0:
  9.8 88.4 all-gather.2
  100.1 145.7 all-gather.4
  394.9 50.9 reduce-scatter.1

commit v4 on v3

--- a/solution.py
+++ b/solution.py
@@ -13,6 +13,7 @@
 VM = pl.BlockSpec(memory_space=pltpu.VMEM)
 ANY = pl.BlockSpec(memory_space=pl.ANY)
 VMEM_LIMIT = 60 * 1024 * 1024
+VMEM_MOST = 63 * 1024 * 1024
 
 norm_eps = 1e-05
 rope_base = 10000.0
@@ -845,120 +846,256 @@
     )(*operands)
 
 
-def moe_body(experts, tile, count, x_ref, g_ref, routes_ref, hidden_ref, gate_w, up_w, *refs):
-    downs = refs[:count]
-    out_ref, dx_ref, out_acc, dx_acc, gate_acc, wgu, wd, sems = refs[count:]
+def moments(chips, subs):
+    when = {}
+    for j in range(chips):
+        for chip in range(j):
+            own = subs * (chips - j) + 1
+            when[chip, j] = max(own, when[chip - 1, j] + 3) if chip > 0 else own
+        for chip in range(chips - 1, j, -1):
+            own = subs * (chips - chip + j) + 1
+            when[chip, j] = max(own, when[chip + 1, j] + 3) if chip < chips - 1 else own
+    last = chips * subs
+    return {place: min(time, last) for place, time in when.items()}
+
+
+def moe_turn_body(experts, chips, subs, count, x_ref, g_ref, routes_ref, *refs):
+    refs = list(refs)
+
+    def take(number):
+        taken = refs[:number]
+        del refs[:number]
+        return taken
+
+    operands = take(9)
+    gate_w, up_w = take(2)
+    downs = take(count)
+    out_ref, o_ref = take(2)
+    results = take(2)
+    p_ref, out_acc, dx_acc, gate_acc, wgu, wd, x_buf, g_buf = take(8)
+    sums_in, pair_buf, line_buf, sums = take(4)
+    w_sems, tile_sems, right_sem, left_sem, mate_sem, line_recv, mate_recv = take(7)
+    gather_sems = refs
+    here, chip, core, mate = line_place()
+    row = lax.axis_index("row")
     hidden = wd.shape[1]
-    tokens, width = g_ref.shape
+    tokens, width = out_ref.shape
+    own = tokens // (2 * chips)
+    tile = 2 * own
     lanes = gate_acc.shape[1]
     local = gate_w.shape[0]
     pieces = gate_w.shape[2] // hidden
     steps = local * pieces
-    here = lax.axis_index("col")
-    row = lax.axis_index("row")
-
-    def start(step, slot):
-        e, piece = step // pieces, step % pieces
+    each = steps // subs
+
+    def fetches(step, e, piece):
         if count == 1:
             place = piece
+            down = downs[0].at[e, pl.ds(piece * hidden, hidden)]
         else:
             place = 2 * ((row // 2 + piece // 2) % 2) + (row + piece) % 2
+            down = downs[1].at[piece - 1, e] if piece > 0 else downs[0].at[e]
         units = pl.ds(pl.multiple_of(place * hidden, 128), hidden)
-        pltpu.make_async_copy(gate_w.at[e, :, units], wgu.at[slot, :, pl.ds(0, hidden)], sems.at[slot, 0]).start()
-        pltpu.make_async_copy(up_w.at[e, :, units], wgu.at[slot, :, pl.ds(hidden, hidden)], sems.at[slot, 1]).start()
-        if count == 1:
-            pltpu.make_async_copy(downs[0].at[e, units], wd.at[slot], sems.at[slot, 2]).start()
+        return (
+            pltpu.make_async_copy(gate_w.at[e, :, units], wgu.at[step, :, pl.ds(0, hidden)], w_sems.at[step, 0]),
+            pltpu.make_async_copy(up_w.at[e, :, units], wgu.at[step, :, pl.ds(hidden, hidden)], w_sems.at[step, 1]),
+            pltpu.make_async_copy(down, wd.at[step], w_sems.at[step, 2]),
+        )
+
+    def order(s):
+        right = chips - 1 - chip
+        return jnp.where(s < right, chips - 1 - s, jnp.where(s < chips - 1, s - right, chip))
+
+    def tile_rows(s):
+        return pl.ds(pl.multiple_of(order(s) * tile, 8), tile)
+
+    def tiles(s):
+        slot = s % 2
+        return (
+            pltpu.make_async_copy(x_ref.at[tile_rows(s)], x_buf.at[slot], tile_sems.at[slot, 0]),
+            pltpu.make_async_copy(g_ref.at[tile_rows(s)], g_buf.at[slot], tile_sems.at[slot, 1]),
+        )
+
+    for copy in tiles(0):
+        copy.start()
+    for step in range(steps):
+        for copy in fetches(step, step // pieces, step % pieces):
+            copy.start()
+    line_barrier(chips)
+
+    def block(number):
+        return pl.ds(pl.multiple_of(number * own, 8), own)
+
+    def mate_copy(j):
+        return remote(p_ref.at[block(2 * j + 1 - core)], pair_buf.at[j], mate_sem.at[j], mate_recv.at[j], mate)
+
+    def line_copy(j, slot, sem, device):
+        return remote(sums.at[j], line_buf.at[slot], sem.at[j], line_recv.at[slot], device)
+
+    def pair_sum(j):
+        mate_copy(j).wait_recv()
+        return p_ref[block(2 * j + core)].astype(F32) + pair_buf[j].astype(F32)
+
+    def pass_on(at, j):
+        rightward = j > at
+        total = pair_sum(j)
+        if 0 < at < chips - 1:
+            line_copy(j, j, right_sem if rightward else left_sem, mate).wait_recv()
+            total = total + line_buf[j].astype(F32)
+        sums[j] = total.astype(BF16)
+        if rightward:
+            line_copy(j, j, right_sem, here + 2).start()
         else:
-
-            @pl.when(piece == 0)
-            def _():
-                pltpu.make_async_copy(downs[0].at[e], wd.at[slot], sems.at[slot, 2]).start()
-
-            @pl.when(piece > 0)
-            def _():
-                other = lax.max(piece - 1, 0)
-                pltpu.make_async_copy(downs[1].at[other, e], wd.at[slot], sems.at[slot, 2]).start()
-
-    def finish(slot):
-        units = pl.ds(0, hidden)
-        pltpu.make_async_copy(gate_w.at[0, :, units], wgu.at[slot, :, units], sems.at[slot, 0]).wait()
-        pltpu.make_async_copy(up_w.at[0, :, units], wgu.at[slot, :, units], sems.at[slot, 1]).wait()
-        pltpu.make_async_copy(downs[0].at[0, units], wd.at[slot], sems.at[slot, 2]).wait()
-
-    start(0, 0)
-    out_acc[...] = jnp.zeros_like(out_acc)
-    dx_acc[...] = jnp.zeros_like(dx_acc)
-    gate_acc[...] = jnp.zeros_like(gate_acc)
-    own = hidden_ref.shape[0]
-    out_acc[pl.ds(pl.multiple_of(here * own, 8), own)] = hidden_ref[...]
-
-    def one_step(step, carry):
-        slot = step % 2
-        finish(slot)
-
-        @pl.when(step + 1 < steps)
+            line_copy(j, chips if at - j == 1 else j, left_sem, here - 2).start()
+
+    when = moments(chips, subs)
+
+    def one_sub(k, carry):
+        s, sub = k // subs, k % subs
+        slot = s % 2
+        rows = tile_rows(s)
+
+        @pl.when(sub == 0)
         def _():
-            start(step + 1, 1 - slot)
-
-        e = here * local + step // pieces
-
-        def one_tile(t, carry):
-            rows = pl.ds(pl.multiple_of(t * tile, tile), tile)
+            for copy in tiles(s):
+                copy.wait()
+
+            @pl.when(s + 1 < chips)
+            def _():
+                for copy in tiles(s + 1):
+                    copy.start()
+
+            out_acc[...] = jnp.zeros_like(out_acc)
+            dx_acc[...] = jnp.zeros_like(dx_acc)
+            gate_acc[...] = jnp.zeros_like(gate_acc)
+
+        def one_step(step, carry):
+            @pl.when(s == 0)
+            def _():
+                units = pl.ds(0, hidden)
+                for number, (source, place) in enumerate(((gate_w, 0), (up_w, hidden))):
+                    pltpu.make_async_copy(
+                        source.at[0, :, units], wgu.at[step, :, pl.ds(place, hidden)], w_sems.at[step, number]
+                    ).wait()
+                pltpu.make_async_copy(downs[0].at[0, units], wd.at[step], w_sems.at[step, 2]).wait()
+
+            e = here * local + step // pieces
             lane = lax.broadcasted_iota(jnp.int32, (tile, lanes), 1)
             mine = lane == e
             halves = jnp.logical_or(mine, lane == e + experts)
             named = jnp.sum(jnp.where(routes_ref[rows] == e, 1.0, 0.0), axis=1, keepdims=True)
-            gate = jnp.sum(jnp.where(halves, x_ref[rows, width:].astype(F32), 0.0), axis=1, keepdims=True)
+            gate = jnp.sum(jnp.where(halves, x_buf[slot, :, width:].astype(F32), 0.0), axis=1, keepdims=True)
             gate = gate * named
-            both = nn(x_ref[rows, :width], wgu[slot])
+            both = nn(x_buf[slot, :, :width], wgu[step])
             gate_in, up_in = both[:, :hidden], both[:, hidden:]
             sigmoid = jax.nn.sigmoid(gate_in)
             silu = gate_in * sigmoid
             active = silu * up_in
-            back = nt(g_ref[rows], wd[slot])
+            back = nt(g_buf[slot], wd[step])
             d_gate = jnp.sum(active * back, axis=1, keepdims=True) * named
-            gate_acc[rows] += jnp.where(mine, d_gate, 0.0)
-            out_acc[rows] += nn((active * gate).astype(BF16), wd[slot])
+            gate_acc[...] += jnp.where(mine, d_gate, 0.0)
+            out_acc[...] += nn((active * gate).astype(BF16), wd[step])
             d_active = back * gate
             d_gate_in = d_active * up_in * (sigmoid + silu * (1.0 - sigmoid))
             d_up_in = d_active * silu
             d_both = jnp.concatenate([d_gate_in.astype(BF16), d_up_in.astype(BF16)], axis=1)
-            dx_acc[rows] += nt(d_both, wgu[slot])
+            dx_acc[...] += nt(d_both, wgu[step])
             return carry
 
-        return lax.fori_loop(0, tokens // tile, one_tile, carry)
-
-    lax.fori_loop(0, steps, one_step, 0)
-    out_ref[...] = out_acc[...].astype(BF16)
-    dx_ref[:, :width] = dx_acc[...].astype(BF16)
-    high = gate_acc[...].astype(BF16).astype(F32)
-    rest = gate_acc[...] - high
-    dx_ref[:, width:] = (high + pltpu.roll(rest, experts, 1)).astype(BF16)
-
-
-def moe(x, g, routes, hidden_rows, experts, gate_w, up_w, downs, tile=512):
+        lax.fori_loop(sub * each, (sub + 1) * each, one_step, 0)
+
+        @pl.when(sub == subs - 1)
+        def _():
+            out_ref[rows] = out_acc[...].astype(BF16)
+            p_ref[rows, :width] = dx_acc[...].astype(BF16)
+            high = gate_acc[...].astype(BF16).astype(F32)
+            rest = gate_acc[...] - high
+            p_ref[rows, width:] = (high + pltpu.roll(rest, experts, 1)).astype(BF16)
+            mate_copy(order(s)).start()
+
+            @pl.when(s == chips - 1)
+            def _():
+                out_ref[block(here)] = (out_acc[pl.ds(pl.multiple_of(core * own, 8), own)] + operands[1][...]).astype(BF16)
+
+        for (at, j), time in sorted(when.items(), key=lambda item: (item[1], abs(item[0][0] - item[0][1]))):
+
+            @pl.when(jnp.logical_and(chip == at, k == time - 1))
+            def _():
+                pass_on(at, j)
+
+        return carry
+
+    lax.fori_loop(0, chips * subs, one_sub, 0)
+    sums_in[...] = pair_sum(chip)
+
+    @pl.when(chip > 0)
+    def _():
+        line_copy(chip, chip, right_sem, mate).wait_recv()
+        sums_in[...] += line_buf[chip].astype(F32)
+
+    @pl.when(chip < chips - 1)
+    def _():
+        line_copy(chip, chips, left_sem, mate).wait_recv()
+        sums_in[...] += line_buf[chips].astype(F32)
+
+    for j in range(chips):
+        mate_copy(j).wait_send()
+
+        @pl.when(j > chip)
+        def _():
+            line_copy(j, j, right_sem, mate).wait_send()
+
+        @pl.when(j < chip)
+        def _():
+            line_copy(j, j, left_sem, mate).wait_send()
+
+    kept = turn_backward(width, experts, sums_in, operands, results, o_ref, block(here))
+    gather_rows(chips, 2, o_ref, *gather_sems, lambda: turn_late(kept, operands, results))
+
+
+def moe_turn(x, g, routes, operands, experts, gate_w, up_w, downs, results, chips, ident):
     tokens, width = g.shape
-    lanes = x.shape[1] - width
-    hidden = downs[0].shape[1] if len(downs) > 1 else min(256, gate_w.shape[2])
+    wide = x.shape[1]
+    lanes = wide - width
+    own = tokens // (2 * chips)
+    hidden = downs[0].shape[1] if len(downs) > 1 else min(256, gate_w.shape[2] // 4)
+    steps = gate_w.shape[0] * gate_w.shape[2] // hidden
+    subs = min(4, steps)
+    whole = jax.ShapeDtypeStruct((tokens, width), BF16)
+    per_chip = pltpu.SemaphoreType.DMA((chips,))
+    halves = pltpu.SemaphoreType.DMA((chips, 2))
     return pl.pallas_call(
-        functools.partial(moe_body, experts, min(tile, tokens), len(downs)),
-        out_shape=(
-            jax.ShapeDtypeStruct((tokens, width), BF16),
-            jax.ShapeDtypeStruct((tokens, width + lanes), BF16),
+        functools.partial(moe_turn_body, experts, chips, subs, len(downs)),
+        out_shape=(whole, whole) + tuple(results),
+        in_specs=[ANY, ANY] + [VM] * (1 + len(operands)) + [ANY] * (2 + len(downs)),
+        out_specs=(VM,) * (2 + len(results)),
+        scratch_shapes=[
+            pltpu.VMEM((tokens, wide), BF16),
+            pltpu.VMEM((2 * own, width), F32),
+            pltpu.VMEM((2 * own, width), F32),
+            pltpu.VMEM((2 * own, lanes), F32),
+            pltpu.VMEM((steps, width, 2 * hidden), BF16),
+            pltpu.VMEM((steps, hidden, width), BF16),
+            pltpu.VMEM((2, 2 * own, wide), BF16),
+            pltpu.VMEM((2, 2 * own, width), BF16),
+            pltpu.VMEM((own, wide), F32),
+            pltpu.VMEM((chips, own, wide), BF16),
+            pltpu.VMEM((chips + 1, own, wide), BF16),
+            pltpu.VMEM((chips, own, wide), BF16),
+            pltpu.SemaphoreType.DMA((steps, 3)),
+            pltpu.SemaphoreType.DMA((2, 2)),
+            per_chip,
+            per_chip,
+            per_chip,
+            pltpu.SemaphoreType.DMA((chips + 1,)),
+            per_chip,
+        ]
+        + [halves] * 5,
+        compiler_params=pltpu.CompilerParams(
+            collective_id=ident, has_side_effects=True, vmem_limit_bytes=VMEM_MOST
         ),
-        in_specs=[VM] * 4 + [ANY] * (2 + len(downs)),
-        out_specs=(VM, VM),
-        scratch_shapes=[
-            pltpu.VMEM((tokens, width), F32),
-            pltpu.VMEM((tokens, width), F32),
-            pltpu.VMEM((tokens, lanes), F32),
-            pltpu.VMEM((2, width, 2 * hidden), BF16),
-            pltpu.VMEM((2, hidden, width), BF16),
-            pltpu.SemaphoreType.DMA((2, 3)),
-        ],
-        compiler_params=pltpu.CompilerParams(vmem_limit_bytes=VMEM_LIMIT),
-        name="moe",
-    )(x, g, routes, hidden_rows, gate_w, up_w, *downs)
+        name="moe_turn",
+    )(x, g, routes, *operands, gate_w, up_w, *downs)
 
 
 def rope_tables(length, head_dim):
@@ -1080,9 +1217,10 @@
     else:
         downs = (lax.all_gather(w_down, "row", axis=1, tiled=True),)
 
-    moe_out, back_out = moe(normed_two, full_cot, routes, hidden_rows, expert_total, full_gate, full_up, downs)
-    grad_attn, late, router_late = line_turn(
-        back_out,
+    moe_out, grad_attn, late, router_late = moe_turn(
+        normed_two,
+        full_cot,
+        routes,
         (
             held_rows(full_cot),
             hidden_rows,
@@ -1094,10 +1232,11 @@
             mid_router,
             mid_out,
         ),
-        full_width,
+        expert_total,
+        full_gate,
+        full_up,
+        downs,
         (row_shape((2 * rank, full_width), F32), row_shape((rank, lanes), F32)),
-        functools.partial(turn_backward, full_width, expert_total),
-        turn_late,
         chips,
         7,
     )

time: 521 us -> 488 us (0.937)
  Pallas kernels: 453 us -> 424 us
    pallas_call x2 -> x1, Pallas kernels: 220 us -> 139 us  [line_turn(): pl.pallas_call(functools.partial(turn_body, chips, parts, first, last, le...]
    pallas_call x1, Pallas kernels: 67.4 us -> 120 us  [moe_turn(): pl.pallas_call(functools.partial(moe_turn_body, experts, chips, subs, len...]
  transfers between devices with their start and end apart: 3 -> 3, of which waited for: 1 -> 1; matrix products, arithmetic and copies ran while one was open for 6% -> 6% of each run, Pallas kernels for 59% -> 63%
where the time goes in v4:
time: 488 us; the launch traced here: 481 us
  Pallas kernels  424 us (87%)
  local copies, waits for them, and re-layouts  19.4 us (4%)
  between operations  15.8 us (3%)
  other arithmetic  10.1 us (2%)
  blocking collectives  8.57 us (2%)
    pallas_call x1, Pallas kernels, line_turn(): pl.pallas_call(functools.partial(turn_body, chips, parts, first, last, le...  139 us
    pallas_call x1, Pallas kernels, moe_turn(): pl.pallas_call(functools.partial(moe_turn_body, experts, chips, subs, len...  120 us
    pallas_call x1, Pallas kernels, line_reduce(): pl.pallas_call(functools.partial(reduce_body, chips, parts, axis), out_sh...  46.5 us
    pallas_call x1, Pallas kernels, line_gather(): pl.pallas_call(functools.partial(gather_body, chips, parts, axis), out_sh...  38.7 us
    pallas_call x2, Pallas kernels, small_gather(): pl.pallas_call(functools.partial(small_body, count), out_shape=jax.ShapeD...  19.4 us
    pallas_call x1, Pallas kernels, inputs_back(): pl.pallas_call(functools.partial(inputs_back_body, min(256, seq_len), ext...  18.8 us
    pallas_call x1, Pallas kernels, attend_back(): pl.pallas_call(functools.partial(attend_back_body, min(256, seq_len), rea...  15.2 us
    pallas_call x1, Pallas kernels, project(): pl.pallas_call(functools.partial(project_body, min(256, seq_len)), out_sh...  14.8 us
  transfers between devices with their start and end apart: 3, of which 1 were waited for; matrix products, arithmetic and copies ran while one was open for 6% of the time, Pallas kernels for 63%

profile of v4, /device:TPU:16, one launch (start us, length us, event | category | flops | bytes accessed | tf_op | source)
XLA Modules:
  0.0 481.3 jit_solution(11558705473021743028)
XLA Ops:
  8.0 0.7 all-gather.5.cloned.1.call-update
  9.4 1.0 dynamic-slice_bitcast_fusion
  11.1 38.7 %line_gather.1.x_ref = bf16[1024,2048]{1,0:T(8,128)(2,1)} custom-call(bf16[1024,256]{1,0:T(8,128)(2,1)} %x_ref.1), custom_call_target="tpu_custom_call" | custom-call | tf_op jit(solution)/shard_map/line_gather/pallas_call | solution.py:172
  49.8 1.0 constant_dynamic-slice_fusion
  51.5 14.8 %project.1 = (f32[1024,768]{1,0:T(8,128)}, bf16[1024,48]{1,0:T(8,128)(2,1)}, f32[1024,1]{1,0:T(8,128)}, f32[2,1024]{1,0:T(2,128)}) custom-call(bf16[1024,2048]{1,0:T(8,128)(2,1)} %line_gather.1.x_ref, f32[1,2048]{1,0:T(1,128)} %bitcast.81, bf16[2048,256]{1,0:T(8,128)(2,1)} %wq.3, bf16[2048,256]{1,0:T(8,128)(2,1)} %wk.3, bf16[2048,256]{1,0:T(8,128)(2,1)} %wv.3, ...), custom_call_target="tpu_custom_call" | custom-call | tf_op jit(solution)/shard_map/project/pallas_call | solution.py:629
  66.2 9.4 %small_gather.2 = f32[8,2,1024]{2,1,0:T(2,128)} custom-call(f32[2,1024]{1,0:T(2,128)} %get-tuple-element.35.x_ref), custom_call_target="tpu_custom_call" | custom-call | tf_op jit(solution)/shard_map/small_gather/pallas_call | solution.py:342
  75.6 0.9 reduce_sum.27
  76.5 1.1 copy.47
  78.4 0.8 dynamic_slice.41
  79.1 0.8 dynamic_slice.42
  81.2 0.9 pad.10.refs_4_
  82.1 1.0 copy.49.routes_ref
  83.1 0.8 dynamic-slice_bitcast_fusion.1.b_ref
  84.4 2.3 concatenate.44.map_ref
  87.3 2.0 fusion.6
  89.3 1.3 pad_maximum_fusion
  90.6 11.8 %attend.1 = (bf16[1024,2176]{1,0:T(8,128)(2,1)}, bf16[1024,256]{1,0:T(8,128)(2,1)}, bf16[1024,256]{1,0:T(8,128)(2,1)}, bf16[1024,256]{1,0:T(8,128)(2,1)}, bf16[1024,256]{1,0:T(8,128)(2,1)}, /*index=5*/f32[1024,2]{1,0:T(8,128)}) custom-call(s32[1]{0:T(128)S(6)} %copy.58.prefix_ref, f32[1024,768]{1,0:T(8,128)} %get-tuple-element.34.proj_ref, ...), custom_call_target="tpu_custom_call" | custom-call | tf_op jit(solution)/shard_map/attend/pallas_call | solution.py:687
  102.3 1.9 constant_dynamic-slice_fusion.2.refs_1_
  104.2 138.9 %line_turn.1 = (bf16[1024,2176]{1,0:T(8,128)(2,1)}, f32[128,2048]{1,0:T(8,128)}, bf16[128,128]{1,0:T(8,128)(2,1)}, bf16[128,16]{1,0:T(8,128)(2,1)}, f32[128,128]...) custom-call(bf16[1024,2176]{1,0:T(8,128)(2,1)} %get-tuple-element.36.refs_0_, ...), custom_call_target="tpu_custom_call" | custom-call | tf_op jit(solution)/shard_map/line_turn/pallas_call | solution.py:513
  243.2 1.9 constant_dynamic-slice_fusion.1.refs_0_
  245.1 1.2 all-gather.5.cloned.1.call-done.refs_10_
  246.3 120.0 %moe_turn.1 = (bf16[1024,2048]{1,0:T(8,128)(2,1)}, bf16[1024,2048]{1,0:T(8,128)(2,1)}, f32[32,2048]{1,0:T(8,128)}, f32[16,128]{1,0:T(8,128)}) custom-call(bf16[1024,2176]{1,0:T(8,128)(2,1)} %get-tuple-element.37.x_ref, bf16[1024,2048]{1,0:T(8,128)(2,1)} %get-tuple-element.38.g_ref, s32[1024,8]{1,0:T(8,128)} %copy.49.routes_ref, ...), custom_call_target="tpu_custom_call" | custom-call | tf_op jit(solution)/shard_map/moe_turn/pallas_call | solution.py:1067
  366.3 0.8 dynamic_slice.49
  367.2 15.2 %attend_back.1 = (f32[1024,512]{1,0:T(8,128)}, bf16[1024,256]{1,0:T(8,128)(2,1)}, f32[2,1024]{1,0:T(2,128)}, f32[16,256]{1,0:T(8,128)}) custom-call(s32[1]{0:T(128)S(6)} %copy.58.prefix_ref, bf16[1024,2048]{1,0:T(8,128)(2,1)} %get-tuple-element.47.g_ref, bf16[256,2048]{1,0:T(8,128)(2,1)} %copy-done.2, bf16[16,2048]{1,0:T(8,128)(2,1)} %copy-done.7, ...), custom_call_target="tpu_custom_call" | custom-call | tf_op jit(solution)/shard_map/attend_back/pallas_call | solution.py:756
  382.4 10.1 %small_gather.3 = f32[8,2,1024]{2,1,0:T(2,128)} custom-call(f32[2,1024]{1,0:T(2,128)} %get-tuple-element.56.x_ref), custom_call_target="tpu_custom_call" | custom-call | tf_op jit(solution)/shard_map/small_gather/pallas_call | solution.py:342
  392.5 0.9 reduce_sum.28
  393.4 1.0 copy.50
  394.4 18.8 %inputs_back.1 = (bf16[1152,2048]{1,0:T(8,128)(2,1)}, f32[48,256]{1,0:T(8,128)}) custom-call(f32[1024,512]{1,0:T(8,128)} %get-tuple-element.54.scaled_ref, bf16[1024,256]{1,0:T(8,128)(2,1)} %get-tuple-element.55.dv_ref, f32[1024,768]{1,0:T(8,128)} %get-tuple-element.34.proj_ref, f32[1024,2]{1,0:T(8,128)} %bitcast.73, f32[1024,2]{1,0:T(8,128)} %bitcast.74, ...), custom_call_target="tpu_custom_call" | custom-call | tf_op jit(solution)/shard_map/inputs_back/pallas_call | solution.py:835
  413.2 46.5 %line_reduce.1 = f32[1152,256]{1,0:T(8,128)} custom-call(bf16[1152,2048]{1,0:T(8,128)(2,1)} %get-tuple-element.60.refs_0_), custom_call_target="tpu_custom_call" | custom-call | tf_op jit(solution)/shard_map/line_reduce/pallas_call | solution.py:297
  459.8 1.0 fusion.9
  460.9 8.6 %all_gather.12 = bf16[4,168,256]{2,1,0:T(8,128)(2,1)S(1)} all-gather(bf16[1,168,256]{2,1,0:T(8,128)(2,1)S(1)} %maximum_maximum_fusion), channel_id=1, replica_groups=mesh['row'=4,'col'=8] {'row'}, dimensions={0}, use_global_device_ids=true | all-gather | bytes 430080 | tf_op jit(solution)/shard_map/all_gather | solution.py:1301
  471.9 2.4 multiply_subtract_fusion
  (73 shorter events, 7.2 us)
Async XLA Ops:
  7.2 73.4 %copy-start = (bf16[8,16,16]{2,1,0:T(8,128)(2,1)S(1)}, bf16[8,16,16]{2,1,0:T(8,128)(2,1)}, u32[]{:S(2)}) copy-start(bf16[8,16,16]{2,1,0:T(8,128)(2,1)} %param.36) | copy-start | bytes 12292
  7.2 237.9 %all-gather.3.cloned.1.call-start = ((), (), s32[]{:S(2)}) async-start(), calls=%async_computation.1 | async-start | bytes 10485760 | tf_op jit(solution)/shard_map/all_gather | solution.py:1161
  7.9 238.3 %all-gather.5.cloned.1.call-start = ((), (), s32[]{:S(2)}) async-start(), calls=%async_computation.2 | async-start | bytes 10485760 | tf_op jit(solution)/shard_map/all_gather | solution.py:1162
  8.7 465.6 %reduce-scatter.2.cloned.1.call-start = ((), (), s32[]{:S(2)}) async-start(), calls=%async_computation.3 | async-start | bytes 4718592 | tf_op jit(solution)/shard_map/reduce_scatter | solution.py:1244
  11.1 39.7 %copy-start.13 = (pred[48]{0:T(512)(128)(4,1)S(1)}, pred[48]{0:T(512)(128)(4,1)}, u32[]{:S(2)}) copy-start(pred[48]{0:T(512)(128)(4,1)} %constant.19.clone.1) | copy-start | bytes 148
  51.5 29.7 %copy-start.8 = (bf16[2048,16]{0,1:T(8,128)(2,1)S(1)}, bf16[2048,16]{0,1:T(8,128)(2,1)}, u32[]{:S(2)}) copy-start(bf16[2048,16]{0,1:T(8,128)(2,1)} %param.30) | copy-start | bytes 196612
  51.5 30.6 %copy-start.10 = (s32[1024,8]{0,1:T(8,128)S(1)}, s32[1024,8]{0,1:T(8,128)}, u32[]{:S(2)}) copy-start(s32[1024,8]{0,1:T(8,128)} %param.37) | copy-start | bytes 98308
  66.2 17.7 %copy-start.6 = (bf16[256,2048]{1,0:T(8,128)(2,1)S(1)}, bf16[256,2048]{1,0:T(8,128)(2,1)}, u32[]{:S(2)}) copy-start(bf16[256,2048]{1,0:T(8,128)(2,1)} %param.29) | copy-start | bytes 3145732
  83.9 2.8 copy-start.7
  84.4 6.2 %copy-start.2 = (bf16[256,2048]{1,0:T(8,128)(2,1)}, bf16[256,2048]{1,0:T(8,128)(2,1)S(1)}, u32[]{:S(2)}) copy-start(bf16[256,2048]{1,0:T(8,128)(2,1)S(1)} %fusion.map_ref) | copy-start | bytes 3145732
  413.2 46.6 %copy-start.11 = (f32[16,256]{1,0:T(8,128)S(1)}, f32[16,256]{1,0:T(8,128)}, u32[]{:S(2)}) copy-start(f32[16,256]{1,0:T(8,128)} %get-tuple-element.61) | copy-start | bytes 49156
  413.2 46.6 %copy-start.9 = (f32[48,256]{1,0:T(8,128)S(1)}, f32[48,256]{1,0:T(8,128)}, u32[]{:S(2)}) copy-start(f32[48,256]{1,0:T(8,128)} %get-tuple-element.62) | copy-start | bytes 147460
  459.7 10.8 %copy-start.3 = (f32[1152,256]{1,0:T(8,128)S(1)}, f32[1152,256]{1,0:T(8,128)}, u32[]{:S(2)}) copy-start(f32[1152,256]{1,0:T(8,128)} %line_reduce.1) | copy-start | bytes 3538948
  459.7 11.7 %copy-start.5 = (f32[1024,1]{1,0:T(8,128)S(1)}, f32[1024,1]{1,0:T(8,128)}, u32[]{:S(2)}) copy-start(f32[1024,1]{1,0:T(8,128)} %get-tuple-element.48.inv1_ref) | copy-start | bytes 12292
  469.5 2.4 copy-start.4
  470.8 3.5 copy-start.1
  471.8 2.4 copy-start.12
Sparse Core Ops, SparseCore 0:
  9.8 88.4 all-gather.2
  100.1 146.1 all-gather.4
  366.4 51.0 reduce-scatter.1

commit v5 on v4

--- a/solution.py
+++ b/solution.py
@@ -92,9 +92,14 @@
                 steps.remove(one)
 
 
-def gather_body(chips, parts, axis, x_ref, o_ref, *sems):
-    line_barrier(chips)
-    run(gather_steps(chips, parts, axis, x_ref, o_ref, *sems))
+def gather_body(chips, parts, axis, riders, x_ref, *refs):
+    line_barrier(chips, row_partners() if riders else ())
+    o_ref = refs[riders]
+    sems = refs[2 * riders + 1 :]
+    steps = [gather_steps(chips, parts, axis, x_ref, o_ref, *sems[:6])]
+    if riders:
+        steps.append(row_gather_steps(2, refs[0], refs[2], *sems[6:]))
+    run(*steps)
 
 
 def gather_steps(chips, parts, axis, x_ref, o_ref, right_sem, left_sem, mate_sem, line_recv, mate_recv, own_sem):
@@ -165,26 +170,26 @@
                 copy(j, part, left_sem, line_recv, here - 2).wait_send()
 
 
-def line_gather(x, chips, axis, ident, parts=2):
+def line_gather(x, chips, axis, ident, parts=2, rider=None):
     rows, cols = x.shape
     sems = pltpu.SemaphoreType.DMA((chips, parts))
     shape = (2 * chips * rows, cols) if axis == 0 else (rows, 2 * chips * cols)
+    whole = jax.ShapeDtypeStruct(shape, x.dtype)
+    more = () if rider is None else (rider,)
+    ridden = tuple(jax.ShapeDtypeStruct((3,) + one.shape, one.dtype) for one in more)
     return pl.pallas_call(
-        functools.partial(gather_body, chips, parts, axis),
-        out_shape=jax.ShapeDtypeStruct(shape, x.dtype),
-        in_specs=[VM],
-        out_specs=VM,
-        scratch_shapes=[sems] * 5 + [pltpu.SemaphoreType.DMA((parts,))],
+        functools.partial(gather_body, chips, parts, axis, len(more)),
+        out_shape=(whole,) + ridden,
+        in_specs=[VM] + [ANY] * len(more),
+        out_specs=(VM,) + (ANY,) * len(more),
+        scratch_shapes=[sems] * 5
+        + [pltpu.SemaphoreType.DMA((parts,))]
+        + [pltpu.SemaphoreType.DMA((6,))] * (2 * len(more)),
         compiler_params=pltpu.CompilerParams(
             collective_id=ident, has_side_effects=True, vmem_limit_bytes=VMEM_LIMIT
         ),
         name="line_gather",
-    )(x)
-
-
-def reduce_body(chips, parts, axis, *refs):
-    line_barrier(chips)
-    run(reduce_steps(chips, parts, axis, *refs))
+    )(x, *more)
 
 
 def reduce_steps(
@@ -285,35 +290,6 @@
             @pl.when(j < chip)
             def _():
                 line_copy(j, j, part, left_sem, mate).wait_send()
-
-
-def line_reduce(p, chips, axis, ident, parts=2):
-    rows, cols = p.shape
-    if axis == 0:
-        rows //= 2 * chips
-    else:
-        cols //= 2 * chips
-    sems = pltpu.SemaphoreType.DMA((chips, parts))
-    return pl.pallas_call(
-        functools.partial(reduce_body, chips, parts, axis),
-        out_shape=jax.ShapeDtypeStruct((rows, cols), F32),
-        in_specs=[VM],
-        out_specs=VM,
-        scratch_shapes=[
-            pltpu.VMEM((chips, rows, cols), BF16),
-            pltpu.VMEM((chips + 1, rows, cols), BF16),
-            pltpu.VMEM((chips, rows, cols), BF16),
-            sems,
-            sems,
-            sems,
-            pltpu.SemaphoreType.DMA((chips + 1, parts)),
-            sems,
-        ],
-        compiler_params=pltpu.CompilerParams(
-            collective_id=ident, has_side_effects=True, vmem_limit_bytes=VMEM_LIMIT
-        ),
-        name="line_reduce",
-    )(p)
 
 
 def small_body(count, x_ref, o_ref, send_sem, recv_sem):
@@ -367,7 +343,7 @@
     return 2 * major + 1 - minor, 2 * (1 - major) + minor
 
 
-def row_gather_steps(x_ref, o_ref, *sems):
+def row_gather_steps(pauses, x_ref, o_ref, *sems):
     near, next_one = row_partners()
     half = x_ref.shape[0] // 2
 
@@ -385,10 +361,8 @@
     side(1, 1).start()
     side(0, 1).start()
     side(1, 0).start()
-    yield
-    yield
-    yield
-    yield
+    for _ in range(pauses):
+        yield
     side(0, 0).wait_recv()
     onward(0).start()
     side(1, 1).wait_recv()
@@ -424,7 +398,7 @@
     if riders > 0:
         steps.append(gather_steps(chips, 2, 1, rider_in[0], rider_out[0], *take(6)))
     if riders > 1:
-        across = row_gather_steps(rider_in[1], rider_out[1], *take(2))
+        across = row_gather_steps(1, rider_in[1], rider_out[1], *take(2))
         next(across)
     run(*steps)
     here = lax.axis_index("col")
@@ -433,8 +407,7 @@
 
     def beside():
         if riders > 1:
-            for _ in range(4):
-                next(across)
+            next(across)
         last(kept, operands, results)
 
     gather_rows(chips, parts, o_ref, *gather_sems, beside)
@@ -701,7 +674,7 @@
     )(prefix, proj, inv, gains, *tables, out_map)
 
 
-def attend_back_body(
+def attend_back(
     tile, reach, scale, prefix_ref, g_ref, map_ref, b_ref, att_ref, q_ref, k_ref, v_ref, log_ref, proj_ref,
     gains_ref, cos_ref, sin_ref, scaled_ref, dv_ref, stat_ref, ga_ref, da_ref, dq_acc, dk_acc, dv_acc,
 ):
@@ -750,100 +723,335 @@
             stat_ref[pl.ds(m, 1), rows] = total[0:1]
 
 
-def attend_back(prefix, grads, out_map, b_out, saved, proj, gains, tables, reach, scale):
-    seq_len = proj.shape[0]
-    part = proj.shape[1] // 3
-    return pl.pallas_call(
-        functools.partial(attend_back_body, min(256, seq_len), reach, scale),
-        out_shape=(
-            jax.ShapeDtypeStruct((seq_len, 2 * part), F32),
-            jax.ShapeDtypeStruct((seq_len, part), BF16),
-            jax.ShapeDtypeStruct((2, seq_len), F32),
-            jax.ShapeDtypeStruct((b_out.shape[0], part), F32),
-        ),
-        in_specs=[pl.BlockSpec(memory_space=pltpu.SMEM)] + [VM] * 12,
-        out_specs=(VM,) * 4,
-        scratch_shapes=[pltpu.VMEM((seq_len, part), BF16)] + [pltpu.VMEM((seq_len, part), F32)] * 3,
-        compiler_params=pltpu.CompilerParams(vmem_limit_bytes=VMEM_LIMIT),
-        name="attend_back",
-    )(prefix, grads, out_map, b_out, *saved, proj, gains, *tables)
-
-
-def inputs_back_body(
-    tile, extra, scaled_ref, dv_ref, proj_ref, inv_ref, stat_ref, wq, wk, wv, b_ref, a_ref, x_ref, inv1_ref,
-    gain_ref, mid_ref, late_ref, router_ref, p_ref, gb_ref, w_ref, w_sems,
-):
+def back_body(tile, reach, scale, chips, row_count, extra, prefix_ref, slot_ref, *refs):
+    refs = list(refs)
+
+    def take(number):
+        taken = refs[:number]
+        del refs[:number]
+        return taken
+
+    g_ref, map_ref, bo_ref, att_ref, q_ref, k_ref, v_ref, log_ref, proj_ref, gains_ref, cos_ref, sin_ref = take(12)
+    inv_ref, b_ref, a_ref, x_ref, inv1_ref, gain_ref, mid_ref, late_ref, router_ref = take(9)
+    weights = take(3)
+    gi_ref, held_ref = take(2)
+    scaled_ref, dv_ref, stat_ref, stats_ref, ga_ref, da_ref, dq_acc, dk_acc, dv_acc = take(9)
+    w_ref, d_ref, middle_ref, p_ref, o_ref, pair_buf, line_buf, sums, flat_ref, every_ref = take(10)
+    w_sems, stat_send, stat_recv, row_send, row_recv = take(5)
+    right_sem, left_sem, mate_sem, line_recv, mate_recv = take(5)
+    here, chip, core, mate = line_place()
+    row = lax.axis_index("row")
+    count = 2 * chips
     seq_len, width = x_ref.shape
     part = dv_ref.shape[1]
     ranks = a_ref.shape[0]
     rank = ranks // 3
+    parts = 2
+
     fetches = [
-        pltpu.make_async_copy(w, w_ref.at[:, pl.ds(m * part, part)], w_sems.at[m]) for m, w in enumerate((wq, wk, wv))
+        pltpu.make_async_copy(w, w_ref.at[:, pl.ds(m * part, part)], w_sems.at[m]) for m, w in enumerate(weights)
     ]
     for fetch in fetches:
         fetch.start()
+    barrier = pltpu.get_barrier_semaphore()
+    for hop in range(1, count):
+        other = lax.rem(here + hop, count)
+        pl.semaphore_signal(barrier, inc=1, device_id={"col": other}, device_id_type=MESH_ID)
+    for hop in range(1, row_count):
+        other = lax.rem(row + hop, row_count)
+        pl.semaphore_signal(barrier, inc=1, device_id={"row": other}, device_id_type=MESH_ID)
+    attend_back(
+        tile, reach, scale, prefix_ref, g_ref, map_ref, bo_ref, att_ref, q_ref, k_ref, v_ref, log_ref, proj_ref,
+        gains_ref, cos_ref, sin_ref, scaled_ref, dv_ref, stat_ref, ga_ref, da_ref, dq_acc, dk_acc, dv_acc,
+    )
+    pl.semaphore_wait(barrier, count + row_count - 2)
+
+    def stat_copy(hop, block):
+        other = lax.rem(here + hop, count)
+        return remote(stat_ref, stats_ref.at[block], stat_send.at[hop], stat_recv.at[hop], other)
+
+    for hop in range(1, count):
+        stat_copy(hop, here).start()
+    stats_ref[here] = stat_ref[...]
+    for hop in range(1, count):
+        stat_copy(hop, lax.rem(here + count - hop, count)).wait_recv()
+    total = stats_ref[0]
+    for n in range(1, count):
+        total = total + stats_ref[n]
+    total = jnp.concatenate([total, jnp.zeros((6, seq_len), F32)], axis=0) * (1.0 / width)
+
     grad_b = jnp.zeros((ranks, 3 * part), F32)
-    grad_a = jnp.zeros((ranks, width), F32)
-    stats = jnp.zeros((8, width), F32)
-    line = lax.broadcasted_iota(jnp.int32, (8, width), 0)
+    first_stats = jnp.zeros((8, part), F32)
+    line = lax.broadcasted_iota(jnp.int32, (8, part), 0)
     for t in range(seq_len // tile):
         rows = pl.ds(t * tile, tile)
-        grads = []
-        for m in range(2):
+        upright = jnp.transpose(total[:, t * tile : (t + 1) * tile])
+        products = jnp.zeros((tile, part), F32)
+        for m in range(3):
             cols = pl.ds(m * part, part)
-            inv = inv_ref[rows, m : m + 1]
-            shift = inv * inv * inv * stat_ref[rows, m : m + 1]
-            grads.append((inv * scaled_ref[rows, cols] - proj_ref[rows, cols] * shift).astype(BF16))
-        grads = jnp.concatenate(grads + [dv_ref[rows]], axis=1)
-        middle = nt(grads, b_ref[...]).astype(BF16)
-        if t == 0:
-            for fetch in fetches:
-                fetch.wait()
-        normed_part = nt(grads, w_ref[...]) + nn(middle, a_ref[...])
+            if m < 2:
+                inv = inv_ref[rows, m : m + 1]
+                shift = inv * inv * inv * upright[:, m : m + 1]
+                grad = (inv * scaled_ref[rows, cols] - proj_ref[rows, cols] * shift).astype(BF16)
+            else:
+                grad = dv_ref[rows]
+            d_ref[rows, cols] = grad
+            products += grad.astype(F32) * proj_ref[rows, cols]
+        grads = d_ref[rows]
+        middle_ref[rows] = nt(grads, b_ref[...]).astype(BF16)
         grad_b += tn(mid_ref[rows], grads)
-        p_ref[rows] = normed_part.astype(BF16)
-        scaled_x = x_ref[rows].astype(F32) * gain_ref[...]
-        normed = (scaled_x * inv1_ref[rows]).astype(BF16)
-        grad_a += tn(middle, normed)
-        first = row_sums(scaled_x * normed_part)
+        first = row_sums(products / inv1_ref[rows])
         for j in range(tile // part):
-            wide = jnp.concatenate([first[:, j * part : (j + 1) * part]] * (width // part), axis=1)
-            stats = jnp.where(line == (t * tile) // part + j, wide, stats)
-    for m in range(3):
-        gb_ref[pl.ds(m * rank, rank)] = grad_b[m * rank : (m + 1) * rank, m * part : (m + 1) * part]
-    high = stats.astype(BF16).astype(F32)
+            first_stats = jnp.where(
+                line == (t * tile) // part + j, first[:, j * part : (j + 1) * part], first_stats
+            )
+    high = first_stats.astype(BF16).astype(F32)
     router = router_ref[...]
     if part > router.shape[1]:
         router = jnp.concatenate([router, jnp.zeros((rank, part - router.shape[1]), F32)], axis=1)
-    pieces = [
-        grad_a,
-        late_ref[...],
-        jnp.concatenate([router] * (width // part), axis=1),
-        high,
-        stats - high,
-    ]
-    used = sum(piece.shape[0] for piece in pieces)
-    pieces.append(jnp.zeros((extra - used, width), F32))
-    p_ref[pl.ds(seq_len, extra)] = jnp.concatenate(pieces, axis=0).astype(BF16)
-
-
-def inputs_back(extra, *operands):
-    x = operands[10]
+    common = jnp.concatenate([router, high, first_stats - high], axis=0).astype(BF16)
+    common = jnp.concatenate([common] * count, axis=1)
+    p_ref[pl.ds(ranks, 2 * rank)] = late_ref[...].astype(BF16)
+    p_ref[pl.ds(ranks + 2 * rank, rank + 16)] = common
+    used = ranks + 3 * rank + 16
+    p_ref[pl.ds(used, extra - used)] = jnp.zeros((extra - used, width), BF16)
+    for fetch in fetches:
+        fetch.wait()
+
+    size = o_ref.shape
+    step = size[0] // parts
+
+    def rows_of(piece):
+        return pl.ds(piece * step, step)
+
+    def at(block, piece):
+        return spot(1, size, parts, block, piece)
+
+    def mate_copy(j, piece):
+        return remote(
+            p_ref.at[at(2 * j + 1 - core, piece)],
+            pair_buf.at[j, rows_of(piece)],
+            mate_sem.at[j, piece],
+            mate_recv.at[j, piece],
+            mate,
+        )
+
+    def line_copy(j, slot, piece, sem, device):
+        return remote(
+            sums.at[j, rows_of(piece)],
+            line_buf.at[slot, rows_of(piece)],
+            sem.at[j, piece],
+            line_recv.at[slot, piece],
+            device,
+        )
+
+    def order(s):
+        right = chips - 1 - chip
+        return jnp.where(s < right, chips - 1 - s, jnp.where(s < chips - 1, s - right, chip))
+
+    def work_out(s):
+        cols = pl.ds(pl.multiple_of(order(s) * (2 * part), 128), 2 * part)
+        gain = gain_ref[:, cols]
+        spread = a_ref[:, cols]
+        chunk = w_ref[cols]
+
+        def one_tile(t, grad_a):
+            rows = pl.ds(pl.multiple_of(t * tile, tile), tile)
+            middle = middle_ref[rows]
+            normed_part = nt(d_ref[rows], chunk) + nn(middle, spread)
+            p_ref[pl.ds(pl.multiple_of(extra + t * tile, 16), tile), cols] = normed_part.astype(BF16)
+            normed = (x_ref[rows, cols].astype(F32) * inv1_ref[rows] * gain).astype(BF16)
+            return grad_a + tn(middle, normed)
+
+        grad_a = lax.fori_loop(0, seq_len // tile, one_tile, jnp.zeros((ranks, 2 * part), F32))
+        p_ref[pl.ds(0, ranks), cols] = grad_a.astype(BF16)
+        for piece in range(parts):
+            mate_copy(order(s), piece).start()
+
+    def pair_sum(j, piece):
+        mate_copy(j, piece).wait_recv()
+        return p_ref[at(2 * j + core, piece)].astype(F32) + pair_buf[j, rows_of(piece)].astype(F32)
+
+    def one_block(s, carry):
+        work_out(s)
+
+        @pl.when(jnp.logical_and(chip == 0, s > 0))
+        def _():
+            for piece in range(parts):
+                j = order(s - 1)
+                sums[j, rows_of(piece)] = pair_sum(j, piece).astype(BF16)
+                line_copy(j, j, piece, right_sem, here + 2).start()
+
+        @pl.when(jnp.logical_and(chip == chips - 1, s > 0))
+        def _():
+            for piece in range(parts):
+                j = order(s - 1)
+                sums[j, rows_of(piece)] = pair_sum(j, piece).astype(BF16)
+
+                @pl.when(j == chips - 2)
+                def _():
+                    line_copy(j, chips, piece, left_sem, here - 2).start()
+
+                @pl.when(j < chips - 2)
+                def _():
+                    line_copy(j, j, piece, left_sem, here - 2).start()
+
+        return carry
+
+    lax.fori_loop(0, chips, one_block, 0)
+    inner = jnp.logical_and(chip > 0, chip < chips - 1)
+
+    def pass_on(j, slot, piece, sem, device):
+        line_copy(j, j, piece, sem, mate).wait_recv()
+        sums[j, rows_of(piece)] = (pair_sum(j, piece) + line_buf[j, rows_of(piece)].astype(F32)).astype(BF16)
+        line_copy(j, slot, piece, sem, device).start()
+
+    for far in range(chips - 2, 0, -1):
+        for piece in range(parts):
+
+            @pl.when(jnp.logical_and(inner, chip + far < chips))
+            def _():
+                pass_on(chip + far, chip + far, piece, right_sem, here + 2)
+
+            @pl.when(jnp.logical_and(inner, chip - far >= 0))
+            def _():
+                pass_on(chip - far, chips if far == 1 else chip - far, piece, left_sem, here - 2)
+
+    def row_copy(hop, block):
+        other = lax.rem(row + hop, row_count)
+        return pltpu.make_async_remote_copy(
+            src_ref=flat_ref,
+            dst_ref=every_ref.at[block],
+            send_sem=row_send.at[hop],
+            recv_sem=row_recv.at[hop],
+            device_id={"row": other},
+            device_id_type=MESH_ID,
+        )
+
+    for piece in range(parts):
+        o_ref[rows_of(piece)] = pair_sum(chip, piece)
+
+        @pl.when(chip > 0)
+        def _():
+            line_copy(chip, chip, piece, right_sem, mate).wait_recv()
+            o_ref[rows_of(piece)] += line_buf[chip, rows_of(piece)].astype(F32)
+
+        @pl.when(chip < chips - 1)
+        def _():
+            line_copy(chip, chips, piece, left_sem, mate).wait_recv()
+            o_ref[rows_of(piece)] += line_buf[chips, rows_of(piece)].astype(F32)
+
+        if piece == 0:
+            flat_ref[pl.ds(0, 6 * rank)] = o_ref[pl.ds(0, 6 * rank)].astype(BF16)
+            flat_ref[pl.ds(6 * rank, rank)] = ga_ref[...].astype(BF16)
+            for m in range(3):
+                flat_ref[pl.ds((7 + m) * rank, rank)] = grad_b[
+                    m * rank : (m + 1) * rank, m * part : (m + 1) * part
+                ].astype(BF16)
+            owner = jnp.full((16, part), slot_ref[0].astype(F32), F32)
+            flat_ref[pl.ds(10 * rank, 16)] = owner.astype(BF16)
+            for hop in range(1, row_count):
+                row_copy(hop, row).start()
+            every_ref[row] = flat_ref[...]
+
+    stat_rows = o_ref[pl.ds(ranks + 3 * rank, 8)] + o_ref[pl.ds(ranks + 3 * rank + 8, 8)]
+    upright = jnp.transpose(stat_rows)
+    own = pl.ds(pl.multiple_of(here * part, 128), part)
+    gain = gain_ref[:, own]
+    for t in range(seq_len // part):
+        rows = pl.ds(t * part, part)
+        inv = inv1_ref[rows]
+        pull = inv * inv * inv * upright[:, t : t + 1] * (1.0 / width)
+        gi_ref[rows] = (
+            g_ref[rows, own].astype(F32)
+            + inv * gain * o_ref[pl.ds(extra + t * part, part)]
+            - x_ref[rows, own].astype(F32) * pull
+        )
+    for hop in range(1, row_count):
+        row_copy(hop, lax.rem(row + row_count - hop, row_count)).wait_recv()
+    held = held_ref.shape[0]
+    for h in range(held):
+        chosen = (row * held + h).astype(F32)
+        picked = jnp.zeros((10 * rank, part), F32)
+        for r in range(row_count):
+            owner = every_ref[r, pl.ds(10 * rank, 16)].astype(F32)[0:1]
+            picked += jnp.where(owner == chosen, every_ref[r, pl.ds(0, 10 * rank)].astype(F32), 0.0)
+        held_ref[h] = picked
+
+    for hop in range(1, row_count):
+        row_copy(hop, row).wait_send()
+    for hop in range(1, count):
+        stat_copy(hop, here).wait_send()
+    for j in range(chips):
+        for piece in range(parts):
+            mate_copy(j, piece).wait_send()
+
+            @pl.when(j > chip)
+            def _():
+                line_copy(j, j, piece, right_sem, mate).wait_send()
+
+            @pl.when(j < chip)
+            def _():
+                line_copy(j, j, piece, left_sem, mate).wait_send()
+
+
+def back(prefix, slot, operands, weights, reach, scale, chips, row_count, held, ident):
+    x = operands[15]
     seq_len, width = x.shape
-    part = operands[1].shape[1]
-    ranks = operands[9].shape[0]
+    part = weights[0].shape[1]
+    count = 2 * chips
+    ranks = operands[14].shape[0]
+    rank = ranks // 3
+    extra = 128
+    tall = seq_len + extra
+    sems = pltpu.SemaphoreType.DMA((chips, 2))
+    hops = pltpu.SemaphoreType.DMA((count,))
+    row_hops = pltpu.SemaphoreType.DMA((row_count,))
+    smem = pl.BlockSpec(memory_space=pltpu.SMEM)
     return pl.pallas_call(
-        functools.partial(inputs_back_body, min(256, seq_len), extra),
+        functools.partial(back_body, min(256, seq_len), reach, scale, chips, row_count, extra),
         out_shape=(
-            jax.ShapeDtypeStruct((seq_len + extra, width), BF16),
-            jax.ShapeDtypeStruct((ranks, part), F32),
+            jax.ShapeDtypeStruct((seq_len, part), F32),
+            jax.ShapeDtypeStruct((held, 10 * rank, part), F32),
         ),
-        in_specs=[ANY if 5 <= n < 8 else VM for n in range(len(operands))],
-        out_specs=(VM,) * 2,
-        scratch_shapes=[pltpu.VMEM((width, 3 * part), BF16), pltpu.SemaphoreType.DMA((3,))],
-        compiler_params=pltpu.CompilerParams(vmem_limit_bytes=VMEM_LIMIT),
-        name="inputs_back",
-    )(*operands)
+        in_specs=[smem, smem] + [VM] * len(operands) + [ANY] * 3,
+        out_specs=(VM, VM),
+        scratch_shapes=[
+            pltpu.VMEM((seq_len, 2 * part), F32),
+            pltpu.VMEM((seq_len, part), BF16),
+            pltpu.VMEM((2, seq_len), F32),
+            pltpu.VMEM((count, 2, seq_len), F32),
+            pltpu.VMEM((rank, part), F32),
+            pltpu.VMEM((seq_len, part), BF16),
+            pltpu.VMEM((seq_len, part), F32),
+            pltpu.VMEM((seq_len, part), F32),
+            pltpu.VMEM((seq_len, part), F32),
+            pltpu.VMEM((width, 3 * part), BF16),
+            pltpu.VMEM((seq_len, 3 * part), BF16),
+            pltpu.VMEM((seq_len, ranks), BF16),
+            pltpu.VMEM((tall, width), BF16),
+            pltpu.VMEM((tall, part), F32),
+            pltpu.VMEM((chips, tall, part), BF16),
+            pltpu.VMEM((chips + 1, tall, part), BF16),
+            pltpu.VMEM((chips, tall, part), BF16),
+            pltpu.VMEM((10 * rank + 16, part), BF16),
+            pltpu.VMEM((row_count, 10 * rank + 16, part), BF16),
+            pltpu.SemaphoreType.DMA((3,)),
+            hops,
+            hops,
+            row_hops,
+            row_hops,
+            sems,
+            sems,
+            sems,
+            pltpu.SemaphoreType.DMA((chips + 1, 2)),
+            sems,
+        ],
+        compiler_params=pltpu.CompilerParams(
+            collective_id=ident, has_side_effects=True, vmem_limit_bytes=VMEM_LIMIT
+        ),
+        name="back",
+    )(prefix, slot, *operands, *weights)
 
 
 def moments(chips, subs):
@@ -894,7 +1102,7 @@
             down = downs[0].at[e, pl.ds(piece * hidden, hidden)]
         else:
             place = 2 * ((row // 2 + piece // 2) % 2) + (row + piece) % 2
-            down = downs[1].at[piece - 1, e] if piece > 0 else downs[0].at[e]
+            down = downs[1 + e].at[piece - 1] if piece > 0 else downs[0].at[e]
         units = pl.ds(pl.multiple_of(place * hidden, 128), hidden)
         return (
             pltpu.make_async_copy(gate_w.at[e, :, units], wgu.at[step, :, pl.ds(0, hidden)], w_sems.at[step, 0]),
@@ -1160,8 +1368,9 @@
 
     full_gate = lax.all_gather(w_gate, "row", axis=2, tiled=True)
     full_up = lax.all_gather(w_up, "row", axis=2, tiled=True)
-    across = row_count == 4
-    riders = (cotangent, w_down) if across else (cotangent,)
+    across = row_count == 4 and local_experts == 2
+    down_halves = w_down.reshape((local_experts, 2, w_down.shape[1] // 2, full_width))
+    riders = (cotangent, down_halves[1]) if across else (cotangent,)
     adapter_slot = adapter_index[0]
     chosen_a = lax.dynamic_index_in_dim(adapter_a, adapter_slot, 1, keepdims=False).swapaxes(1, 2)
     chosen_b = lax.dynamic_index_in_dim(adapter_b, adapter_slot, 1, keepdims=False)
@@ -1186,7 +1395,7 @@
     tables = rope_tables(seq_len, HD)
     gain_first, gain_second = norm_first[None], norm_second[None]
 
-    full_inputs = line_gather(inputs, chips, 1, 0)
+    full_inputs, *down_first = line_gather(inputs, chips, 1, 0, rider=down_halves[0] if across else None)
     proj, mid, inv_first, squares = project(
         full_inputs, gain_first, (w_query, w_key, w_value), a_three, b_cols
     )
@@ -1196,7 +1405,7 @@
     )
     wide = full_width + lanes
     row_shape = jax.ShapeDtypeStruct
-    normed_two, hidden_rows, mid_out, mid_router, probs, full_cot, *down_others = line_turn(
+    normed_two, hidden_rows, mid_out, mid_router, probs, full_cot, *down_second = line_turn(
         part_out,
         (held_rows(full_inputs), gain_second, chosen_a[4], router_rows, router_up),
         wide,
@@ -1213,7 +1422,9 @@
         riders,
     )
     if across:
-        downs = (w_down,) + tuple(down_others)
+        downs = (w_down,) + tuple(
+            others.reshape((3,) + w_down.shape[1:]) for others in down_first + down_second
+        )
     else:
         downs = (lax.all_gather(w_down, "row", axis=1, tiled=True),)
 
@@ -1243,67 +1454,41 @@
     moe_out, grad_attn = lax.optimization_barrier((moe_out, grad_attn))
     layer_out = lax.psum_scatter(moe_out, "col", scatter_dimension=1, tiled=True)
 
-    scaled, grad_value, norm_stats, grad_a_out = attend_back(
+    held_adapters = adapter_a.shape[1] // row_count
+    grad_inputs, held = back(
         prefix,
-        grad_attn,
-        out_map,
-        chosen_b[3],
-        (attended, rot_query, rot_key, value_rows, log_totals),
-        proj,
-        gains,
-        tables,
+        adapter_index,
+        (
+            grad_attn,
+            out_map,
+            chosen_b[3],
+            attended,
+            rot_query,
+            rot_key,
+            value_rows,
+            log_totals,
+            proj,
+            gains,
+            *tables,
+            inv,
+            b_cols,
+            a_three,
+            full_inputs,
+            inv_first,
+            gain_first,
+            mid,
+            late,
+            router_late,
+        ),
+        (w_query, w_key, w_value),
         reach,
         score_scale,
+        chips,
+        row_count,
+        held_adapters,
+        12,
     )
-    stats = (col_sum(norm_stats, 10) / full_width).T
-    extra = 128
-    normed_part, grad_b_three = inputs_back(
-        extra,
-        scaled,
-        grad_value,
-        proj,
-        inv,
-        stats,
-        w_query,
-        w_key,
-        w_value,
-        b_cols,
-        a_three,
-        full_inputs,
-        inv_first,
-        gain_first,
-        mid,
-        late,
-        router_late,
-    )
-    summed_part = line_reduce(normed_part, chips, 1, 12)
-    stat_rows = seq_len // width_part
-    tail = summed_part[seq_len:]
-    stat_start = 6 * rank
-    first_stat = (
-        tail[stat_start : stat_start + stat_rows] + tail[stat_start + 8 : stat_start + 8 + stat_rows]
-    ).reshape(seq_len, 1)
-    grad_inputs = (
-        columns(grad_attn, 1).astype(F32)
-        + inv_first * columns(norm_first, 0) * summed_part[:seq_len]
-        - inputs.astype(F32) * (inv_first * inv_first * inv_first * first_stat / full_width)
-    )
-
-    held_adapters = adapter_a.shape[1] // row_count
-    flat = jnp.concatenate(
-        [
-            tail[: 6 * rank],
-            grad_a_out,
-            grad_b_three,
-            jnp.broadcast_to(adapter_slot.astype(F32), (8, width_part)),
-        ]
-    ).astype(BF16)
-    every = lax.all_gather(flat, "row", axis=0).astype(F32)
-    owners = every[:, -1, 0]
-    held_ids = (row_index * held_adapters + jnp.arange(held_adapters)).astype(F32)
-    pick = (owners[None, :] == held_ids[:, None])[:, :, None, None]
-    summed = jnp.sum(jnp.where(pick, every[None], 0.0), axis=1)
-    pieces = [summed[:, n * rank : (n + 1) * rank] for n in range(10)]
+    pieces = [held[:, n * rank : (n + 1) * rank] for n in range(10)]
     query_a, key_a, value_a, router_a, out_b, router_up_grad, out_a, query_b, key_b, value_b = pieces
     grad_a = jnp.stack([query_a, key_a, value_a, out_a, router_a]).swapaxes(2, 3)
     grad_b = jnp.stack([query_b, key_b, value_b, out_b])

time: 488 us -> 479 us (0.982)
  Pallas kernels: 424 us -> 407 us
  waiting for transfers between devices: 2.59 us -> 16.6 us
  blocking collectives: 8.57 us -> 0 us
  local copies, waits for them, and re-layouts: 19.4 us -> 24.9 us
    pallas_call x1, Pallas kernels: 139 us -> 96.3 us  [line_turn(): pl.pallas_call(functools.partial(turn_body, chips, parts, first, last, le...]
    pallas_call x4 -> x2, Pallas kernels: 119 us -> 159 us  [the longest x1 91.5 us: back(): pl.pallas_call(functools.partial(back_body, min(256, seq_len), reach, sca...]
    all_gather x1, waiting for transfers between devices: 1.19 us -> 15.2 us  [shards(): full_up = lax.all_gather(w_up, 'row', axis=2, tiled=True)]
    pallas_call x2 -> x1, Pallas kernels: 19.4 us -> 7.12 us  [small_gather(): pl.pallas_call(functools.partial(small_body, count), out_shape=jax.ShapeD...]
    all_gather x1 -> x0, blocking collectives: 8.57 us -> none  [shards(): every = lax.all_gather(flat, 'row', axis=0).astype(F32)]
    unnamed x35 -> x26, local copies, waits for them, and re-layouts: 1.32 us -> 6.43 us
  transfers between devices with their start and end apart: 3 -> 3, of which waited for: 1 -> 1; matrix products, arithmetic and copies ran while one was open for 6% -> 6% of each run, Pallas kernels for 63% -> 61%
where the time goes in v5:
time: 479 us; the launch traced here: 471 us
  Pallas kernels  407 us (85%)
  local copies, waits for them, and re-layouts  24.9 us (5%)
  waiting for transfers between devices  16.6 us (3%)
  between operations  15.7 us (3%)
  other arithmetic  6.16 us (1%)
    pallas_call x1, Pallas kernels, moe_turn(): pl.pallas_call(functools.partial(moe_turn_body, experts, chips, subs, len...  118 us
    pallas_call x1, Pallas kernels, line_turn(): pl.pallas_call(functools.partial(turn_body, chips, parts, first, last, le...  96.3 us
    pallas_call x1, Pallas kernels, back(): pl.pallas_call(functools.partial(back_body, min(256, seq_len), reach, sca...  91.5 us
    pallas_call x1, Pallas kernels, line_gather(): pl.pallas_call(functools.partial(gather_body, chips, parts, axis, len(mor...  67.6 us
    all_gather x1, waiting for transfers between devices, shards(): full_up = lax.all_gather(w_up, 'row', axis=2, tiled=True)  15.2 us
    pallas_call x1, Pallas kernels, project(): pl.pallas_call(functools.partial(project_body, min(256, seq_len)), out_sh...  14.4 us
    pallas_call x1, Pallas kernels, attend(): pl.pallas_call(functools.partial(attend_body, min(256, seq_len), reach, s...  11.8 us
  transfers between devices with their start and end apart: 3, of which 1 were waited for; matrix products, arithmetic and copies ran while one was open for 6% of the time, Pallas kernels for 61%

profile of v5, /device:TPU:16, one launch (start us, length us, event | category | flops | bytes accessed | tf_op | source)
XLA Modules:
  0.0 471.1 jit_solution(15627622186254908379)
XLA Ops:
  8.0 0.7 all-gather.5.cloned.1.call-update
  10.0 0.8 dynamic_slice.35
  10.8 0.8 dynamic_slice.36
  11.6 1.0 dynamic-slice_bitcast_fusion
  14.6 0.8 pad.10.refs_4_
  15.5 1.0 copy.34.routes_ref
  16.5 1.5 fusion.7
  18.0 67.6 %line_gather.1 = (bf16[1024,2048]{1,0:T(8,128)(2,1)}, bf16[3,2,128,2048]{3,2,1,0:T(8,128)(2,1)}) custom-call(bf16[1024,256]{1,0:T(8,128)(2,1)} %x_ref.1, bf16[2,128,2048]{2,1,0:T(8,128)(2,1)} %bitcast.54), custom_call_target="tpu_custom_call" | custom-call | tf_op jit(solution)/shard_map/line_gather/pallas_call | solution.py:180
  85.6 1.0 constant_dynamic-slice_fusion
  87.3 14.4 %project.1 = (f32[1024,768]{1,0:T(8,128)}, bf16[1024,48]{1,0:T(8,128)(2,1)}, f32[1024,1]{1,0:T(8,128)}, f32[2,1024]{1,0:T(2,128)}) custom-call(bf16[1024,2048]{1,0:T(8,128)(2,1)} %get-tuple-element.32.x_ref.refs_15_, f32[1,2048]{1,0:T(1,128)} %bitcast.64, bf16[2048,256]{1,0:T(8,128)(2,1)} %refs_21_.1, bf16[2048,256]{1,0:T(8,128)(2,1)} %refs_22_.1, ...), custom_call_target="tpu_custom_call" | custom-call | tf_op jit(solution)/shard_map/project/pallas_call | solution.py:602
  101.7 7.1 %small_gather.1 = f32[8,2,1024]{2,1,0:T(2,128)} custom-call(f32[2,1024]{1,0:T(2,128)} %get-tuple-element.34.x_ref), custom_call_target="tpu_custom_call" | custom-call | tf_op jit(solution)/shard_map/small_gather/pallas_call | solution.py:318
  108.8 0.9 reduce_sum.9
  109.7 1.0 copy.32
  110.7 0.8 dynamic-slice_bitcast_fusion.1.refs_2_
  112.1 2.1 concatenate.27.map_ref
  114.7 2.0 fusion.3
  116.7 1.3 pad_maximum_fusion
  118.0 11.8 %attend.1 = (bf16[1024,2176]{1,0:T(8,128)(2,1)}, bf16[1024,256]{1,0:T(8,128)(2,1)}, bf16[1024,256]{1,0:T(8,128)(2,1)}, bf16[1024,256]{1,0:T(8,128)(2,1)}, bf16[1024,256]{1,0:T(8,128)(2,1)}, /*index=5*/f32[1024,2]{1,0:T(8,128)}) custom-call(s32[1]{0:T(128)S(6)} %copy.40.prefix_ref, f32[1024,768]{1,0:T(8,128)} %get-tuple-element.33.proj_ref.refs_8_, ...), custom_call_target="tpu_custom_call" | custom-call | tf_op jit(solution)/shard_map/attend/pallas_call | solution.py:660
  129.8 1.9 constant_dynamic-slice_fusion.2.refs_1_
  131.7 96.3 %line_turn.1 = (bf16[1024,2176]{1,0:T(8,128)(2,1)}, f32[128,2048]{1,0:T(8,128)}, bf16[128,128]{1,0:T(8,128)(2,1)}, bf16[128,16]{1,0:T(8,128)(2,1)}, f32[128,128]...) custom-call(bf16[1024,2176]{1,0:T(8,128)(2,1)} %get-tuple-element.35.refs_0_, ...), custom_call_target="tpu_custom_call" | custom-call | tf_op jit(solution)/shard_map/line_turn/pallas_call | solution.py:486
  228.0 1.9 constant_dynamic-slice_fusion.1.refs_0_
  229.9 15.2 %all-gather.5.cloned.1.call-done.refs_10_ = bf16[2,2048,1024]{2,1,0:T(8,128)(2,1)} async-done(((bf16[2,2048,256]{2,1,0:T(8,128)(2,1)}), bf16[2,2048,1024]{2,1,0:T(8,128)(2,1)}) %all-gather.5.cloned.1.call-update) | async-done | bytes 8388624 | tf_op jit(solution)/shard_map/all_gather | solution.py:1370
  245.1 118.4 %moe_turn.1 = (bf16[1024,2048]{1,0:T(8,128)(2,1)}, bf16[1024,2048]{1,0:T(8,128)(2,1)}, f32[32,2048]{1,0:T(8,128)}, f32[16,128]{1,0:T(8,128)}) custom-call(bf16[1024,2176]{1,0:T(8,128)(2,1)} %get-tuple-element.36.x_ref, bf16[1024,2048]{1,0:T(8,128)(2,1)} %get-tuple-element.37.g_ref, s32[1024,8]{1,0:T(8,128)} %copy.34.routes_ref, ...), custom_call_target="tpu_custom_call" | custom-call | tf_op jit(solution)/shard_map/moe_turn/pallas_call | solution.py:1275
  363.6 91.5 %back.1 = (f32[1024,256]{1,0:T(8,128)}, f32[2,160,256]{2,1,0:T(8,128)}) custom-call(s32[1]{0:T(128)S(6)} %copy.40.prefix_ref, s32[1]{0:T(128)} %copy.41.slot_ref, bf16[1024,2048]{1,0:T(8,128)(2,1)} %get-tuple-element.47.refs_0_, bf16[256,2048]{1,0:T(8,128)(2,1)} %copy-done.2, bf16[16,2048]{1,0:T(8,128)(2,1)} %copy-done.5, ...), custom_call_target="tpu_custom_call" | custom-call | tf_op jit(solution)/shard_map/back/pallas_call | solution.py:1011
  455.2 1.3 slice.85
  456.5 0.8 slice_bitcast_fusion.4
  458.0 0.8 bitcast_dynamic-update-slice_fusion.4
  458.7 0.8 bitcast_dynamic-update-slice_fusion.3
  459.5 0.8 bitcast_dynamic-update-slice_fusion.2
  460.3 0.8 bitcast_dynamic-update-slice_fusion.1
  461.0 0.8 bitcast_dynamic-update-slice_fusion
  461.8 2.3 copy.42
  (43 shorter events, 5.4 us)
Async XLA Ops:
  7.2 6.9 %copy-start = (bf16[8,16,16]{2,1,0:T(8,128)(2,1)S(1)}, bf16[8,16,16]{2,1,0:T(8,128)(2,1)}, u32[]{:S(2)}) copy-start(bf16[8,16,16]{2,1,0:T(8,128)(2,1)} %param.36) | copy-start | bytes 12292
  7.2 7.5 %copy-start.6 = (bf16[2048,16]{0,1:T(8,128)(2,1)S(1)}, bf16[2048,16]{0,1:T(8,128)(2,1)}, u32[]{:S(2)}) copy-start(bf16[2048,16]{0,1:T(8,128)(2,1)} %param.30) | copy-start | bytes 196612
  7.2 8.3 %copy-start.7 = (s32[1024,8]{0,1:T(8,128)S(1)}, s32[1024,8]{0,1:T(8,128)}, u32[]{:S(2)}) copy-start(s32[1024,8]{0,1:T(8,128)} %param.37) | copy-start | bytes 98308
  7.2 9.3 %copy-start.3 = (bf16[2,256,2048]{2,1,0:T(8,128)(2,1)S(1)}, bf16[2,256,2048]{2,1,0:T(8,128)(2,1)}, u32[]{:S(2)}) copy-start(bf16[2,256,2048]{2,1,0:T(8,128)(2,1)} %refs_11_.1) | copy-start | bytes 6291460
  7.2 222.7 %all-gather.3.cloned.1.call-start = ((), (), s32[]{:S(2)}) async-start(), calls=%async_computation.1 | async-start | bytes 10485760 | tf_op jit(solution)/shard_map/all_gather | solution.py:1369
  8.0 237.2 %all-gather.5.cloned.1.call-start = ((), (), s32[]{:S(2)}) async-start(), calls=%async_computation.2 | async-start | bytes 10485760 | tf_op jit(solution)/shard_map/all_gather | solution.py:1370
  8.7 453.1 %reduce-scatter.2.cloned.1.call-start = ((), (), s32[]{:S(2)}) async-start(), calls=%async_computation.3 | async-start | bytes 4718592 | tf_op jit(solution)/shard_map/reduce_scatter | solution.py:1455
  16.5 70.1 %copy-start.9 = (pred[48]{0:T(512)(128)(4,1)S(1)}, pred[48]{0:T(512)(128)(4,1)}, u32[]{:S(2)}) copy-start(pred[48]{0:T(512)(128)(4,1)} %constant.17.clone.1) | copy-start | bytes 148
  87.3 24.3 %copy-start.4 = (bf16[256,2048]{1,0:T(8,128)(2,1)S(1)}, bf16[256,2048]{1,0:T(8,128)(2,1)}, u32[]{:S(2)}) copy-start(bf16[256,2048]{1,0:T(8,128)(2,1)} %param.29) | copy-start | bytes 3145732
  111.6 6.4 %copy-start.5 = (bf16[16,2048]{1,0:T(8,128)(2,1)}, bf16[16,2048]{1,0:T(8,128)(2,1)S(1)}, u32[]{:S(2)}) copy-start(bf16[16,2048]{1,0:T(8,128)(2,1)S(1)} %dynamic-slice_bitcast_fusion.1.refs_2_) | copy-start | bytes 196612
  112.0 6.0 %copy-start.2 = (bf16[256,2048]{1,0:T(8,128)(2,1)}, bf16[256,2048]{1,0:T(8,128)(2,1)S(1)}, u32[]{:S(2)}) copy-start(bf16[256,2048]{1,0:T(8,128)(2,1)S(1)} %fusion.refs_1_) | copy-start | bytes 3145732
  363.6 100.5 %copy-start.1 = (bf16[8,16,16]{2,1,0:T(8,128)(2,1)S(1)}, bf16[8,16,16]{2,1,0:T(8,128)(2,1)}, u32[]{:S(2)}) copy-start(bf16[8,16,16]{2,1,0:T(8,128)(2,1)} %param.36) | copy-start | bytes 12292
  461.8 2.3 copy-start.8
Sparse Core Ops, SparseCore 0:
  9.8 114.3 all-gather.2
  126.1 119.0 all-gather.4
  363.7 62.7 reduce-scatter.1

commit v6 on v5

--- a/solution.py
+++ b/solution.py
@@ -13,7 +13,8 @@
 VM = pl.BlockSpec(memory_space=pltpu.VMEM)
 ANY = pl.BlockSpec(memory_space=pl.ANY)
 VMEM_LIMIT = 60 * 1024 * 1024
-VMEM_MOST = 63 * 1024 * 1024
+VMEM_MOST = 67_000_000
+SHARES, FIRST_SHARE = 8, 2
 
 norm_eps = 1e-05
 rope_base = 10000.0
@@ -98,7 +99,7 @@
     sems = refs[2 * riders + 1 :]
     steps = [gather_steps(chips, parts, axis, x_ref, o_ref, *sems[:6])]
     if riders:
-        steps.append(row_gather_steps(2, refs[0], refs[2], *sems[6:]))
+        steps.append(row_gather_steps(2, 0, refs[0], refs[2], *sems[6:]))
     run(*steps)
 
 
@@ -176,7 +177,7 @@
     shape = (2 * chips * rows, cols) if axis == 0 else (rows, 2 * chips * cols)
     whole = jax.ShapeDtypeStruct(shape, x.dtype)
     more = () if rider is None else (rider,)
-    ridden = tuple(jax.ShapeDtypeStruct((3,) + one.shape, one.dtype) for one in more)
+    ridden = tuple(jax.ShapeDtypeStruct((3, FIRST_SHARE) + one.shape[1:], one.dtype) for one in more)
     return pl.pallas_call(
         functools.partial(gather_body, chips, parts, axis, len(more)),
         out_shape=(whole,) + ridden,
@@ -343,14 +344,15 @@
     return 2 * major + 1 - minor, 2 * (1 - major) + minor
 
 
-def row_gather_steps(pauses, x_ref, o_ref, *sems):
+def row_gather_steps(pauses, begin, x_ref, o_ref, *sems):
     near, next_one = row_partners()
-    half = x_ref.shape[0] // 2
+    half = o_ref.shape[1] // 2
 
     def side(neighbour, first):
         slot, device = (0, near) if neighbour == 0 else (1, next_one)
         rows = pl.ds(first * half, half)
-        return row_copy(x_ref.at[rows], o_ref.at[slot, rows], sems, 2 * slot + first, device)
+        source = x_ref.at[pl.ds(begin + first * half, half)]
+        return row_copy(source, o_ref.at[slot, rows], sems, 2 * slot + first, device)
 
     def onward(neighbour):
         slot, device = (0, next_one) if neighbour == 0 else (1, near)
@@ -398,7 +400,7 @@
     if riders > 0:
         steps.append(gather_steps(chips, 2, 1, rider_in[0], rider_out[0], *take(6)))
     if riders > 1:
-        across = row_gather_steps(1, rider_in[1], rider_out[1], *take(2))
+        across = row_gather_steps(1, FIRST_SHARE, rider_in[1], rider_out[1], *take(2))
         next(across)
     run(*steps)
     here = lax.axis_index("col")
@@ -410,12 +412,12 @@
             next(across)
         last(kept, operands, results)
 
-    gather_rows(chips, parts, o_ref, *gather_sems, beside)
+    run(gather_rows_steps(chips, parts, o_ref, *gather_sems, beside))
     if riders > 1:
         run(across)
 
 
-def gather_rows(chips, parts, o_ref, right_sem, left_sem, mate_sem, line_recv, mate_recv, beside):
+def gather_rows_steps(chips, parts, o_ref, right_sem, left_sem, mate_sem, line_recv, mate_recv, beside):
     here, chip, core, mate = line_place()
     size = (o_ref.shape[0] // (2 * chips), o_ref.shape[1])
 
@@ -442,6 +444,7 @@
     for part in range(parts):
         forward(chip, part, True, True)
     beside()
+    yield
     for far in range(1, chips):
         for part in range(parts):
 
@@ -454,6 +457,8 @@
             def _():
                 copy(chip + far, part, left_sem, line_recv, mate).wait_recv()
                 forward(chip + far, part, False, True)
+
+        yield
 
     for j in range(chips):
         for part in range(parts):
@@ -481,7 +486,7 @@
         ridden.append(jax.ShapeDtypeStruct((height, 2 * chips * part), BF16))
         more += [pltpu.SemaphoreType.DMA((chips, 2))] * 5 + [pltpu.SemaphoreType.DMA((2,))]
     if len(riders) > 1:
-        ridden.append(jax.ShapeDtypeStruct((3,) + riders[1].shape, BF16))
+        ridden.append(jax.ShapeDtypeStruct((3, SHARES - FIRST_SHARE) + riders[1].shape[1:], BF16))
         more += [pltpu.SemaphoreType.DMA((6,))] * 2
     return pl.pallas_call(
         functools.partial(turn_body, chips, parts, first, last, len(operands), len(results), len(riders)),
@@ -534,15 +539,14 @@
     return None
 
 
-def turn_backward(width, experts, sums, operands, results, o_ref, own):
+def turn_backward(experts, grads, pair, operands, results, o_ref, own):
     g_ref, hidden_ref, gain_ref, a_ref, router_ref, up_ref, probs_ref, mid_router_ref, mid_ref = operands
-    pair = sums[:, width:]
     lanes = pair.shape[1]
     grad_probs = pair + pltpu.roll(pair, lanes - experts, 1)
     probs = probs_ref[...]
     grad_logits = (probs * (grad_probs - jnp.sum(probs * grad_probs, axis=1, keepdims=True))).astype(BF16)
     grad_mid = nt(grad_logits, up_ref[...]).astype(BF16)
-    grad_normed = sums[:, :width] + nn(grad_logits, router_ref[...]) + nn(grad_mid, a_ref[...])
+    grad_normed = grads + nn(grad_logits, router_ref[...]) + nn(grad_mid, a_ref[...])
     hidden = hidden_ref[...]
     inv = inverse_rms(hidden)
     scaled = grad_normed * gain_ref[...]
@@ -734,7 +738,7 @@
     g_ref, map_ref, bo_ref, att_ref, q_ref, k_ref, v_ref, log_ref, proj_ref, gains_ref, cos_ref, sin_ref = take(12)
     inv_ref, b_ref, a_ref, x_ref, inv1_ref, gain_ref, mid_ref, late_ref, router_ref = take(9)
     weights = take(3)
-    gi_ref, held_ref = take(2)
+    gi_ref, held_a, held_b, held_router = take(4)
     scaled_ref, dv_ref, stat_ref, stats_ref, ga_ref, da_ref, dq_acc, dk_acc, dv_acc = take(9)
     w_ref, d_ref, middle_ref, p_ref, o_ref, pair_buf, line_buf, sums, flat_ref, every_ref = take(10)
     w_sems, stat_send, stat_recv, row_send, row_recv = take(5)
@@ -969,14 +973,18 @@
         )
     for hop in range(1, row_count):
         row_copy(hop, lax.rem(row + row_count - hop, row_count)).wait_recv()
-    held = held_ref.shape[0]
+    held = held_router.shape[0]
     for h in range(held):
         chosen = (row * held + h).astype(F32)
         picked = jnp.zeros((10 * rank, part), F32)
         for r in range(row_count):
             owner = every_ref[r, pl.ds(10 * rank, 16)].astype(F32)[0:1]
             picked += jnp.where(owner == chosen, every_ref[r, pl.ds(0, 10 * rank)].astype(F32), 0.0)
-        held_ref[h] = picked
+        for n, piece in enumerate((0, 1, 2, 6, 3)):
+            held_a[n, h] = picked[piece * rank : (piece + 1) * rank]
+        for n, piece in enumerate((7, 8, 9, 4)):
+            held_b[n, h] = picked[piece * rank : (piece + 1) * rank]
+        held_router[h] = picked[5 * rank : 6 * rank]
 
     for hop in range(1, row_count):
         row_copy(hop, row).wait_send()
@@ -1012,10 +1020,12 @@
         functools.partial(back_body, min(256, seq_len), reach, scale, chips, row_count, extra),
         out_shape=(
             jax.ShapeDtypeStruct((seq_len, part), F32),
-            jax.ShapeDtypeStruct((held, 10 * rank, part), F32),
+            jax.ShapeDtypeStruct((5, held, rank, part), F32),
+            jax.ShapeDtypeStruct((4, held, rank, part), F32),
+            jax.ShapeDtypeStruct((held, rank, part), F32),
         ),
         in_specs=[smem, smem] + [VM] * len(operands) + [ANY] * 3,
-        out_specs=(VM, VM),
+        out_specs=(VM,) * 4,
         scratch_shapes=[
             pltpu.VMEM((seq_len, 2 * part), F32),
             pltpu.VMEM((seq_len, part), BF16),
@@ -1075,15 +1085,17 @@
         del refs[:number]
         return taken
 
-    operands = take(9)
+    operands = [None] + take(8)
     gate_w, up_w = take(2)
     downs = take(count)
-    out_ref, o_ref = take(2)
+    layer_ref, o_ref = take(2)
     results = take(2)
+    out_ref, out_pair, out_line = take(3)
     p_ref, out_acc, dx_acc, gate_acc, wgu, wd, x_buf, g_buf = take(8)
-    sums_in, pair_buf, line_buf, sums = take(4)
+    pair_buf, line_buf, sums = take(3)
     w_sems, tile_sems, right_sem, left_sem, mate_sem, line_recv, mate_recv = take(7)
-    gather_sems = refs
+    gather_sems = take(5)
+    out_sems = refs
     here, chip, core, mate = line_place()
     row = lax.axis_index("row")
     hidden = wd.shape[1]
@@ -1099,16 +1111,29 @@
     def fetches(step, e, piece):
         if count == 1:
             place = piece
-            down = downs[0].at[e, pl.ds(piece * hidden, hidden)]
+            pairs = [(downs[0].at[e, pl.ds(piece * hidden, hidden)], wd.at[step])]
         else:
             place = 2 * ((row // 2 + piece // 2) % 2) + (row + piece) % 2
-            down = downs[1 + e].at[piece - 1] if piece > 0 else downs[0].at[e]
+            if piece == 0:
+                pairs = [(downs[0].at[e], wd.at[step])]
+            else:
+                early = downs[1].shape[1]
+                pairs = [
+                    (
+                        ref.at[piece - 1, pl.ds(low - start, high - low)],
+                        wd.at[step, pl.ds(low - e * hidden, high - low)],
+                    )
+                    for ref, start, low, high in (
+                        (downs[1], 0, e * hidden, min(early, (e + 1) * hidden)),
+                        (downs[2], early, max(early, e * hidden), (e + 1) * hidden),
+                    )
+                    if high > low
+                ]
         units = pl.ds(pl.multiple_of(place * hidden, 128), hidden)
         return (
             pltpu.make_async_copy(gate_w.at[e, :, units], wgu.at[step, :, pl.ds(0, hidden)], w_sems.at[step, 0]),
             pltpu.make_async_copy(up_w.at[e, :, units], wgu.at[step, :, pl.ds(hidden, hidden)], w_sems.at[step, 1]),
-            pltpu.make_async_copy(down, wd.at[step], w_sems.at[step, 2]),
-        )
+        ) + tuple(pltpu.make_async_copy(source, place, w_sems.at[step, 2]) for source, place in pairs)
 
     def order(s):
         right = chips - 1 - chip
@@ -1118,10 +1143,9 @@
         return pl.ds(pl.multiple_of(order(s) * tile, 8), tile)
 
     def tiles(s):
-        slot = s % 2
         return (
-            pltpu.make_async_copy(x_ref.at[tile_rows(s)], x_buf.at[slot], tile_sems.at[slot, 0]),
-            pltpu.make_async_copy(g_ref.at[tile_rows(s)], g_buf.at[slot], tile_sems.at[slot, 1]),
+            pltpu.make_async_copy(x_ref.at[tile_rows(s)], x_buf, tile_sems.at[0]),
+            pltpu.make_async_copy(g_ref.at[tile_rows(s)], g_buf, tile_sems.at[1]),
         )
 
     for copy in tiles(0):
@@ -1160,18 +1184,12 @@
 
     def one_sub(k, carry):
         s, sub = k // subs, k % subs
-        slot = s % 2
         rows = tile_rows(s)
 
         @pl.when(sub == 0)
         def _():
             for copy in tiles(s):
                 copy.wait()
-
-            @pl.when(s + 1 < chips)
-            def _():
-                for copy in tiles(s + 1):
-                    copy.start()
 
             out_acc[...] = jnp.zeros_like(out_acc)
             dx_acc[...] = jnp.zeros_like(dx_acc)
@@ -1192,14 +1210,14 @@
             mine = lane == e
             halves = jnp.logical_or(mine, lane == e + experts)
             named = jnp.sum(jnp.where(routes_ref[rows] == e, 1.0, 0.0), axis=1, keepdims=True)
-            gate = jnp.sum(jnp.where(halves, x_buf[slot, :, width:].astype(F32), 0.0), axis=1, keepdims=True)
+            gate = jnp.sum(jnp.where(halves, x_buf[:, width:].astype(F32), 0.0), axis=1, keepdims=True)
             gate = gate * named
-            both = nn(x_buf[slot, :, :width], wgu[step])
+            both = nn(x_buf[:, :width], wgu[step])
             gate_in, up_in = both[:, :hidden], both[:, hidden:]
             sigmoid = jax.nn.sigmoid(gate_in)
             silu = gate_in * sigmoid
             active = silu * up_in
-            back = nt(g_buf[slot], wd[step])
+            back = nt(g_buf[...], wd[step])
             d_gate = jnp.sum(active * back, axis=1, keepdims=True) * named
             gate_acc[...] += jnp.where(mine, d_gate, 0.0)
             out_acc[...] += nn((active * gate).astype(BF16), wd[step])
@@ -1221,9 +1239,18 @@
             p_ref[rows, width:] = (high + pltpu.roll(rest, experts, 1)).astype(BF16)
             mate_copy(order(s)).start()
 
+            @pl.when(s + 1 < chips)
+            def _():
+                for copy in tiles(s + 1):
+                    copy.start()
+
             @pl.when(s == chips - 1)
             def _():
-                out_ref[block(here)] = (out_acc[pl.ds(pl.multiple_of(core * own, 8), own)] + operands[1][...]).astype(BF16)
+                fetch = pltpu.make_async_copy(operands[1], dx_acc.at[pl.ds(own, own)], tile_sems.at[0])
+                fetch.start()
+                fetch.wait()
+                mine = out_acc[pl.ds(pl.multiple_of(core * own, 8), own)]
+                out_ref[block(here)] = (mine + dx_acc[pl.ds(own, own)]).astype(BF16)
 
         for (at, j), time in sorted(when.items(), key=lambda item: (item[1], abs(item[0][0] - item[0][1]))):
 
@@ -1234,17 +1261,31 @@
         return carry
 
     lax.fori_loop(0, chips * subs, one_sub, 0)
-    sums_in[...] = pair_sum(chip)
+    out_sums = wgu.at[:, pl.ds(0, tokens), pl.ds(0, layer_ref.shape[1])]
+    operands[0] = g_buf.at[pl.ds(pl.multiple_of(core * own, 8), own)]
+    operands[1] = dx_acc.at[pl.ds(own, own)]
+    layer = reduce_steps(chips, 2, 1, out_ref, layer_ref, out_pair, out_line, out_sums, *out_sems)
+    next(layer)
+    next(layer)
+    first = pl.ds(0, own)
+
+    def add(total):
+        dx_acc[first] += total[:, :width]
+        gate_acc[first] += total[:, width:]
+
+    total = pair_sum(chip)
+    dx_acc[first] = total[:, :width]
+    gate_acc[first] = total[:, width:]
 
     @pl.when(chip > 0)
     def _():
         line_copy(chip, chip, right_sem, mate).wait_recv()
-        sums_in[...] += line_buf[chip].astype(F32)
+        add(line_buf[chip].astype(F32))
 
     @pl.when(chip < chips - 1)
     def _():
         line_copy(chip, chips, left_sem, mate).wait_recv()
-        sums_in[...] += line_buf[chips].astype(F32)
+        add(line_buf[chips].astype(F32))
 
     for j in range(chips):
         mate_copy(j).wait_send()
@@ -1257,8 +1298,8 @@
         def _():
             line_copy(j, j, left_sem, mate).wait_send()
 
-    kept = turn_backward(width, experts, sums_in, operands, results, o_ref, block(here))
-    gather_rows(chips, 2, o_ref, *gather_sems, lambda: turn_late(kept, operands, results))
+    kept = turn_backward(experts, dx_acc[first], gate_acc[first], operands, results, o_ref, block(here))
+    run(gather_rows_steps(chips, 2, o_ref, *gather_sems, lambda: turn_late(kept, operands, results)), layer)
 
 
 def moe_turn(x, g, routes, operands, experts, gate_w, up_w, downs, results, chips, ident):
@@ -1270,35 +1311,39 @@
     steps = gate_w.shape[0] * gate_w.shape[2] // hidden
     subs = min(4, steps)
     whole = jax.ShapeDtypeStruct((tokens, width), BF16)
+    part = width // (2 * chips)
     per_chip = pltpu.SemaphoreType.DMA((chips,))
     halves = pltpu.SemaphoreType.DMA((chips, 2))
     return pl.pallas_call(
         functools.partial(moe_turn_body, experts, chips, subs, len(downs)),
-        out_shape=(whole, whole) + tuple(results),
-        in_specs=[ANY, ANY] + [VM] * (1 + len(operands)) + [ANY] * (2 + len(downs)),
+        out_shape=(jax.ShapeDtypeStruct((tokens, part), F32), whole) + tuple(results),
+        in_specs=[ANY, ANY, VM, ANY] + [VM] * (len(operands) - 1) + [ANY] * (2 + len(downs)),
         out_specs=(VM,) * (2 + len(results)),
         scratch_shapes=[
+            pltpu.VMEM((tokens, width), BF16),
+            pltpu.VMEM((chips, tokens, part), BF16),
+            pltpu.VMEM((chips + 1, tokens, part), BF16),
             pltpu.VMEM((tokens, wide), BF16),
             pltpu.VMEM((2 * own, width), F32),
             pltpu.VMEM((2 * own, width), F32),
             pltpu.VMEM((2 * own, lanes), F32),
             pltpu.VMEM((steps, width, 2 * hidden), BF16),
             pltpu.VMEM((steps, hidden, width), BF16),
-            pltpu.VMEM((2, 2 * own, wide), BF16),
-            pltpu.VMEM((2, 2 * own, width), BF16),
-            pltpu.VMEM((own, wide), F32),
+            pltpu.VMEM((2 * own, wide), BF16),
+            pltpu.VMEM((2 * own, width), BF16),
             pltpu.VMEM((chips, own, wide), BF16),
             pltpu.VMEM((chips + 1, own, wide), BF16),
             pltpu.VMEM((chips, own, wide), BF16),
             pltpu.SemaphoreType.DMA((steps, 3)),
-            pltpu.SemaphoreType.DMA((2, 2)),
+            pltpu.SemaphoreType.DMA((2,)),
             per_chip,
             per_chip,
             per_chip,
             pltpu.SemaphoreType.DMA((chips + 1,)),
             per_chip,
         ]
-        + [halves] * 5,
+        + [halves] * 8
+        + [pltpu.SemaphoreType.DMA((chips + 1, 2)), halves],
         compiler_params=pltpu.CompilerParams(
             collective_id=ident, has_side_effects=True, vmem_limit_bytes=VMEM_MOST
         ),
@@ -1369,8 +1414,8 @@
     full_gate = lax.all_gather(w_gate, "row", axis=2, tiled=True)
     full_up = lax.all_gather(w_up, "row", axis=2, tiled=True)
     across = row_count == 4 and local_experts == 2
-    down_halves = w_down.reshape((local_experts, 2, w_down.shape[1] // 2, full_width))
-    riders = (cotangent, down_halves[1]) if across else (cotangent,)
+    down_shares = w_down.reshape(SHARES, -1, full_width)
+    riders = (cotangent, down_shares) if across else (cotangent,)
     adapter_slot = adapter_index[0]
     chosen_a = lax.dynamic_index_in_dim(adapter_a, adapter_slot, 1, keepdims=False).swapaxes(1, 2)
     chosen_b = lax.dynamic_index_in_dim(adapter_b, adapter_slot, 1, keepdims=False)
@@ -1395,7 +1440,7 @@
     tables = rope_tables(seq_len, HD)
     gain_first, gain_second = norm_first[None], norm_second[None]
 
-    full_inputs, *down_first = line_gather(inputs, chips, 1, 0, rider=down_halves[0] if across else None)
+    full_inputs, *down_first = line_gather(inputs, chips, 1, 0, rider=down_shares if across else None)
     proj, mid, inv_first, squares = project(
         full_inputs, gain_first, (w_query, w_key, w_value), a_three, b_cols
     )
@@ -1423,17 +1468,16 @@
     )
     if across:
         downs = (w_down,) + tuple(
-            others.reshape((3,) + w_down.shape[1:]) for others in down_first + down_second
+            others.reshape(3, -1, full_width) for others in down_first + down_second
         )
     else:
         downs = (lax.all_gather(w_down, "row", axis=1, tiled=True),)
 
-    moe_out, grad_attn, late, router_late = moe_turn(
+    layer_out, grad_attn, late, router_late = moe_turn(
         normed_two,
         full_cot,
         routes,
         (
-            held_rows(full_cot),
             hidden_rows,
             gain_second,
             chosen_a[4],
@@ -1451,11 +1495,10 @@
         chips,
         7,
     )
-    moe_out, grad_attn = lax.optimization_barrier((moe_out, grad_attn))
-    layer_out = lax.psum_scatter(moe_out, "col", scatter_dimension=1, tiled=True)
+    layer_out = layer_out.astype(BF16)
 
     held_adapters = adapter_a.shape[1] // row_count
-    grad_inputs, held = back(
+    grad_inputs, grad_a, grad_b, grad_router = back(
         prefix,
         adapter_index,
         (
@@ -1488,11 +1531,8 @@
         held_adapters,
         12,
     )
-    pieces = [held[:, n * rank : (n + 1) * rank] for n in range(10)]
-    query_a, key_a, value_a, router_a, out_b, router_up_grad, out_a, query_b, key_b, value_b = pieces
-    grad_a = jnp.stack([query_a, key_a, value_a, out_a, router_a]).swapaxes(2, 3)
-    grad_b = jnp.stack([query_b, key_b, value_b, out_b])
-    grad_router = router_up_grad[:, :, :expert_total]
+    grad_a = grad_a.swapaxes(2, 3)
+    grad_router = grad_router[:, :, :expert_total]
     return (layer_out, grad_inputs, grad_a, grad_b, grad_router)
 
 

time: 479 us -> 463 us (0.967)
  Pallas kernels: 407 us -> 382 us
  waiting for transfers between devices: 16.6 us -> 30.4 us
    pallas_call x1, Pallas kernels: 67.6 us -> 42.5 us  [line_gather(): pl.pallas_call(functools.partial(gather_body, chips, parts, axis, len(mor...]
    pallas_call x1, Pallas kernels: 91.5 us -> 74.4 us  [back(): pl.pallas_call(functools.partial(back_body, min(256, seq_len), reach, sca...]
    pallas_call x1, Pallas kernels: 118 us -> 135 us  [moe_turn(): pl.pallas_call(functools.partial(moe_turn_body, experts, chips, subs, len...]
    all_gather x1, waiting for transfers between devices: 15.2 us -> 29 us  [shards(): full_up = lax.all_gather(w_up, 'row', axis=2, tiled=True)]
  transfers between devices with their start and end apart: 3 -> 2, of which waited for: 1 -> 1; matrix products, arithmetic and copies ran while one was open for 6% -> 4% of each run, Pallas kernels for 61% -> 38%
where the time goes in v6:
time: 463 us; the launch traced here: 456 us
  Pallas kernels  382 us (83%)
  waiting for transfers between devices  30.4 us (7%)
  local copies, waits for them, and re-layouts  20.2 us (4%)
  between operations  15.7 us (3%)
  other arithmetic  7.58 us (2%)
    pallas_call x1, Pallas kernels, moe_turn(): pl.pallas_call(functools.partial(moe_turn_body, experts, chips, subs, len...  135 us
    pallas_call x1, Pallas kernels, line_turn(): pl.pallas_call(functools.partial(turn_body, chips, parts, first, last, le...  96.1 us
    pallas_call x1, Pallas kernels, back(): pl.pallas_call(functools.partial(back_body, min(256, seq_len), reach, sca...  74.4 us
    pallas_call x1, Pallas kernels, line_gather(): pl.pallas_call(functools.partial(gather_body, chips, parts, axis, len(mor...  42.5 us
    all_gather x1, waiting for transfers between devices, shards(): full_up = lax.all_gather(w_up, 'row', axis=2, tiled=True)  29 us
    pallas_call x1, Pallas kernels, project(): pl.pallas_call(functools.partial(project_body, min(256, seq_len)), out_sh...  14.4 us
    pallas_call x1, Pallas kernels, attend(): pl.pallas_call(functools.partial(attend_body, min(256, seq_len), reach, s...  11.8 us
  transfers between devices with their start and end apart: 2, of which 1 were waited for; matrix products, arithmetic and copies ran while one was open for 4% of the time, Pallas kernels for 38%

profile of v6, /device:TPU:16, one launch (start us, length us, event | category | flops | bytes accessed | tf_op | source)
XLA Modules:
  0.0 456.1 jit_solution(1878275712783953558)
XLA Ops:
  7.2 0.7 all-gather.3.cloned.1.call-update
  8.0 0.7 all-gather.5.cloned.1.call-update
  10.0 0.8 dynamic_slice.32
  10.8 0.8 dynamic_slice.33
  11.5 1.0 dynamic-slice_bitcast_fusion
  12.5 0.7 slice.38
  13.2 0.6 slice_bitcast_fusion
  14.0 0.6 pad.11.refs_5_.refs_4_
  14.6 0.8 pad.10.refs_4_.refs_3_
  15.4 1.0 copy.34.routes_ref
  16.5 42.5 %line_gather.1 = (bf16[1024,2048]{1,0:T(8,128)(2,1)}, bf16[3,2,64,2048]{3,2,1,0:T(8,128)(2,1)}) custom-call(bf16[1024,256]{1,0:T(8,128)(2,1)} %x_ref.1, bf16[8,64,2048]{2,1,0:T(8,128)(2,1)} %bitcast.33), custom_call_target="tpu_custom_call" | custom-call | tf_op jit(solution)/shard_map/line_gather/pallas_call | solution.py:181
  59.0 1.0 constant_dynamic-slice_fusion
  60.1 0.6 fusion.5.b_ref.refs_13_
  60.7 14.4 %project.1 = (f32[1024,768]{1,0:T(8,128)}, bf16[1024,48]{1,0:T(8,128)(2,1)}, f32[1024,1]{1,0:T(8,128)}, f32[2,1024]{1,0:T(2,128)}) custom-call(bf16[1024,2048]{1,0:T(8,128)(2,1)} %get-tuple-element.32.x_ref.refs_15_, f32[1,2048]{1,0:T(1,128)} %bitcast.46, bf16[2048,256]{1,0:T(8,128)(2,1)} %refs_21_.1, bf16[2048,256]{1,0:T(8,128)(2,1)} %refs_22_.1, ...), custom_call_target="tpu_custom_call" | custom-call | tf_op jit(solution)/shard_map/project/pallas_call | solution.py:606
  75.1 8.0 %small_gather.1 = f32[8,2,1024]{2,1,0:T(2,128)} custom-call(f32[2,1024]{1,0:T(2,128)} %get-tuple-element.34.x_ref), custom_call_target="tpu_custom_call" | custom-call | tf_op jit(solution)/shard_map/small_gather/pallas_call | solution.py:319
  83.1 0.9 reduce_sum.9
  84.0 1.0 copy.32
  85.0 0.8 dynamic-slice_bitcast_fusion.1.refs_2_
  86.5 2.1 concatenate.27.map_ref
  89.2 2.0 fusion.3
  91.1 1.3 pad_maximum_fusion
  92.5 11.8 %attend.1 = (bf16[1024,2176]{1,0:T(8,128)(2,1)}, bf16[1024,256]{1,0:T(8,128)(2,1)}, bf16[1024,256]{1,0:T(8,128)(2,1)}, bf16[1024,256]{1,0:T(8,128)(2,1)}, bf16[1024,256]{1,0:T(8,128)(2,1)}, /*index=5*/f32[1024,2]{1,0:T(8,128)}) custom-call(s32[1]{0:T(128)S(6)} %copy.38.prefix_ref, f32[1024,768]{1,0:T(8,128)} %get-tuple-element.33.proj_ref.refs_8_, ...), custom_call_target="tpu_custom_call" | custom-call | tf_op jit(solution)/shard_map/attend/pallas_call | solution.py:664
  104.3 1.9 constant_dynamic-slice_fusion.1.refs_1_
  106.2 96.1 %line_turn.1 = (bf16[1024,2176]{1,0:T(8,128)(2,1)}, f32[128,2048]{1,0:T(8,128)}, bf16[128,128]{1,0:T(8,128)(2,1)}, bf16[128,16]{1,0:T(8,128)(2,1)}, f32[128,128]...) custom-call(bf16[1024,2176]{1,0:T(8,128)(2,1)} %get-tuple-element.35.refs_0_, ...), custom_call_target="tpu_custom_call" | custom-call | tf_op jit(solution)/shard_map/line_turn/pallas_call | solution.py:491
  202.3 29.0 %all-gather.5.cloned.1.call-done.refs_9_ = bf16[2,2048,1024]{2,1,0:T(8,128)(2,1)} async-done(((bf16[2,2048,256]{2,1,0:T(8,128)(2,1)}), bf16[2,2048,1024]{2,1,0:T(8,128)(2,1)}) %all-gather.5.cloned.1.call-update) | async-done | bytes 8388624 | tf_op jit(solution)/shard_map/all_gather | solution.py:1415
  231.3 134.6 %moe_turn.1 = (f32[1024,256]{1,0:T(8,128)}, bf16[1024,2048]{1,0:T(8,128)(2,1)}, f32[32,2048]{1,0:T(8,128)}, f32[16,128]{1,0:T(8,128)}) custom-call(bf16[1024,2176]{1,0:T(8,128)(2,1)} %get-tuple-element.36.x_ref, bf16[1024,2048]{1,0:T(8,128)(2,1)} %get-tuple-element.37.g_ref, s32[1024,8]{1,0:T(8,128)} %copy.34.routes_ref, ...), custom_call_target="tpu_custom_call" | custom-call | tf_op jit(solution)/shard_map/moe_turn/pallas_call | solution.py:1317
  365.9 2.1 convert_element_type.15
  368.0 74.4 %back.1 = (f32[1024,256]{1,0:T(8,128)}, f32[5,2,16,256]{3,2,1,0:T(8,128)}, f32[4,2,16,256]{3,2,1,0:T(8,128)}, f32[2,16,256]{2,1,0:T(8,128)}) custom-call(s32[1]{0:T(128)S(6)} %copy.38.prefix_ref, s32[1]{0:T(128)} %copy.39.slot_ref, bf16[1024,2048]{1,0:T(8,128)(2,1)} %get-tuple-element.45.refs_0_, bf16[256,2048]{1,0:T(8,128)(2,1)} %copy-done.2, ...), custom_call_target="tpu_custom_call" | custom-call | tf_op jit(solution)/shard_map/back/pallas_call | solution.py:1019
  442.4 1.3 slice.37
  443.7 2.3 copy.40
  445.9 1.6 copy.41
  447.5 1.6 copy.42
  (30 shorter events, 1.6 us)
Async XLA Ops:
  7.2 6.8 %copy-start = (bf16[8,16,16]{2,1,0:T(8,128)(2,1)S(1)}, bf16[8,16,16]{2,1,0:T(8,128)(2,1)}, u32[]{:S(2)}) copy-start(bf16[8,16,16]{2,1,0:T(8,128)(2,1)} %param.36) | copy-start | bytes 12292
  7.2 7.4 %copy-start.5 = (bf16[2048,16]{0,1:T(8,128)(2,1)S(1)}, bf16[2048,16]{0,1:T(8,128)(2,1)}, u32[]{:S(2)}) copy-start(bf16[2048,16]{0,1:T(8,128)(2,1)} %param.30) | copy-start | bytes 196612
  7.2 8.2 %copy-start.6 = (s32[1024,8]{0,1:T(8,128)S(1)}, s32[1024,8]{0,1:T(8,128)}, u32[]{:S(2)}) copy-start(s32[1024,8]{0,1:T(8,128)} %param.37) | copy-start | bytes 98308
  7.2 195.1 %all-gather.3.cloned.1.call-start = ((), (), s32[]{:S(2)}) async-start(), calls=%async_computation | async-start | bytes 10485760 | tf_op jit(solution)/shard_map/all_gather | solution.py:1414
  7.9 223.4 %all-gather.5.cloned.1.call-start = ((), (), s32[]{:S(2)}) async-start(), calls=%async_computation.1 | async-start | bytes 10485760 | tf_op jit(solution)/shard_map/all_gather | solution.py:1415
  12.5 47.5 %copy-start.7 = (pred[48]{0:T(512)(128)(4,1)S(1)}, pred[48]{0:T(512)(128)(4,1)}, u32[]{:S(2)}) copy-start(pred[48]{0:T(512)(128)(4,1)} %constant.17.clone.1) | copy-start | bytes 148
  60.7 25.2 %copy-start.3 = (bf16[256,2048]{1,0:T(8,128)(2,1)S(1)}, bf16[256,2048]{1,0:T(8,128)(2,1)}, u32[]{:S(2)}) copy-start(bf16[256,2048]{1,0:T(8,128)(2,1)} %param.29) | copy-start | bytes 3145732
  85.9 0.6 copy-start.4
  86.5 6.0 %copy-start.2 = (bf16[256,2048]{1,0:T(8,128)(2,1)}, bf16[256,2048]{1,0:T(8,128)(2,1)S(1)}, u32[]{:S(2)}) copy-start(bf16[256,2048]{1,0:T(8,128)(2,1)S(1)} %fusion.refs_1_) | copy-start | bytes 3145732
  368.0 81.1 %copy-start.1 = (bf16[8,16,16]{2,1,0:T(8,128)(2,1)S(1)}, bf16[8,16,16]{2,1,0:T(8,128)(2,1)}, u32[]{:S(2)}) copy-start(bf16[8,16,16]{2,1,0:T(8,128)(2,1)} %param.36) | copy-start | bytes 12292
Sparse Core Ops, SparseCore 0:
  9.8 103.5 all-gather.2
  115.2 116.0 all-gather.4

commit v7 on v6

--- a/solution.py
+++ b/solution.py
@@ -75,6 +75,14 @@
     @pl.when(jnp.logical_not(inner))
     def _():
         pl.semaphore_wait(barrier, 2 + len(across))
+
+
+def in_chunks(rows, size, body):
+    def one(c, carry):
+        body(pl.multiple_of(c * size, size))
+        return carry
+
+    lax.fori_loop(0, rows // size, one, 0)
 
 
 def spot(axis, size, parts, block, part):
@@ -235,20 +243,39 @@
 
     yield
 
-    def pair_sum(j, part):
+    chunk = 16 if axis == 0 else 64
+
+    def pair_sum(j, part, low):
+        block = 2 * j + core
+        if axis == 0:
+            where = (pl.ds(pl.multiple_of(block * size[0] + part * step + low, 16), chunk), slice(None))
+        else:
+            cols = pl.ds(pl.multiple_of(block * size[1], 128), size[1])
+            where = (pl.ds(pl.multiple_of(part * step + low, 16), chunk), cols)
+        return p_ref[where].astype(F32) + pair_buf[j, chunk_rows(part, low)].astype(F32)
+
+    def chunk_rows(part, low):
+        return pl.ds(pl.multiple_of(part * step + low, 16), chunk)
+
+    def pass_on(j, slot, part, more, sem, device):
         mate_copy(j, part).wait_recv()
-        return p_ref[at(2 * j + core, part)].astype(F32) + pair_buf[j, rows(part)].astype(F32)
-
-    def pass_on(j, slot, part, more, sem, device):
+
         @pl.when(more)
         def _():
             line_copy(j, j, part, sem, mate).wait_recv()
-            total = pair_sum(j, part) + line_buf[j, rows(part)].astype(F32)
-            sums[j, rows(part)] = total.astype(BF16)
+
+            def add_up(low):
+                total = pair_sum(j, part, low) + line_buf[j, chunk_rows(part, low)].astype(F32)
+                sums[j, chunk_rows(part, low)] = total.astype(BF16)
+
+            in_chunks(step, chunk, add_up)
 
         @pl.when(jnp.logical_not(more))
         def _():
-            sums[j, rows(part)] = pair_sum(j, part).astype(BF16)
+            def add_up(low):
+                sums[j, chunk_rows(part, low)] = pair_sum(j, part, low).astype(BF16)
+
+            in_chunks(step, chunk, add_up)
 
         line_copy(j, slot, part, sem, device).start()
 
@@ -268,17 +295,28 @@
         yield
 
     for part in range(parts):
-        o_ref[rows(part)] = pair_sum(chip, part)
+        mate_copy(chip, part).wait_recv()
+
+        def begin(low):
+            o_ref[chunk_rows(part, low)] = pair_sum(chip, part, low)
+
+        in_chunks(step, chunk, begin)
+
+        def add_line(slot):
+            def add_up(low):
+                o_ref[chunk_rows(part, low)] += line_buf[slot, chunk_rows(part, low)].astype(F32)
+
+            in_chunks(step, chunk, add_up)
 
         @pl.when(chip > 0)
         def _():
             line_copy(chip, chip, part, right_sem, mate).wait_recv()
-            o_ref[rows(part)] += line_buf[chip, rows(part)].astype(F32)
+            add_line(chip)
 
         @pl.when(chip < chips - 1)
         def _():
             line_copy(chip, chips, part, left_sem, mate).wait_recv()
-            o_ref[rows(part)] += line_buf[chips, rows(part)].astype(F32)
+            add_line(chips)
 
     for j in range(chips):
         for part in range(parts):
@@ -583,8 +621,8 @@
 
 def project_body(tile, x_ref, gain_ref, wq, wk, wv, a_ref, b_ref, proj_ref, mid_ref, inv_ref, sq_ref):
     part = wq.shape[1]
-    for t in range(x_ref.shape[0] // tile):
-        rows = pl.ds(t * tile, tile)
+    def one_tile(t, carry):
+        rows = pl.ds(pl.multiple_of(t * tile, tile), tile)
         x = x_ref[rows].astype(F32)
         inv = inverse_rms(x)
         inv_ref[rows] = inv
@@ -597,6 +635,9 @@
             proj_ref[rows, cols] = proj
             if m < 2:
                 sq_ref[pl.ds(m, 1), rows] = row_sums(proj * proj)[0:1]
+        return carry
+
+    lax.fori_loop(0, x_ref.shape[0] // tile, one_tile, 0)
 
 
 def project(x, gain, weights, a_rows, b_cols):
@@ -634,12 +675,19 @@
 ):
     seq_len, part = att_ref.shape
     prefix_len = prefix_ref[0]
-    for h in range(part // HD):
-        cols = pl.ds(h * HD, HD)
-        for m, ref in ((0, q_ref), (1, k_ref)):
-            plain = proj_ref[:, pl.ds(m * part + h * HD, HD)] * inv_ref[:, m : m + 1] * gains_ref[m : m + 1, cols]
-            ref[:, cols] = (plain * cos_ref[...] + pltpu.roll(plain, HD // 2, 1) * sin_ref[...]).astype(BF16)
-        v_ref[:, cols] = proj_ref[:, pl.ds(2 * part + h * HD, HD)].astype(BF16)
+
+    def one_tile(t, carry):
+        rows = pl.ds(pl.multiple_of(t * tile, tile), tile)
+        for h in range(part // HD):
+            cols = pl.ds(h * HD, HD)
+            for m, ref in ((0, q_ref), (1, k_ref)):
+                plain = proj_ref[rows, pl.ds(m * part + h * HD, HD)] * inv_ref[rows, m : m + 1]
+                plain = plain * gains_ref[m : m + 1, cols]
+                ref[rows, cols] = (plain * cos_ref[rows] + pltpu.roll(plain, HD // 2, 1) * sin_ref[rows]).astype(BF16)
+            v_ref[rows, cols] = proj_ref[rows, pl.ds(2 * part + h * HD, HD)].astype(BF16)
+        return carry
+
+    lax.fori_loop(0, seq_len // tile, one_tile, 0)
     for start in range(0, seq_len, tile):
         rows = pl.ds(start, tile)
         limit = key_limit(start, tile, seq_len, reach)
@@ -685,13 +733,15 @@
     seq_len, part = att_ref.shape
     prefix_len = prefix_ref[0]
     grad_a = jnp.zeros(ga_ref.shape, F32)
-    for start in range(0, seq_len, tile):
-        rows = pl.ds(start, tile)
+
+    def first_tile(t, grad_a):
+        rows = pl.ds(pl.multiple_of(t * tile, tile), tile)
         grads = g_ref[rows]
         da_ref[rows] = nt(grads, map_ref[...]).astype(BF16)
         grad_mid = nt(grads, b_ref[...]).astype(BF16)
-        grad_a += tn(grad_mid, att_ref[rows])
-    ga_ref[...] = grad_a
+        return grad_a + tn(grad_mid, att_ref[rows])
+
+    ga_ref[...] = lax.fori_loop(0, seq_len // tile, first_tile, grad_a)
     dk_acc[...] = jnp.zeros_like(dk_acc)
     dv_acc[...] = jnp.zeros_like(dv_acc)
     for start in range(0, seq_len, tile):
@@ -713,8 +763,9 @@
             dv_acc[keys, cols] += tn(weights.astype(BF16), grads)
     dv_ref[...] = dv_acc[...].astype(BF16)
     for m, acc in ((0, dq_acc), (1, dk_acc)):
-        for start in range(0, seq_len, tile):
-            rows = pl.ds(start, tile)
+
+        def turn_back(t, carry):
+            rows = pl.ds(pl.multiple_of(t * tile, tile), tile)
             total = jnp.zeros((8, tile), F32)
             for h in range(part // HD):
                 cols = pl.ds(h * HD, HD)
@@ -725,6 +776,9 @@
                 scaled_ref[rows, here] = scaled
                 total += row_sums(proj_ref[rows, here] * scaled)
             stat_ref[pl.ds(m, 1), rows] = total[0:1]
+            return carry
+
+        lax.fori_loop(0, seq_len // tile, turn_back, 0)
 
 
 def back_body(tile, reach, scale, chips, row_count, extra, prefix_ref, slot_ref, *refs):
@@ -782,14 +836,16 @@
     total = stats_ref[0]
     for n in range(1, count):
         total = total + stats_ref[n]
-    total = jnp.concatenate([total, jnp.zeros((6, seq_len), F32)], axis=0) * (1.0 / width)
+    stats_ref[0] = total * (1.0 / width)
 
     grad_b = jnp.zeros((ranks, 3 * part), F32)
     first_stats = jnp.zeros((8, part), F32)
     line = lax.broadcasted_iota(jnp.int32, (8, part), 0)
-    for t in range(seq_len // tile):
-        rows = pl.ds(t * tile, tile)
-        upright = jnp.transpose(total[:, t * tile : (t + 1) * tile])
+
+    def grads_tile(t, carry):
+        grad_b, first_stats = carry
+        rows = pl.ds(pl.multiple_of(t * tile, tile), tile)
+        upright = jnp.transpose(jnp.concatenate([stats_ref[0, :, rows], jnp.zeros((6, tile), F32)], axis=0))
         products = jnp.zeros((tile, part), F32)
         for m in range(3):
             cols = pl.ds(m * part, part)
@@ -809,6 +865,9 @@
             first_stats = jnp.where(
                 line == (t * tile) // part + j, first[:, j * part : (j + 1) * part], first_stats
             )
+        return grad_b, first_stats
+
+    grad_b, first_stats = lax.fori_loop(0, seq_len // tile, grads_tile, (grad_b, first_stats))
     high = first_stats.astype(BF16).astype(F32)
     router = router_ref[...]
     if part > router.shape[1]:
@@ -872,9 +931,23 @@
         for piece in range(parts):
             mate_copy(order(s), piece).start()
 
-    def pair_sum(j, piece):
+    chunk = 64
+
+    def chunk_rows(piece, low):
+        return pl.ds(pl.multiple_of(piece * step + low, 16), chunk)
+
+    def pair_sum(j, piece, low):
+        cols = pl.ds(pl.multiple_of((2 * j + core) * part, 128), part)
+        rows = chunk_rows(piece, low)
+        return p_ref[rows, cols].astype(F32) + pair_buf[j, rows].astype(F32)
+
+    def pair_up(j, piece):
         mate_copy(j, piece).wait_recv()
-        return p_ref[at(2 * j + core, piece)].astype(F32) + pair_buf[j, rows_of(piece)].astype(F32)
+
+        def add_up(low):
+            sums[j, chunk_rows(piece, low)] = pair_sum(j, piece, low).astype(BF16)
+
+        in_chunks(step, chunk, add_up)
 
     def one_block(s, carry):
         work_out(s)
@@ -883,14 +956,14 @@
         def _():
             for piece in range(parts):
                 j = order(s - 1)
-                sums[j, rows_of(piece)] = pair_sum(j, piece).astype(BF16)
+                pair_up(j, piece)
                 line_copy(j, j, piece, right_sem, here + 2).start()
 
         @pl.when(jnp.logical_and(chip == chips - 1, s > 0))
         def _():
             for piece in range(parts):
                 j = order(s - 1)
-                sums[j, rows_of(piece)] = pair_sum(j, piece).astype(BF16)
+                pair_up(j, piece)
 
                 @pl.when(j == chips - 2)
                 def _():
@@ -907,7 +980,13 @@
 
     def pass_on(j, slot, piece, sem, device):
         line_copy(j, j, piece, sem, mate).wait_recv()
-        sums[j, rows_of(piece)] = (pair_sum(j, piece) + line_buf[j, rows_of(piece)].astype(F32)).astype(BF16)
+        mate_copy(j, piece).wait_recv()
+
+        def add_up(low):
+            rows = chunk_rows(piece, low)
+            sums[j, rows] = (pair_sum(j, piece, low) + line_buf[j, rows].astype(F32)).astype(BF16)
+
+        in_chunks(step, chunk, add_up)
         line_copy(j, slot, piece, sem, device).start()
 
     for far in range(chips - 2, 0, -1):
@@ -933,17 +1012,28 @@
         )
 
     for piece in range(parts):
-        o_ref[rows_of(piece)] = pair_sum(chip, piece)
+        mate_copy(chip, piece).wait_recv()
+
+        def begin(low):
+            o_ref[chunk_rows(piece, low)] = pair_sum(chip, piece, low)
+
+        in_chunks(step, chunk, begin)
+
+        def add_line(slot):
+            def add_up(low):
+                o_ref[chunk_rows(piece, low)] += line_buf[slot, chunk_rows(piece, low)].astype(F32)
+
+            in_chunks(step, chunk, add_up)
 
         @pl.when(chip > 0)
         def _():
             line_copy(chip, chip, piece, right_sem, mate).wait_recv()
-            o_ref[rows_of(piece)] += line_buf[chip, rows_of(piece)].astype(F32)
+            add_line(chip)
 
         @pl.when(chip < chips - 1)
         def _():
             line_copy(chip, chips, piece, left_sem, mate).wait_recv()
-            o_ref[rows_of(piece)] += line_buf[chips, rows_of(piece)].astype(F32)
+            add_line(chips)
 
         if piece == 0:
             flat_ref[pl.ds(0, 6 * rank)] = o_ref[pl.ds(0, 6 * rank)].astype(BF16)
@@ -1095,10 +1185,12 @@
     pair_buf, line_buf, sums = take(3)
     w_sems, tile_sems, right_sem, left_sem, mate_sem, line_recv, mate_recv = take(7)
     gather_sems = take(5)
-    out_sems = refs
+    out_sems = take(5)
+    out_more = refs
     here, chip, core, mate = line_place()
     row = lax.axis_index("row")
-    hidden = wd.shape[1]
+    hidden = wd.shape[1] // 2
+    both_hidden = 2 * hidden
     tokens, width = out_ref.shape
     own = tokens // (2 * chips)
     tile = 2 * own
@@ -1106,22 +1198,23 @@
     local = gate_w.shape[0]
     pieces = gate_w.shape[2] // hidden
     steps = local * pieces
-    each = steps // subs
+    each = steps // subs // 2
 
     def fetches(step, e, piece):
+        slot, shift = step // 2, (step % 2) * hidden
         if count == 1:
             place = piece
-            pairs = [(downs[0].at[e, pl.ds(piece * hidden, hidden)], wd.at[step])]
+            pairs = [(downs[0].at[e, pl.ds(piece * hidden, hidden)], wd.at[slot, pl.ds(shift, hidden)])]
         else:
             place = 2 * ((row // 2 + piece // 2) % 2) + (row + piece) % 2
             if piece == 0:
-                pairs = [(downs[0].at[e], wd.at[step])]
+                pairs = [(downs[0].at[e], wd.at[slot, pl.ds(shift, hidden)])]
             else:
                 early = downs[1].shape[1]
                 pairs = [
                     (
                         ref.at[piece - 1, pl.ds(low - start, high - low)],
-                        wd.at[step, pl.ds(low - e * hidden, high - low)],
+                        wd.at[slot, pl.ds(shift + low - e * hidden, high - low)],
                     )
                     for ref, start, low, high in (
                         (downs[1], 0, e * hidden, min(early, (e + 1) * hidden)),
@@ -1131,9 +1224,11 @@
                 ]
         units = pl.ds(pl.multiple_of(place * hidden, 128), hidden)
         return (
-            pltpu.make_async_copy(gate_w.at[e, :, units], wgu.at[step, :, pl.ds(0, hidden)], w_sems.at[step, 0]),
-            pltpu.make_async_copy(up_w.at[e, :, units], wgu.at[step, :, pl.ds(hidden, hidden)], w_sems.at[step, 1]),
-        ) + tuple(pltpu.make_async_copy(source, place, w_sems.at[step, 2]) for source, place in pairs)
+            pltpu.make_async_copy(gate_w.at[e, :, units], wgu.at[slot, :, pl.ds(shift, hidden)], w_sems.at[slot, 0]),
+            pltpu.make_async_copy(
+                up_w.at[e, :, units], wgu.at[slot, :, pl.ds(both_hidden + shift, hidden)], w_sems.at[slot, 1]
+            ),
+        ) + tuple(pltpu.make_async_copy(source, target, w_sems.at[slot, 2]) for source, target in pairs)
 
     def order(s):
         right = chips - 1 - chip
@@ -1170,11 +1265,20 @@
 
     def pass_on(at, j):
         rightward = j > at
-        total = pair_sum(j)
-        if 0 < at < chips - 1:
+        mate_copy(j).wait_recv()
+        inner = 0 < at < chips - 1
+        if inner:
             line_copy(j, j, right_sem if rightward else left_sem, mate).wait_recv()
-            total = total + line_buf[j].astype(F32)
-        sums[j] = total.astype(BF16)
+
+        def add_up(low):
+            rows = pl.ds(low, 16)
+            mine = p_ref[pl.ds(pl.multiple_of((2 * j + core) * own + low, 16), 16)]
+            total = mine.astype(F32) + pair_buf[j, rows].astype(F32)
+            if inner:
+                total = total + line_buf[j, rows].astype(F32)
+            sums[j, rows] = total.astype(BF16)
+
+        in_chunks(own, 16, add_up)
         if rightward:
             line_copy(j, j, right_sem, here + 2).start()
         else:
@@ -1198,14 +1302,13 @@
         def one_step(step, carry):
             @pl.when(s == 0)
             def _():
-                units = pl.ds(0, hidden)
-                for number, (source, place) in enumerate(((gate_w, 0), (up_w, hidden))):
-                    pltpu.make_async_copy(
-                        source.at[0, :, units], wgu.at[step, :, pl.ds(place, hidden)], w_sems.at[step, number]
-                    ).wait()
-                pltpu.make_async_copy(downs[0].at[0, units], wd.at[step], w_sems.at[step, 2]).wait()
-
-            e = here * local + step // pieces
+                units = pl.ds(0, both_hidden)
+                for number in range(2):
+                    target = wgu.at[step, :, pl.ds(number * both_hidden, both_hidden)]
+                    pltpu.make_async_copy(gate_w.at[0, :, units], target, w_sems.at[step, number]).wait()
+                pltpu.make_async_copy(wd.at[step], wd.at[step], w_sems.at[step, 2]).wait()
+
+            e = here * local + (2 * step) // pieces
             lane = lax.broadcasted_iota(jnp.int32, (tile, lanes), 1)
             mine = lane == e
             halves = jnp.logical_or(mine, lane == e + experts)
@@ -1213,7 +1316,7 @@
             gate = jnp.sum(jnp.where(halves, x_buf[:, width:].astype(F32), 0.0), axis=1, keepdims=True)
             gate = gate * named
             both = nn(x_buf[:, :width], wgu[step])
-            gate_in, up_in = both[:, :hidden], both[:, hidden:]
+            gate_in, up_in = both[:, :both_hidden], both[:, both_hidden:]
             sigmoid = jax.nn.sigmoid(gate_in)
             silu = gate_in * sigmoid
             active = silu * up_in
@@ -1261,7 +1364,10 @@
         return carry
 
     lax.fori_loop(0, chips * subs, one_sub, 0)
-    out_sums = wgu.at[:, pl.ds(0, tokens), pl.ds(0, layer_ref.shape[1])]
+    if wgu.shape[0] >= chips:
+        out_sums = wgu.at[:, pl.ds(0, tokens), pl.ds(0, layer_ref.shape[1])]
+    else:
+        (out_sums,) = out_more
     operands[0] = g_buf.at[pl.ds(pl.multiple_of(core * own, 8), own)]
     operands[1] = dx_acc.at[pl.ds(own, own)]
     layer = reduce_steps(chips, 2, 1, out_ref, layer_ref, out_pair, out_line, out_sums, *out_sems)
@@ -1309,7 +1415,7 @@
     own = tokens // (2 * chips)
     hidden = downs[0].shape[1] if len(downs) > 1 else min(256, gate_w.shape[2] // 4)
     steps = gate_w.shape[0] * gate_w.shape[2] // hidden
-    subs = min(4, steps)
+    subs = min(4, steps // 2)
     whole = jax.ShapeDtypeStruct((tokens, width), BF16)
     part = width // (2 * chips)
     per_chip = pltpu.SemaphoreType.DMA((chips,))
@@ -1327,14 +1433,14 @@
             pltpu.VMEM((2 * own, width), F32),
             pltpu.VMEM((2 * own, width), F32),
             pltpu.VMEM((2 * own, lanes), F32),
-            pltpu.VMEM((steps, width, 2 * hidden), BF16),
-            pltpu.VMEM((steps, hidden, width), BF16),
+            pltpu.VMEM((steps // 2, width, 4 * hidden), BF16),
+            pltpu.VMEM((steps // 2, 2 * hidden, width), BF16),
             pltpu.VMEM((2 * own, wide), BF16),
             pltpu.VMEM((2 * own, width), BF16),
             pltpu.VMEM((chips, own, wide), BF16),
             pltpu.VMEM((chips + 1, own, wide), BF16),
             pltpu.VMEM((chips, own, wide), BF16),
-            pltpu.SemaphoreType.DMA((steps, 3)),
+            pltpu.SemaphoreType.DMA((steps // 2, 3)),
             pltpu.SemaphoreType.DMA((2,)),
             per_chip,
             per_chip,
@@ -1343,7 +1449,8 @@
             per_chip,
         ]
         + [halves] * 8
-        + [pltpu.SemaphoreType.DMA((chips + 1, 2)), halves],
+        + [pltpu.SemaphoreType.DMA((chips + 1, 2)), halves]
+        + ([] if steps // 2 >= chips else [pltpu.VMEM((chips, tokens, part), BF16)]),
         compiler_params=pltpu.CompilerParams(
             collective_id=ident, has_side_effects=True, vmem_limit_bytes=VMEM_MOST
         ),

time: 463 us -> 460 us (level); the launches traced: 456 us -> 459 us
  no operation moved by 1% of the time
where the time goes in v7:
time: 460 us; the launch traced here: 459 us
  Pallas kernels  384 us (83%)
  waiting for transfers between devices  30.6 us (7%)
  local copies, waits for them, and re-layouts  20 us (4%)
  between operations  15.5 us (3%)
  other arithmetic  7.58 us (2%)
    pallas_call x1, Pallas kernels, moe_turn(): pl.pallas_call(functools.partial(moe_turn_body, experts, chips, subs, len...  130 us
    pallas_call x1, Pallas kernels, line_turn(): pl.pallas_call(functools.partial(turn_body, chips, parts, first, last, le...  95.7 us
    pallas_call x1, Pallas kernels, back(): pl.pallas_call(functools.partial(back_body, min(256, seq_len), reach, sca...  77.9 us
    pallas_call x1, Pallas kernels, line_gather(): pl.pallas_call(functools.partial(gather_body, chips, parts, axis, len(mor...  42.5 us
    all_gather x1, waiting for transfers between devices, shards(): full_up = lax.all_gather(w_up, 'row', axis=2, tiled=True)  29.2 us
    pallas_call x1, Pallas kernels, project(): pl.pallas_call(functools.partial(project_body, min(256, seq_len)), out_sh...  17.1 us
    pallas_call x1, Pallas kernels, attend(): pl.pallas_call(functools.partial(attend_body, min(256, seq_len), reach, s...  12.8 us
  transfers between devices with their start and end apart: 2, of which 1 were waited for; matrix products, arithmetic and copies ran while one was open for 4% of the time, Pallas kernels for 38%

profile of v7, /device:TPU:16, one launch (start us, length us, event | category | flops | bytes accessed | tf_op | source)
XLA Modules:
  0.0 458.7 jit_solution(6424736567312601524)
XLA Ops:
  7.2 0.7 all-gather.3.cloned.1.call-update
  8.0 0.7 all-gather.5.cloned.1.call-update
  10.0 0.8 dynamic_slice.32
  10.8 0.8 dynamic_slice.33
  11.5 1.0 dynamic-slice_bitcast_fusion
  12.5 0.7 slice.38
  13.2 0.6 slice_bitcast_fusion
  14.0 0.6 pad.11.refs_5_.refs_4_
  14.6 0.8 pad.10.refs_4_.refs_3_
  15.4 1.0 copy.34.routes_ref
  16.5 42.5 %line_gather.1 = (bf16[1024,2048]{1,0:T(8,128)(2,1)}, bf16[3,2,64,2048]{3,2,1,0:T(8,128)(2,1)}) custom-call(bf16[1024,256]{1,0:T(8,128)(2,1)} %x_ref.1, bf16[8,64,2048]{2,1,0:T(8,128)(2,1)} %bitcast.33), custom_call_target="tpu_custom_call" | custom-call | tf_op jit(solution)/shard_map/line_gather/pallas_call | solution.py:189
  59.0 1.0 constant_dynamic-slice_fusion
  60.1 0.6 fusion.5.b_ref.refs_13_
  60.7 17.1 %project.1 = (f32[1024,768]{1,0:T(8,128)}, bf16[1024,48]{1,0:T(8,128)(2,1)}, f32[1024,1]{1,0:T(8,128)}, f32[2,1024]{1,0:T(2,128)}) custom-call(bf16[1024,2048]{1,0:T(8,128)(2,1)} %get-tuple-element.32.x_ref.refs_15_, f32[1,2048]{1,0:T(1,128)} %bitcast.46, bf16[2048,256]{1,0:T(8,128)(2,1)} %refs_21_.1, bf16[2048,256]{1,0:T(8,128)(2,1)} %refs_22_.1, ...), custom_call_target="tpu_custom_call" | custom-call | tf_op jit(solution)/shard_map/project/pallas_call | solution.py:647
  77.8 8.0 %small_gather.1 = f32[8,2,1024]{2,1,0:T(2,128)} custom-call(f32[2,1024]{1,0:T(2,128)} %get-tuple-element.34.x_ref), custom_call_target="tpu_custom_call" | custom-call | tf_op jit(solution)/shard_map/small_gather/pallas_call | solution.py:357
  85.8 0.9 reduce_sum.9
  86.7 1.0 copy.32
  87.7 0.8 dynamic-slice_bitcast_fusion.1.refs_2_
  89.2 1.9 concatenate.27.map_ref
  91.7 2.0 fusion.3
  93.7 1.3 pad_maximum_fusion
  95.1 12.8 %attend.1 = (bf16[1024,2176]{1,0:T(8,128)(2,1)}, bf16[1024,256]{1,0:T(8,128)(2,1)}, bf16[1024,256]{1,0:T(8,128)(2,1)}, bf16[1024,256]{1,0:T(8,128)(2,1)}, bf16[1024,256]{1,0:T(8,128)(2,1)}, /*index=5*/f32[1024,2]{1,0:T(8,128)}) custom-call(s32[1]{0:T(128)S(6)} %copy.38.prefix_ref, f32[1024,768]{1,0:T(8,128)} %get-tuple-element.33.proj_ref.refs_8_, ...), custom_call_target="tpu_custom_call" | custom-call | tf_op jit(solution)/shard_map/attend/pallas_call | solution.py:712
  107.9 1.9 constant_dynamic-slice_fusion.1.refs_1_
  109.7 95.7 %line_turn.1 = (bf16[1024,2176]{1,0:T(8,128)(2,1)}, f32[128,2048]{1,0:T(8,128)}, bf16[128,128]{1,0:T(8,128)(2,1)}, bf16[128,16]{1,0:T(8,128)(2,1)}, f32[128,128]...) custom-call(bf16[1024,2176]{1,0:T(8,128)(2,1)} %get-tuple-element.35.refs_0_, ...), custom_call_target="tpu_custom_call" | custom-call | tf_op jit(solution)/shard_map/line_turn/pallas_call | solution.py:529
  205.5 29.2 %all-gather.5.cloned.1.call-done.refs_9_ = bf16[2,2048,1024]{2,1,0:T(8,128)(2,1)} async-done(((bf16[2,2048,256]{2,1,0:T(8,128)(2,1)}), bf16[2,2048,1024]{2,1,0:T(8,128)(2,1)}) %all-gather.5.cloned.1.call-update) | async-done | bytes 8388624 | tf_op jit(solution)/shard_map/all_gather | solution.py:1522
  234.7 130.5 %moe_turn.1 = (f32[1024,256]{1,0:T(8,128)}, bf16[1024,2048]{1,0:T(8,128)(2,1)}, f32[32,2048]{1,0:T(8,128)}, f32[16,128]{1,0:T(8,128)}) custom-call(bf16[1024,2176]{1,0:T(8,128)(2,1)} %get-tuple-element.36.x_ref, bf16[1024,2048]{1,0:T(8,128)(2,1)} %get-tuple-element.37.g_ref, s32[1024,8]{1,0:T(8,128)} %copy.34.routes_ref, ...), custom_call_target="tpu_custom_call" | custom-call | tf_op jit(solution)/shard_map/moe_turn/pallas_call | solution.py:1423
  365.2 2.1 convert_element_type.15
  367.3 77.9 %back.1 = (f32[1024,256]{1,0:T(8,128)}, f32[5,2,16,256]{3,2,1,0:T(8,128)}, f32[4,2,16,256]{3,2,1,0:T(8,128)}, f32[2,16,256]{2,1,0:T(8,128)}) custom-call(s32[1]{0:T(128)S(6)} %copy.38.prefix_ref, s32[1]{0:T(128)} %copy.39.slot_ref, bf16[1024,2048]{1,0:T(8,128)(2,1)} %get-tuple-element.45.refs_0_, bf16[256,2048]{1,0:T(8,128)(2,1)} %copy-done.2, ...), custom_call_target="tpu_custom_call" | custom-call | tf_op jit(solution)/shard_map/back/pallas_call | solution.py:1109
  445.1 1.3 slice.37
  446.5 2.3 copy.40
  448.7 1.6 copy.41
  450.3 1.6 copy.42
  (30 shorter events, 1.6 us)
Async XLA Ops:
  7.2 6.8 %copy-start = (bf16[8,16,16]{2,1,0:T(8,128)(2,1)S(1)}, bf16[8,16,16]{2,1,0:T(8,128)(2,1)}, u32[]{:S(2)}) copy-start(bf16[8,16,16]{2,1,0:T(8,128)(2,1)} %param.36) | copy-start | bytes 12292
  7.2 7.4 %copy-start.5 = (bf16[2048,16]{0,1:T(8,128)(2,1)S(1)}, bf16[2048,16]{0,1:T(8,128)(2,1)}, u32[]{:S(2)}) copy-start(bf16[2048,16]{0,1:T(8,128)(2,1)} %param.30) | copy-start | bytes 196612
  7.2 8.2 %copy-start.6 = (s32[1024,8]{0,1:T(8,128)S(1)}, s32[1024,8]{0,1:T(8,128)}, u32[]{:S(2)}) copy-start(s32[1024,8]{0,1:T(8,128)} %param.37) | copy-start | bytes 98308
  7.2 198.2 %all-gather.3.cloned.1.call-start = ((), (), s32[]{:S(2)}) async-start(), calls=%async_computation | async-start | bytes 10485760 | tf_op jit(solution)/shard_map/all_gather | solution.py:1521
  7.9 226.8 %all-gather.5.cloned.1.call-start = ((), (), s32[]{:S(2)}) async-start(), calls=%async_computation.1 | async-start | bytes 10485760 | tf_op jit(solution)/shard_map/all_gather | solution.py:1522
  12.5 47.5 %copy-start.7 = (pred[48]{0:T(512)(128)(4,1)S(1)}, pred[48]{0:T(512)(128)(4,1)}, u32[]{:S(2)}) copy-start(pred[48]{0:T(512)(128)(4,1)} %constant.17.clone.1) | copy-start | bytes 148
  60.7 27.9 %copy-start.3 = (bf16[256,2048]{1,0:T(8,128)(2,1)S(1)}, bf16[256,2048]{1,0:T(8,128)(2,1)}, u32[]{:S(2)}) copy-start(bf16[256,2048]{1,0:T(8,128)(2,1)} %param.29) | copy-start | bytes 3145732
  88.6 0.6 copy-start.4
  89.2 5.9 %copy-start.2 = (bf16[256,2048]{1,0:T(8,128)(2,1)}, bf16[256,2048]{1,0:T(8,128)(2,1)S(1)}, u32[]{:S(2)}) copy-start(bf16[256,2048]{1,0:T(8,128)(2,1)S(1)} %fusion.refs_1_) | copy-start | bytes 3145732
  367.3 84.6 %copy-start.1 = (bf16[8,16,16]{2,1,0:T(8,128)(2,1)S(1)}, bf16[8,16,16]{2,1,0:T(8,128)(2,1)}, u32[]{:S(2)}) copy-start(bf16[8,16,16]{2,1,0:T(8,128)(2,1)} %param.36) | copy-start | bytes 12292
Sparse Core Ops, SparseCore 0:
  9.8 103.4 all-gather.2
  115.2 119.4 all-gather.4

commit v8 on v7

--- a/solution.py
+++ b/solution.py
@@ -14,7 +14,7 @@
 ANY = pl.BlockSpec(memory_space=pl.ANY)
 VMEM_LIMIT = 60 * 1024 * 1024
 VMEM_MOST = 67_000_000
-SHARES, FIRST_SHARE = 8, 2
+SHARES, FIRST_SHARE = 16, 6
 
 norm_eps = 1e-05
 rope_base = 10000.0

time: 460 us -> 463 us (level)
  Pallas kernels: 384 us -> 396 us
  waiting for transfers between devices: 30.6 us -> 22.4 us
    pallas_call x1, Pallas kernels: 42.5 us -> 55.3 us  [line_gather(): pl.pallas_call(functools.partial(gather_body, chips, parts, axis, len(mor...]
    all_gather x1, waiting for transfers between devices: 29.2 us -> 21 us  [shards(): full_up = lax.all_gather(w_up, 'row', axis=2, tiled=True)]
  transfers between devices with their start and end apart: 2 -> 2, of which waited for: 1 -> 1; matrix products, arithmetic and copies ran while one was open for 4% -> 4% of each run, Pallas kernels for 38% -> 41%
where the time goes in v8:
time: 463 us; the launch traced here: 462 us
  Pallas kernels  396 us (86%)
  waiting for transfers between devices  22.4 us (5%)
  local copies, waits for them, and re-layouts  20 us (4%)
  between operations  15.5 us (3%)
  other arithmetic  7.58 us (2%)
    pallas_call x1, Pallas kernels, moe_turn(): pl.pallas_call(functools.partial(moe_turn_body, experts, chips, subs, len...  130 us
    pallas_call x1, Pallas kernels, line_turn(): pl.pallas_call(functools.partial(turn_body, chips, parts, first, last, le...  95 us
    pallas_call x1, Pallas kernels, back(): pl.pallas_call(functools.partial(back_body, min(256, seq_len), reach, sca...  77.9 us
    pallas_call x1, Pallas kernels, line_gather(): pl.pallas_call(functools.partial(gather_body, chips, parts, axis, len(mor...  55.3 us
    all_gather x1, waiting for transfers between devices, shards(): full_up = lax.all_gather(w_up, 'row', axis=2, tiled=True)  21 us
    pallas_call x1, Pallas kernels, project(): pl.pallas_call(functools.partial(project_body, min(256, seq_len)), out_sh...  17.4 us
    pallas_call x1, Pallas kernels, attend(): pl.pallas_call(functools.partial(attend_body, min(256, seq_len), reach, s...  12.7 us
  transfers between devices with their start and end apart: 2, of which 1 were waited for; matrix products, arithmetic and copies ran while one was open for 4% of the time, Pallas kernels for 41%

profile of v8, /device:TPU:16, one launch (start us, length us, event | category | flops | bytes accessed | tf_op | source)
XLA Modules:
  0.0 461.8 jit_solution(9794860738328083863)
XLA Ops:
  7.2 0.7 all-gather.3.cloned.1.call-update
  8.0 0.7 all-gather.5.cloned.1.call-update
  10.0 0.8 dynamic_slice.32
  10.8 0.8 dynamic_slice.33
  11.5 1.0 dynamic-slice_bitcast_fusion
  12.5 0.7 slice.38
  13.2 0.6 slice_bitcast_fusion
  14.0 0.6 pad.11.refs_5_.refs_4_
  14.6 0.8 pad.10.refs_4_.refs_3_
  15.4 1.0 copy.34.routes_ref
  16.5 55.3 %line_gather.1 = (bf16[1024,2048]{1,0:T(8,128)(2,1)}, bf16[3,6,32,2048]{3,2,1,0:T(8,128)(2,1)}) custom-call(bf16[1024,256]{1,0:T(8,128)(2,1)} %x_ref.1, bf16[16,32,2048]{2,1,0:T(8,128)(2,1)} %bitcast.33), custom_call_target="tpu_custom_call" | custom-call | tf_op jit(solution)/shard_map/line_gather/pallas_call | solution.py:189
  71.8 1.0 constant_dynamic-slice_fusion
  72.8 0.6 fusion.5.b_ref.refs_13_
  73.5 17.4 %project.1 = (f32[1024,768]{1,0:T(8,128)}, bf16[1024,48]{1,0:T(8,128)(2,1)}, f32[1024,1]{1,0:T(8,128)}, f32[2,1024]{1,0:T(2,128)}) custom-call(bf16[1024,2048]{1,0:T(8,128)(2,1)} %get-tuple-element.32.x_ref.refs_15_, f32[1,2048]{1,0:T(1,128)} %bitcast.46, bf16[2048,256]{1,0:T(8,128)(2,1)} %refs_21_.1, bf16[2048,256]{1,0:T(8,128)(2,1)} %refs_22_.1, ...), custom_call_target="tpu_custom_call" | custom-call | tf_op jit(solution)/shard_map/project/pallas_call | solution.py:647
  90.9 7.1 %small_gather.1 = f32[8,2,1024]{2,1,0:T(2,128)} custom-call(f32[2,1024]{1,0:T(2,128)} %get-tuple-element.34.x_ref), custom_call_target="tpu_custom_call" | custom-call | tf_op jit(solution)/shard_map/small_gather/pallas_call | solution.py:357
  98.0 0.9 reduce_sum.9
  98.9 1.0 copy.32
  99.9 0.8 dynamic-slice_bitcast_fusion.1.refs_2_
  101.4 1.9 concatenate.27.map_ref
  103.9 2.0 fusion.3
  105.9 1.3 pad_maximum_fusion
  107.2 12.7 %attend.1 = (bf16[1024,2176]{1,0:T(8,128)(2,1)}, bf16[1024,256]{1,0:T(8,128)(2,1)}, bf16[1024,256]{1,0:T(8,128)(2,1)}, bf16[1024,256]{1,0:T(8,128)(2,1)}, bf16[1024,256]{1,0:T(8,128)(2,1)}, /*index=5*/f32[1024,2]{1,0:T(8,128)}) custom-call(s32[1]{0:T(128)S(6)} %copy.38.prefix_ref, f32[1024,768]{1,0:T(8,128)} %get-tuple-element.33.proj_ref.refs_8_, ...), custom_call_target="tpu_custom_call" | custom-call | tf_op jit(solution)/shard_map/attend/pallas_call | solution.py:712
  119.9 1.9 constant_dynamic-slice_fusion.1.refs_1_
  121.8 95.0 %line_turn.1 = (bf16[1024,2176]{1,0:T(8,128)(2,1)}, f32[128,2048]{1,0:T(8,128)}, bf16[128,128]{1,0:T(8,128)(2,1)}, bf16[128,16]{1,0:T(8,128)(2,1)}, f32[128,128]...) custom-call(bf16[1024,2176]{1,0:T(8,128)(2,1)} %get-tuple-element.35.refs_0_, ...), custom_call_target="tpu_custom_call" | custom-call | tf_op jit(solution)/shard_map/line_turn/pallas_call | solution.py:529
  216.8 21.0 %all-gather.5.cloned.1.call-done.refs_9_ = bf16[2,2048,1024]{2,1,0:T(8,128)(2,1)} async-done(((bf16[2,2048,256]{2,1,0:T(8,128)(2,1)}), bf16[2,2048,1024]{2,1,0:T(8,128)(2,1)}) %all-gather.5.cloned.1.call-update) | async-done | bytes 8388624 | tf_op jit(solution)/shard_map/all_gather | solution.py:1522
  237.8 130.4 %moe_turn.1 = (f32[1024,256]{1,0:T(8,128)}, bf16[1024,2048]{1,0:T(8,128)(2,1)}, f32[32,2048]{1,0:T(8,128)}, f32[16,128]{1,0:T(8,128)}) custom-call(bf16[1024,2176]{1,0:T(8,128)(2,1)} %get-tuple-element.36.x_ref, bf16[1024,2048]{1,0:T(8,128)(2,1)} %get-tuple-element.37.g_ref, s32[1024,8]{1,0:T(8,128)} %copy.34.routes_ref, ...), custom_call_target="tpu_custom_call" | custom-call | tf_op jit(solution)/shard_map/moe_turn/pallas_call | solution.py:1423
  368.3 2.1 convert_element_type.15
  370.4 77.9 %back.1 = (f32[1024,256]{1,0:T(8,128)}, f32[5,2,16,256]{3,2,1,0:T(8,128)}, f32[4,2,16,256]{3,2,1,0:T(8,128)}, f32[2,16,256]{2,1,0:T(8,128)}) custom-call(s32[1]{0:T(128)S(6)} %copy.38.prefix_ref, s32[1]{0:T(128)} %copy.39.slot_ref, bf16[1024,2048]{1,0:T(8,128)(2,1)} %get-tuple-element.45.refs_0_, bf16[256,2048]{1,0:T(8,128)(2,1)} %copy-done.2, ...), custom_call_target="tpu_custom_call" | custom-call | tf_op jit(solution)/shard_map/back/pallas_call | solution.py:1109
  448.2 1.3 slice.37
  449.5 2.3 copy.40
  451.8 1.6 copy.41
  453.4 1.6 copy.42
  (30 shorter events, 1.6 us)
Async XLA Ops:
  7.2 6.8 %copy-start = (bf16[8,16,16]{2,1,0:T(8,128)(2,1)S(1)}, bf16[8,16,16]{2,1,0:T(8,128)(2,1)}, u32[]{:S(2)}) copy-start(bf16[8,16,16]{2,1,0:T(8,128)(2,1)} %param.36) | copy-start | bytes 12292
  7.2 7.4 %copy-start.5 = (bf16[2048,16]{0,1:T(8,128)(2,1)S(1)}, bf16[2048,16]{0,1:T(8,128)(2,1)}, u32[]{:S(2)}) copy-start(bf16[2048,16]{0,1:T(8,128)(2,1)} %param.30) | copy-start | bytes 196612
  7.2 8.2 %copy-start.6 = (s32[1024,8]{0,1:T(8,128)S(1)}, s32[1024,8]{0,1:T(8,128)}, u32[]{:S(2)}) copy-start(s32[1024,8]{0,1:T(8,128)} %param.37) | copy-start | bytes 98308
  7.2 209.6 %all-gather.3.cloned.1.call-start = ((), (), s32[]{:S(2)}) async-start(), calls=%async_computation | async-start | bytes 10485760 | tf_op jit(solution)/shard_map/all_gather | solution.py:1521
  7.9 229.9 %all-gather.5.cloned.1.call-start = ((), (), s32[]{:S(2)}) async-start(), calls=%async_computation.1 | async-start | bytes 10485760 | tf_op jit(solution)/shard_map/all_gather | solution.py:1522
  12.5 60.2 %copy-start.7 = (pred[48]{0:T(512)(128)(4,1)S(1)}, pred[48]{0:T(512)(128)(4,1)}, u32[]{:S(2)}) copy-start(pred[48]{0:T(512)(128)(4,1)} %constant.17.clone.1) | copy-start | bytes 148
  73.5 27.3 %copy-start.3 = (bf16[256,2048]{1,0:T(8,128)(2,1)S(1)}, bf16[256,2048]{1,0:T(8,128)(2,1)}, u32[]{:S(2)}) copy-start(bf16[256,2048]{1,0:T(8,128)(2,1)} %param.29) | copy-start | bytes 3145732
  100.7 0.6 copy-start.4
  101.4 5.8 %copy-start.2 = (bf16[256,2048]{1,0:T(8,128)(2,1)}, bf16[256,2048]{1,0:T(8,128)(2,1)S(1)}, u32[]{:S(2)}) copy-start(bf16[256,2048]{1,0:T(8,128)(2,1)S(1)} %fusion.refs_1_) | copy-start | bytes 3145732
  370.4 84.6 %copy-start.1 = (bf16[8,16,16]{2,1,0:T(8,128)(2,1)S(1)}, bf16[8,16,16]{2,1,0:T(8,128)(2,1)}, u32[]{:S(2)}) copy-start(bf16[8,16,16]{2,1,0:T(8,128)(2,1)} %param.36) | copy-start | bytes 12292
Sparse Core Ops, SparseCore 0:
  9.8 110.8 all-gather.2
  122.5 115.2 all-gather.4
